TPU v7x, 32 devices: a whole 2x2x4 slice. The times are simulated.
32 devices in a mesh: dp: 16 (over z, x, core), tensor: 2 (over y).
Axes of the slice: x: 2, y: 2, z: 4, core: 2. Of those that a mesh axis runs over, the one named last changes fastest.
Arguments:
- layer_input: bfloat16 [16384, 1536], P(('dp', 'tensor')), may hold values from -6 to 6
- gain_attn: float32 [1536], replicated, may hold values from 0.25 to 1.75
- w_attn: bfloat16 [1536, 4, 1536], P('dp', None, 'tensor'), may hold values from -0.15625 to 0.15625
- w_forget: bfloat16 [1536, 24], P('dp', 'tensor'), may hold values from -0.15625 to 0.15625
- forget_bias: float32 [24], replicated, may hold values from 1.5 to 8
- w_out: bfloat16 [1536, 1536], P('tensor', 'dp'), may hold values from -2.5 to 2.5
- gain_mlp: float32 [1536], replicated, may hold values from 0.25 to 1.75
- w_mlp: bfloat16 [1536, 2, 4096], P('dp', None, 'tensor'), may hold values from -0.15625 to 0.15625
- w_down: bfloat16 [4096, 1536], P('tensor', 'dp'), may hold values from -0.09375 to 0.09375
- lengths: int32 [16], P('dp'), may hold values from 256 to 1024, as said below
- cotangent: bfloat16 [16384, 1536], P(('dp', 'tensor')), may hold values from -6 to 6
Outputs:
- layer_output: bfloat16 [16384, 1536], P(('dp', 'tensor'))
- grad_input: float32 [16384, 1536], P(('dp', 'tensor'))
- grad_gain_attn: float32 [1536], replicated
- grad_w_attn: float32 [1536, 4, 1536], P('dp', None, 'tensor')
- grad_w_forget: float32 [1536, 24], P('dp', 'tensor')
- grad_forget_bias: float32 [24], replicated
- grad_w_out: float32 [1536, 1536], P('tensor', 'dp')
- grad_gain_mlp: float32 [1536], replicated
- grad_w_mlp: float32 [1536, 2, 4096], P('dp', None, 'tensor')
- grad_w_down: float32 [4096, 1536], P('tensor', 'dp')
Inputs may be any that keep to these rules, and one draw needn't show every extreme that they name: `lengths`: used slots of each sequence, from its first slot on; some sequence uses all 1024 slots and some only 256.
All inputs are finite; a program needn't handle non-finite values.
Results may differ from a plain program's by a relative error of at most 0.015.
Values may be sent and summed in bfloat16 or wider, within the bound.
No kernel may reach another device: no remote copies, remote signals or barrier semaphores. Data moves between devices by JAX's collectives and lax.ppermute only.
A program may use at most 256 MiB of HBM per device.

v0:
```python
import jax
import jax.numpy as jnp
from jax import lax
from jax.sharding import PartitionSpec as P

HEAD = 64
SLOTS = 1024


EPS = 1e-06


def norm_parts(hidden_rows):
    inverse = lax.rsqrt(jnp.mean(hidden_rows * hidden_rows, axis=-1, keepdims=True) + EPS)
    return (hidden_rows * inverse, inverse)


def norm_back(grad_normed, scaled, inverse, gain):
    grad_scaled = grad_normed * gain
    inner_sum = jnp.mean(grad_scaled * scaled, axis=-1, keepdims=True)
    return inverse * (grad_scaled - scaled * inner_sum)


def gather_weights(w_attn, w_forget, w_out, w_mlp, w_down):
    return (
        lax.all_gather(w_attn, "dp", axis=0, tiled=True),
        lax.all_gather(w_forget, "dp", axis=0, tiled=True),
        lax.all_gather(w_out, "dp", axis=1, tiled=True),
        lax.all_gather(w_mlp, "dp", axis=0, tiled=True),
        lax.all_gather(w_down, "dp", axis=1, tiled=True),
    )


def gather_normed(hidden_rows, gain):
    scaled, inverse = norm_parts(hidden_rows)
    normed = (scaled * gain).astype(jnp.bfloat16)
    return (lax.all_gather(normed, "tensor", axis=0, tiled=True), scaled, inverse)


def gather_grads(grad_rows):
    return lax.all_gather(grad_rows.astype(jnp.bfloat16), "tensor", axis=0, tiled=True)


def branch_sum(term_fn, own_rows):
    return lax.psum_scatter(
        term_fn(jnp.int32(0), own_rows * lax.axis_size("tensor")),
        "tensor",
        scatter_dimension=0,
        tiled=True,
    )


def input_sum(term_fn, own_rows):
    return lax.psum_scatter(
        term_fn(jnp.int32(0), own_rows * lax.axis_size("tensor")),
        "tensor",
        scatter_dimension=0,
        tiled=True,
    )


def attention_inputs(normed_all, weights, bias_own, group_seqs):
    projected = jnp.einsum(
        "td,dkc->tkc", normed_all, weights[0], preferred_element_type=jnp.float32
    )
    logits = jnp.dot(normed_all, weights[1], preferred_element_type=jnp.float32) + bias_own
    heads_dev = projected.shape[2] // HEAD

    def split_heads(column):
        return projected[:, column].astype(jnp.bfloat16).reshape(group_seqs, SLOTS, heads_dev, HEAD)

    log_forget = jax.nn.log_sigmoid(logits)
    decays = jnp.cumsum(log_forget.reshape(group_seqs, SLOTS, heads_dev), axis=1)
    return (split_heads(0), split_heads(1), split_heads(2), projected[:, 3], logits, decays)


def mlp_inputs(normed_mid, weights):
    paired = jnp.einsum("td,dkf->tkf", normed_mid, weights[3], preferred_element_type=jnp.float32)
    gate_pre = paired[:, 0]
    up_pre = paired[:, 1]
    hidden = (jax.nn.silu(gate_pre) * up_pre).astype(jnp.bfloat16)
    return (gate_pre, up_pre, hidden)


def block_scores(queries, key_rows, decays, length, block_start, block_rows):
    picked = lax.slice_in_dim(queries, block_start, block_start + block_rows, axis=0)
    scores = jnp.einsum(
        "qhe,khe->hqk", picked, key_rows, preferred_element_type=jnp.float32
    ) * HEAD ** (-0.5)
    scores = (
        scores + decays[block_start : block_start + block_rows].T[:, :, None] - decays.T[:, None, :]
    )
    query_pos = block_start + jnp.arange(block_rows, dtype=jnp.int32)
    key_pos = jnp.arange(SLOTS, dtype=jnp.int32)
    allowed = (key_pos[None, :] <= query_pos[:, None]) & (key_pos[None, :] < length)
    return (picked, jnp.where(allowed[None], scores, -1e30), allowed[None])


def sequence_forward(packed):
    queries, key_rows, value_rows, decays, length = packed
    block_rows = min(512, SLOTS)
    outputs = []
    log_totals = []
    for block_start in range(0, SLOTS, block_rows):
        picked, scores, allowed = block_scores(
            queries, key_rows, decays, length, block_start, block_rows
        )
        row_max = jnp.max(scores, axis=-1, keepdims=True)
        exponent = jnp.exp(scores - row_max)
        totals = jnp.sum(exponent, axis=-1, keepdims=True)
        soft_low = (exponent / totals).astype(jnp.bfloat16)
        outputs.append(
            jnp.einsum("hqk,khe->qhe", soft_low, value_rows, preferred_element_type=jnp.float32)
        )
        log_totals.append((row_max + jnp.log(totals))[:, :, 0])
    return (jnp.concatenate(outputs, axis=0), jnp.concatenate(log_totals, axis=1))


def sequence_backward(packed):
    queries, key_rows, value_rows, decays, length, log_totals, grad_attended = packed
    block_rows = min(512, SLOTS)
    score_scale = HEAD ** (-0.5)
    grad_keys = jnp.zeros(key_rows.shape, jnp.float32)
    grad_values = jnp.zeros(value_rows.shape, jnp.float32)
    column_terms = jnp.zeros((decays.shape[1], decays.shape[0]), jnp.float32)
    query_grads = []
    row_terms = []
    for block_start in range(0, SLOTS, block_rows):
        picked, scores, allowed = block_scores(
            queries, key_rows, decays, length, block_start, block_rows
        )
        shifted = scores - log_totals[:, block_start : block_start + block_rows, None]
        soft = jnp.where(allowed, jnp.exp(shifted), 0.0)
        grad_picked = lax.slice_in_dim(grad_attended, block_start, block_start + block_rows, axis=0)
        grad_soft = jnp.einsum(
            "qhe,khe->hqk", grad_picked, value_rows, preferred_element_type=jnp.float32
        )
        inner_sum = jnp.sum(soft * grad_soft, axis=-1, keepdims=True)
        grad_scores = (soft * (grad_soft - inner_sum)).astype(jnp.bfloat16)
        query_grads.append(
            jnp.einsum("hqk,khe->qhe", grad_scores, key_rows, preferred_element_type=jnp.float32)
            * score_scale
        )
        grad_keys = (
            grad_keys
            + jnp.einsum("hqk,qhe->khe", grad_scores, picked, preferred_element_type=jnp.float32)
            * score_scale
        )
        grad_values = grad_values + jnp.einsum(
            "hqk,qhe->khe",
            soft.astype(jnp.bfloat16),
            grad_picked,
            preferred_element_type=jnp.float32,
        )
        wide_grads = grad_scores.astype(jnp.float32)
        row_terms.append(jnp.sum(wide_grads, axis=2))
        column_terms = column_terms - jnp.sum(wide_grads, axis=1)
    grad_decay = jnp.concatenate(row_terms, axis=1) + column_terms
    grad_forget = jnp.cumsum(grad_decay[:, ::-1], axis=1)[:, ::-1].T
    return (
        jnp.concatenate(query_grads, axis=0).astype(jnp.bfloat16),
        grad_keys.astype(jnp.bfloat16),
        grad_values.astype(jnp.bfloat16),
        grad_forget,
    )


def on_device(
    layer_input,
    gain_attn,
    w_attn,
    w_forget,
    forget_bias,
    w_out,
    gain_mlp,
    w_mlp,
    w_down,
    lengths,
    cotangent,
):
    own_rows = layer_input.shape[0]
    group_seqs = lengths.shape[0]
    group_rows = group_seqs * SLOTS
    heads_dev = w_attn.shape[2] // HEAD
    tensor_index = lax.axis_index("tensor")
    bias_own = lax.dynamic_slice_in_dim(forget_bias, tensor_index * heads_dev, heads_dev)
    positions = tensor_index * own_rows + jnp.arange(own_rows, dtype=jnp.int32)
    seq_of_row = positions // SLOTS
    matches = seq_of_row[:, None] == jnp.arange(group_seqs, dtype=jnp.int32)[None, :]
    own_lengths = jnp.sum(jnp.where(matches, lengths[None, :], 0), axis=1)
    valid = (positions % SLOTS < own_lengths).astype(jnp.float32)[:, None]
    weights = gather_weights(w_attn, w_forget, w_out, w_mlp, w_down)
    input_wide = layer_input.astype(jnp.float32)
    normed_all, scaled_attn, inverse_attn = gather_normed(input_wide, gain_attn)
    queries, key_rows, value_rows, out_gate, logits, decays = attention_inputs(
        normed_all, weights, bias_own, group_seqs
    )
    attended, log_totals = lax.map(
        sequence_forward, (queries, key_rows, value_rows, decays, lengths)
    )
    attended = attended.reshape(group_rows, heads_dev * HEAD)
    gate_sig = jax.nn.sigmoid(out_gate)
    gated = (attended * gate_sig).astype(jnp.bfloat16)

    def attn_term(first_row, row_count):
        picked = lax.dynamic_slice_in_dim(gated, first_row, row_count)
        return jnp.dot(picked, weights[2], preferred_element_type=jnp.float32)

    attn_branch = branch_sum(attn_term, own_rows)
    middle = input_wide + attn_branch
    normed_mid, scaled_mlp, inverse_mlp = gather_normed(middle, gain_mlp)
    gate_pre, up_pre, hidden = mlp_inputs(normed_mid, weights)

    def mlp_term(first_row, row_count):
        picked = lax.dynamic_slice_in_dim(hidden, first_row, row_count)
        return jnp.dot(picked, weights[4], preferred_element_type=jnp.float32)

    mlp_branch = branch_sum(mlp_term, own_rows)
    layer_output = (valid * (middle + mlp_branch)).astype(jnp.bfloat16)
    weights = gather_weights(w_attn, w_forget, w_out, w_mlp, w_down)
    normed_mid = gather_normed(middle, gain_mlp)[0]
    gate_pre, up_pre, hidden = mlp_inputs(normed_mid, weights)
    grad_final = cotangent.astype(jnp.float32) * valid
    grad_final_all = gather_grads(grad_final)
    grad_hidden = jnp.einsum(
        "td,fd->tf", grad_final_all, weights[4], preferred_element_type=jnp.float32
    )
    gate_s = jax.nn.sigmoid(gate_pre)
    grad_gate = (grad_hidden * up_pre * gate_s * (1.0 + gate_pre * (1.0 - gate_s))).astype(
        jnp.bfloat16
    )
    grad_up = (grad_hidden * gate_pre * gate_s).astype(jnp.bfloat16)
    grad_pair = jnp.stack([grad_gate, grad_up], axis=1)
    grad_w_down = jnp.einsum(
        "tf,td->fd", hidden, grad_final_all, preferred_element_type=jnp.float32
    )
    grad_w_mlp = jnp.einsum(
        "td,tkf->dkf", normed_mid, grad_pair, preferred_element_type=jnp.float32
    )

    def mlp_back_term(first_row, row_count):
        picked = lax.dynamic_slice_in_dim(grad_pair, first_row, row_count)
        return jnp.einsum("tkf,dkf->td", picked, weights[3], preferred_element_type=jnp.float32)

    grad_normed_mlp = input_sum(mlp_back_term, own_rows)
    gain_mlp_part = jnp.sum(scaled_mlp * grad_normed_mlp, axis=0)
    grad_middle = grad_final + norm_back(grad_normed_mlp, scaled_mlp, inverse_mlp, gain_mlp)
    normed_all = gather_normed(input_wide, gain_attn)[0]
    queries, key_rows, value_rows, out_gate, logits, decays = attention_inputs(
        normed_all, weights, bias_own, group_seqs
    )
    gate_sig = jax.nn.sigmoid(out_gate)
    gated = (attended * gate_sig).astype(jnp.bfloat16)
    grad_branch_all = gather_grads(grad_middle)
    grad_w_out = jnp.einsum("tc,td->cd", gated, grad_branch_all, preferred_element_type=jnp.float32)
    grad_gated = jnp.einsum(
        "td,cd->tc", grad_branch_all, weights[2], preferred_element_type=jnp.float32
    )
    grad_attended = (grad_gated * gate_sig).astype(jnp.bfloat16)
    grad_out_gate = (grad_gated * attended * gate_sig * (1.0 - gate_sig)).astype(jnp.bfloat16)
    grad_heads = grad_attended.reshape(group_seqs, SLOTS, heads_dev, HEAD)
    grad_queries, grad_keys, grad_values, grad_forget = lax.map(
        sequence_backward, (queries, key_rows, value_rows, decays, lengths, log_totals, grad_heads)
    )
    grad_logit = grad_forget.reshape(group_rows, heads_dev) * jax.nn.sigmoid(-logits)
    bias_part = jnp.sum(grad_logit, axis=0)
    grad_logit_low = grad_logit.astype(jnp.bfloat16)
    grad_proj = jnp.stack(
        [
            grad_queries.reshape(group_rows, heads_dev * HEAD),
            grad_keys.reshape(group_rows, heads_dev * HEAD),
            grad_values.reshape(group_rows, heads_dev * HEAD),
            grad_out_gate,
        ],
        axis=1,
    )
    grad_w_attn = jnp.einsum(
        "td,tkc->dkc", normed_all, grad_proj, preferred_element_type=jnp.float32
    )
    grad_w_forget = jnp.einsum(
        "td,th->dh", normed_all, grad_logit_low, preferred_element_type=jnp.float32
    )

    def attn_back_term(first_row, row_count):
        picked = lax.dynamic_slice_in_dim(grad_proj, first_row, row_count)
        picked_logit = lax.dynamic_slice_in_dim(grad_logit_low, first_row, row_count)
        term = jnp.einsum("tkc,dkc->td", picked, weights[0], preferred_element_type=jnp.float32)
        return term + jnp.einsum(
            "th,dh->td", picked_logit, weights[1], preferred_element_type=jnp.float32
        )

    grad_normed_attn = input_sum(attn_back_term, own_rows)
    gain_attn_part = jnp.sum(scaled_attn * grad_normed_attn, axis=0)
    grad_input = grad_middle + norm_back(grad_normed_attn, scaled_attn, inverse_attn, gain_attn)
    grad_w_attn, grad_w_forget, grad_w_out, grad_w_mlp, grad_w_down = (
        lax.psum_scatter(grad_w_attn, "dp", scatter_dimension=0, tiled=True),
        lax.psum_scatter(grad_w_forget, "dp", scatter_dimension=0, tiled=True),
        lax.psum_scatter(grad_w_out, "dp", scatter_dimension=1, tiled=True),
        lax.psum_scatter(grad_w_mlp, "dp", scatter_dimension=0, tiled=True),
        lax.psum_scatter(grad_w_down, "dp", scatter_dimension=1, tiled=True),
    )
    bias_full = lax.dynamic_update_slice_in_dim(
        jnp.zeros(forget_bias.shape, jnp.float32), bias_part, tensor_index * heads_dev, 0
    )
    grad_gain_attn, grad_gain_mlp, grad_forget_bias = lax.psum(
        (gain_attn_part, gain_mlp_part, bias_full), ("dp", "tensor")
    )
    return (
        layer_output,
        grad_input,
        grad_gain_attn,
        grad_w_attn,
        grad_w_forget,
        grad_forget_bias,
        grad_w_out,
        grad_gain_mlp,
        grad_w_mlp,
        grad_w_down,
    )


def solution(mesh):
    placed = (
        P(("dp", "tensor"), None),
        P(),
        P("dp", None, "tensor"),
        P("dp", "tensor"),
        P(),
        P("tensor", "dp"),
        P(),
        P("dp", None, "tensor"),
        P("tensor", "dp"),
        P("dp"),
        P(("dp", "tensor"), None),
    )
    return jax.shard_map(
        on_device,
        mesh=mesh,
        in_specs=placed,
        out_specs=(
            P(("dp", "tensor"), None),
            P(("dp", "tensor"), None),
            P(),
            P("dp", None, "tensor"),
            P("dp", "tensor"),
            P(),
            P("tensor", "dp"),
            P(),
            P("dp", None, "tensor"),
            P("tensor", "dp"),
        ),
        check_vma=False,
    )
```

profile of v0, /device:TPU:0, one launch (start us, length us, event | category | flops | bytes accessed | tf_op | source)
XLA Modules:
  0.0 1772.0 jit_solution(3117024105663561134)
XLA Ops:
  7.3 1.8 fusion.31
  9.7 3.0 fusion.25
  15.1 23.3 %all-gather = bf16[16,96,12]{1,2,0:T(8,128)(2,1)S(1)} all-gather(bf16[1,96,12]{1,2,0:T(8,128)(2,1)S(1)} %bitcast.211), channel_id=1, replica_groups=mesh['dp'=16,'tensor'=2] {'dp'}, dimensions={0}, use_global_device_ids=true | all-gather | bytes 39168 | tf_op jit(solution)/shard_map/all_gather | solution.py:27
  40.2 20.3 %all-gather.10.cloned.1.call-done = bf16[1024,1536]{1,0:T(8,128)(2,1)} async-done(((bf16[512,1536]{1,0:T(8,128)(2,1)}), bf16[1024,1536]{1,0:T(8,128)(2,1)}) %all-gather.10.cloned.1.call-update) | async-done | bytes 3145744 | tf_op jit(solution)/shard_map/all_gather | solution.py:37
  60.5 3.6 fusion.54
  64.1 3.4 reduce-window.14
  68.0 76.3 %all-gather.12.cloned.1.call-done = bf16[1536,4,768]{2,0,1:T(8,128)(2,1)} async-done(((bf16[96,4,768]{2,0,1:T(8,128)(2,1)}), bf16[1536,4,768]{2,0,1:T(8,128)(2,1)}) %all-gather.12.cloned.1.call-update) | async-done | bytes 9437200 | tf_op jit(solution)/shard_map/all_gather | solution.py:26
  144.3 16.2 fusion.74
  162.0 2.8 fusion.71
  164.8 11.3 fusion.75
  176.1 11.1 fusion.1
  187.2 10.4 fusion.52
  197.7 11.5 fusion.76
  209.2 10.9 fusion
  220.1 10.3 fusion.53
  232.4 3.1 fusion.39
  235.5 6.8 fusion.77
  244.7 73.5 %reduce-scatter.12.cloned.1.call-done = f32[512,1536]{1,0:T(8,128)} async-done(((f32[1024,1536]{1,0:T(8,128)}), f32[512,1536]{1,0:T(8,128)}) %reduce-scatter.12.cloned.1.call-update) | async-done | bytes 3145744 | tf_op jit(solution)/shard_map/reduce_scatter | solution.py:45
  318.1 2.8 multiply_reduce_fusion.4
  322.5 2.9 fusion.47
  326.2 95.0 %all-gather.18.cloned.1.call-done = bf16[1536,2,2048]{2,0,1:T(8,128)(2,1)} async-done(((bf16[96,2,2048]{2,0,1:T(8,128)(2,1)}), bf16[1536,2,2048]{2,0,1:T(8,128)(2,1)}) %all-gather.18.cloned.1.call-update) | async-done | bytes 12582928 | tf_op jit(solution)/shard_map/all_gather | solution.py:29
  421.3 45.2 %all-gather.16.cloned.1.call-done = bf16[1024,1536]{1,0:T(8,128)(2,1)} async-done(((bf16[512,1536]{1,0:T(8,128)(2,1)}), bf16[1024,1536]{1,0:T(8,128)(2,1)}) %all-gather.16.cloned.1.call-update) | async-done | bytes 3145744 | tf_op jit(solution)/shard_map/all_gather | solution.py:37
  466.4 20.6 %fusion.37 = f32[1024,2,2048]{2,0,1:T(8,128)} fusion(bf16[1536,2,2048]{2,0,1:T(8,128)(2,1)} %all-gather.18.cloned.1.call-done, bf16[1024,1536]{1,0:T(8,128)(2,1)} %all-gather.16.cloned.1.call-done), kind=kOutput, calls=%fused_computation.65 | convolution fusion | flops 12884901888 | bytes 32505856 | tf_op jit(solution)/shard_map/td,dkf->tkf/dot_general | solution.py:78
  487.1 26.4 %all-gather.22.cloned.1.call-done = bf16[1024,1536]{1,0:T(8,128)(2,1)} async-done(((bf16[512,1536]{1,0:T(8,128)(2,1)}), bf16[1024,1536]{1,0:T(8,128)(2,1)}) %all-gather.22.cloned.1.call-update) | async-done | bytes 3145744 | tf_op jit(solution)/shard_map/all_gather | solution.py:41
  513.5 63.7 %all-gather.20.cloned.1.call-done = bf16[2048,1536]{0,1:T(8,128)(2,1)} async-done(((bf16[2048,96]{0,1:T(8,128)(2,1)}), bf16[2048,1536]{0,1:T(8,128)(2,1)}) %all-gather.20.cloned.1.call-update) | async-done | bytes 6291472 | tf_op jit(solution)/shard_map/all_gather | solution.py:30
  577.2 18.2 %fusion.24 = (bf16[1024,1,2048]{2,0,1:T(8,128)(2,1)S(1)}, bf16[1024,1,2048]{2,0,1:T(8,128)(2,1)}, bf16[1024,2048]{1,0:T(8,128)(2,1)}) fusion(f32[1024,2,2048]{2,0,1:T(8,128)} %fusion.37, bf16[1024,1536]{1,0:T(8,128)(2,1)} %all-gather.22.cloned.1.call-done, bf16[2048,1536]{0,1:T(8,128)(2,1)} %all-gather.20.cloned.1.call-done), kind=kOutput, calls=%fused_computation.50 | convolution fusion | flops 6476005376 | bytes 38797312 | tf_op jit(solution)/shard_map/td,fd->tf/dot_general | solution.py:225
  595.4 1.9 copy-done.42
  597.4 18.5 %fusion.22 = f32[1024,1536]{1,0:T(8,128)} fusion(bf16[1536,2,2048]{2,0,1:T(8,128)(2,1)} %all-gather.18.cloned.1.call-done, bf16[1024,1,2048]{2,0,1:T(8,128)(2,1)} %get-tuple-element.120, bf16[1024,1,2048]{2,0,1:T(8,128)(2,1)S(1)} %get-tuple-element.119), kind=kOutput, calls=%fused_computation.48 | convolution fusion | flops 12889096192 | bytes 27262976 | tf_op jit(solution)/shard_map/tkf,dkf->td/dot_general | solution.py:243
  616.0 12.0 fusion.78
  628.0 63.9 %reduce-scatter.16.cloned.1.call-done = f32[512,1536]{1,0:T(8,128)} async-done(((f32[1024,1536]{1,0:T(8,128)}), f32[512,1536]{1,0:T(8,128)}) %reduce-scatter.16.cloned.1.call-update) | async-done | bytes 3145744 | tf_op jit(solution)/shard_map/reduce_scatter | solution.py:54
  692.0 3.2 multiply_reduce_fusion.2
  695.2 76.1 %reduce-scatter.14.cloned.1.call-done = f32[512,1536]{1,0:T(8,128)} async-done(((f32[1024,1536]{1,0:T(8,128)}), f32[512,1536]{1,0:T(8,128)}) %reduce-scatter.14.cloned.1.call-update) | async-done | bytes 3145744 | tf_op jit(solution)/shard_map/reduce_scatter | solution.py:45
  771.3 5.6 fusion.69
  777.1 44.9 %all-gather.24.cloned.1.call-done = bf16[1024,1536]{1,0:T(8,128)(2,1)} async-done(((bf16[512,1536]{1,0:T(8,128)(2,1)}), bf16[1024,1536]{1,0:T(8,128)(2,1)}) %all-gather.24.cloned.1.call-update) | async-done | bytes 3145744 | tf_op jit(solution)/shard_map/all_gather | solution.py:41
  822.0 9.0 multiply_convert_fusion.6
  832.8 21.2 %multiply_reduce_fusion.1 = (f32[12,512]{1,0:T(8,128)S(1)}, f32[12,512,1024]{2,1,0:T(8,128)}) fusion(f32[12,512,1024]{2,1,0:T(8,128)} %get-tuple-element.142, f32[12,512]{1,0:T(8,128)S(1)} %log_add_fusion.1, pred[512,1024]{1,0:T(8,128)(4,1)S(1)} %copy-done.12, bf16[512,12,64]{0,2,1:T(8,128)(2,1)S(1)} %bitcast.183, bf16[1024,12,64]{0,2,1:T(8,128)(2,1)S(1)} %bitcast.177), kind=kOutput, calls=%fused_computation.8 | convolution fusion | flops 830466048 | bytes 53264384 | tf_op jit(solution)/shard_map/while/body/eval_jaxpr/qhe,khe->hqk/dot_general | solution.py:135
  853.9 19.4 %convert_reduce_fusion.2 = (f32[12,1024]{1,0:T(8,128)S(1)}, f32[12,512]{1,0:T(8,128)}, bf16[12,512,1024]{2,1,0:T(8,128)(2,1)S(1)}) fusion(f32[12,512,1024]{2,1,0:T(8,128)} %get-tuple-element.144, f32[12,512]{1,0:T(8,128)S(1)} %get-tuple-element.143, f32[12,512,1024]{2,1,0:T(8,128)} %get-tuple-element.142, f32[12,512]{1,0:T(8,128)S(1)} %log_add_fusion.1, ...), kind=kLoop, calls=%fused_computation.2 | loop fusion | flops 50313216 | bytes 63561728 | tf_op jit(solution)/shard_map/while/body/eval_jaxpr/reduce_sum | solution.py:157
  873.4 6.2 multiply_convert_fusion.10
  879.6 5.2 fusion.79
  884.8 12.2 fusion.4
  897.0 17.9 %multiply_reduce_fusion = (f32[12,512]{1,0:T(8,128)}, f32[12,512,1024]{2,1,0:T(8,128)}) fusion(f32[12,512,1024]{2,1,0:T(8,128)} %get-tuple-element.140, f32[12,512]{1,0:T(8,128)S(1)} %log_add_fusion, pred[512,1024]{1,0:T(8,128)(4,1)S(1)} %copy-done.10, bf16[512,12,64]{0,2,1:T(8,128)(2,1)} %bitcast.185, bf16[1024,12,64]{0,2,1:T(8,128)(2,1)S(1)} %bitcast.178), kind=kOutput, calls=%fused_computation.5 | convolution fusion | flops 830466048 | bytes 53264384 | tf_op jit(solution)/shard_map/while/body/eval_jaxpr/qhe,khe->hqk/dot_general | solution.py:135
  914.9 12.8 add_convert_fusion
  927.7 19.0 %convert_reduce_fusion = (f32[12,1024]{1,0:T(8,128)S(1)}, f32[12,512]{1,0:T(8,128)S(1)}, bf16[12,512,1024]{2,1,0:T(8,128)(2,1)S(1)}) fusion(f32[12,512,1024]{2,1,0:T(8,128)} %get-tuple-element.146, f32[12,512]{1,0:T(8,128)} %get-tuple-element.145, f32[12,512,1024]{2,1,0:T(8,128)} %get-tuple-element.140, f32[12,512]{1,0:T(8,128)S(1)} %log_add_fusion, ...), kind=kLoop, calls=%fused_computation | loop fusion | flops 50313216 | bytes 63561728 | tf_op jit(solution)/shard_map/while/body/eval_jaxpr/reduce_sum | solution.py:157
  946.7 6.2 multiply_convert_fusion.9
  952.9 5.6 multiply_convert_fusion.5
  959.2 3.4 reduce-window.16
  963.7 3.8 fusion.55
  967.8 14.6 fusion.67
  982.4 3.6 bitcast_add_fusion
  987.9 20.2 %fusion.16 = f32[1536,2,2048]{2,0,1:T(8,128)} fusion(bf16[1024,1,2048]{2,0,1:T(8,128)(2,1)} %get-tuple-element.120, bf16[1024,1,2048]{2,0,1:T(8,128)(2,1)} %copy-done.42, bf16[1024,1536]{1,0:T(8,128)(2,1)S(1)} %copy-done.40), kind=kOutput, calls=%fused_computation.39 | convolution fusion | flops 12901679104 | bytes 36700160 | tf_op jit(solution)/shard_map/td,tkf->dkf/dot_general | solution.py:237
  1008.2 1.8 copy-done.2
  1010.0 14.7 fusion.43
  1026.6 11.4 fusion.81
  1039.4 6.7 fusion.80
  1048.0 54.9 %reduce-scatter.18.cloned.1.call-done = f32[512,1536]{1,0:T(8,128)} async-done(((f32[1024,1536]{1,0:T(8,128)}), f32[512,1536]{1,0:T(8,128)}) %reduce-scatter.18.cloned.1.call-update) | async-done | bytes 3145744 | tf_op jit(solution)/shard_map/reduce_scatter | solution.py:54
  1102.9 2.7 fusion.30
  1105.7 39.7 %all-reduce = (f32[1536]{0:T(1024)}, f32[24]{0:T(128)}, f32[1536]{0:T(1024)}) all-reduce(f32[1536]{0:T(1024)S(1)} %get-tuple-element.106, f32[24]{0:T(128)S(1)} %dynamic_update_slice.19, f32[1536]{0:T(1024)S(1)} %copy-done.35), channel_id=1, replica_groups=mesh['dp'=16,'tensor'=2] {'dp','tensor'}, use_global_device_ids=true, to_apply=%region_23.24 | all-reduce | flops 3096 | bytes 24768 | tf_op jit(solution)/shard_map/psum | solution.py:305
  1145.4 5.5 fusion.29
  1150.9 199.4 %reduce-scatter.24.cloned.1.call-done = f32[96,2,2048]{2,0,1:T(8,128)} async-done(((f32[1536,2,2048]{2,0,1:T(8,128)}), f32[96,2,2048]{2,0,1:T(8,128)}) %reduce-scatter.24.cloned.1.call-update) | async-done | bytes 1572880 | tf_op jit(solution)/shard_map/reduce_scatter | solution.py:299
  1350.3 3.8 copy.62
  1354.0 193.4 %reduce-scatter.20.cloned.1.call-done = f32[96,4,768]{2,0,1:T(8,128)} async-done(((f32[1536,4,768]{2,0,1:T(8,128)}), f32[96,4,768]{2,0,1:T(8,128)}) %reduce-scatter.20.cloned.1.call-update) | async-done | bytes 1179664 | tf_op jit(solution)/shard_map/reduce_scatter | solution.py:296
  1547.4 3.0 copy.61
  1550.5 135.4 %reduce-scatter.26.cloned.1.call-done = f32[2048,96]{0,1:T(8,128)} async-done(((f32[2048,1536]{0,1:T(8,128)}), f32[2048,96]{0,1:T(8,128)}) %reduce-scatter.26.cloned.1.call-update) | async-done | bytes 786448 | tf_op jit(solution)/shard_map/reduce_scatter | solution.py:300
  1685.9 79.1 %reduce-scatter.22.cloned.1.call-done = f32[768,96]{0,1:T(8,128)} async-done(((f32[768,1536]{0,1:T(8,128)}), f32[768,96]{0,1:T(8,128)}) %reduce-scatter.22.cloned.1.call-update) | async-done | bytes 294928 | tf_op jit(solution)/shard_map/reduce_scatter | solution.py:298
  (168 shorter events, 23.9 us)
Async XLA Ops:
  7.2 5.6 copy-start.24
  7.2 7.9 copy-start.38
  7.2 53.3 %all-gather.10.cloned.1.call-start = ((), (), s32[]{:S(2)}) async-start(), calls=%async_computation.9 | async-start | bytes 4718592 | tf_op jit(solution)/shard_map/all_gather | solution.py:37
  7.2 31.3 %copy-start.41 = (f32[24]{0:T(128)S(1)}, f32[24]{0:T(128)}, u32[]{:S(2)}) copy-start(f32[24]{0:T(128)} %param.15) | copy-start | bytes 292
  9.1 0.6 copy-start.36
  12.7 131.6 %all-gather.12.cloned.1.call-start = ((), (), s32[]{:S(2)}) async-start(), calls=%async_computation.10 | async-start | bytes 10027008 | tf_op jit(solution)/shard_map/all_gather | solution.py:26
  13.6 221.9 %all-gather.14.cloned.1.call-start = ((), (), s32[]{:S(2)}) async-start(), calls=%async_computation.11 | async-start | bytes 2506752 | tf_op jit(solution)/shard_map/all_gather | solution.py:28
  14.4 303.7 %reduce-scatter.12.cloned.1.call-start = ((), (), s32[]{:S(2)}) async-start(), calls=%async_computation.12 | async-start | bytes 9437184 | tf_op jit(solution)/shard_map/reduce_scatter | solution.py:45
  38.5 121.9 %copy-start.25 = (bf16[1536,12]{0,1:T(8,128)(2,1)}, bf16[1536,12]{0,1:T(8,128)(2,1)S(1)}, u32[]{:S(2)}) copy-start(bf16[1536,12]{0,1:T(8,128)(2,1)S(1)} %reshape.316) | copy-start | bytes 110596
  60.5 83.8 %copy-start.1 = (bf16[1024,1536]{1,0:T(8,128)(2,1)S(1)}, bf16[1024,1536]{1,0:T(8,128)(2,1)}, u32[]{:S(2)}) copy-start(bf16[1024,1536]{1,0:T(8,128)(2,1)} %all-gather.10.cloned.1.call-done) | copy-start | bytes 9437188
  160.5 4.3 copy-start.8
  162.0 14.1 copy-start.17
  162.0 35.6 %copy-start.18 = (bf16[512,1,768]{0,2,1:T(8,128)(2,1)}, bf16[512,1,768]{0,2,1:T(8,128)(2,1)S(1)}, u32[]{:S(2)}) copy-start(bf16[512,1,768]{0,2,1:T(8,128)(2,1)S(1)} %get-tuple-element.124) | copy-start | bytes 2359300
  164.8 32.9 %copy-start.6 = (bf16[1024,1,768]{0,2,1:T(8,128)(2,1)}, bf16[1024,1,768]{0,2,1:T(8,128)(2,1)S(1)}, u32[]{:S(2)}) copy-start(bf16[1024,1,768]{0,2,1:T(8,128)(2,1)S(1)} %get-tuple-element.126) | copy-start | bytes 4718596
  164.8 55.3 %copy-start.3 = (bf16[1024,1,768]{0,2,1:T(8,128)(2,1)}, bf16[1024,1,768]{0,2,1:T(8,128)(2,1)S(1)}, u32[]{:S(2)}) copy-start(bf16[1024,1,768]{0,2,1:T(8,128)(2,1)S(1)} %get-tuple-element.127) | copy-start | bytes 4718596
  176.1 11.1 copy-start.29
  187.2 10.4 copy-start.31
  187.2 10.5 copy-start.11
  230.7 1.7 copy-start.7
  235.5 6.8 copy-start.21
  242.3 1.1 copy-start.23
  242.3 179.0 %all-gather.18.cloned.1.call-start = ((), (), s32[]{:S(2)}) async-start(), calls=%async_computation.14 | async-start | bytes 13369344 | tf_op jit(solution)/shard_map/all_gather | solution.py:29
  244.6 76.4 %copy-start.33 = (f32[1536]{0:T(1024)S(1)}, f32[1536]{0:T(1024)}, u32[]{:S(2)}) copy-start(f32[1536]{0:T(1024)} %param.17) | copy-start | bytes 18436
  244.6 221.8 %all-gather.16.cloned.1.call-start = ((), (), s32[]{:S(2)}) async-start(), calls=%async_computation.13 | async-start | bytes 4718592 | tf_op jit(solution)/shard_map/all_gather | solution.py:37
  322.5 191.0 %all-gather.22.cloned.1.call-start = ((), (), s32[]{:S(2)}) async-start(), calls=%async_computation.17 | async-start | bytes 4718592 | tf_op jit(solution)/shard_map/all_gather | solution.py:41
  325.4 251.8 %all-gather.20.cloned.1.call-start = ((), (), s32[]{:S(2)}) async-start(), calls=%async_computation.15 | async-start | bytes 6684672 | tf_op jit(solution)/shard_map/all_gather | solution.py:30
  326.2 365.8 %reduce-scatter.16.cloned.1.call-start = ((), (), s32[]{:S(2)}) async-start(), calls=%async_computation.18 | async-start | bytes 9437184 | tf_op jit(solution)/shard_map/reduce_scatter | solution.py:54
  595.4 1.9 copy-start.42
  616.0 155.3 %reduce-scatter.14.cloned.1.call-start = ((), (), s32[]{:S(2)}) async-start(), calls=%async_computation.16 | async-start | bytes 9437184 | tf_op jit(solution)/shard_map/reduce_scatter | solution.py:45
  628.0 194.0 %all-gather.24.cloned.1.call-start = ((), (), s32[]{:S(2)}) async-start(), calls=%async_computation.19 | async-start | bytes 4718592 | tf_op jit(solution)/shard_map/all_gather | solution.py:41
  695.2 81.8 %copy-start.30 = (f32[12,512]{1,0:T(8,128)S(1)}, f32[12,512]{1,0:T(8,128)}, u32[]{:S(2)}) copy-start(f32[12,512]{1,0:T(8,128)} %copy-done.29) | copy-start | bytes 73732
  695.2 81.8 %copy-start.32 = (f32[12,512]{1,0:T(8,128)S(1)}, f32[12,512]{1,0:T(8,128)}, u32[]{:S(2)}) copy-start(f32[12,512]{1,0:T(8,128)} %copy-done.31) | copy-start | bytes 73732
  777.0 269.4 %reduce-scatter.28.cloned.1.call-start = ((), (), s32[]{:S(2)}) async-start(), calls=%async_computation.25 | async-start | bytes 835584
  777.1 55.0 %copy-start.12 = (pred[512,1024]{1,0:T(8,128)(4,1)S(1)}, pred[512,1024]{1,0:T(8,128)(4,1)}, u32[]{:S(2)}) copy-start(pred[512,1024]{1,0:T(8,128)(4,1)} %get-tuple-element.133) | copy-start | bytes 1572868
  831.1 1.7 copy-start.4
  832.1 21.9 %copy-start.14 = (bf16[512,768]{0,1:T(8,128)(2,1)}, bf16[512,768]{0,1:T(8,128)(2,1)S(1)}, u32[]{:S(2)}) copy-start(bf16[512,768]{0,1:T(8,128)(2,1)S(1)} %get-tuple-element.129) | copy-start | bytes 2359300
  879.6 5.2 copy-start.9
  879.6 5.2 copy-start.16
  884.8 12.2 copy-start.5
  884.8 12.2 copy-start.10
  897.0 17.9 %copy-start.13 = (pred[512,1024]{1,0:T(8,128)(4,1)S(1)}, pred[512,1024]{1,0:T(8,128)(4,1)}, u32[]{:S(2)}) copy-start(pred[512,1024]{1,0:T(8,128)(4,1)} %get-tuple-element.133) | copy-start | bytes 1572868
  897.0 17.9 %copy-start.15 = (bf16[512,768]{0,1:T(8,128)(2,1)S(1)}, bf16[512,768]{0,1:T(8,128)(2,1)}, u32[]{:S(2)}) copy-start(bf16[512,768]{0,1:T(8,128)(2,1)} %copy-done.14) | copy-start | bytes 2359300
  952.9 5.6 copy-start.28
  952.9 10.7 copy-start.27
  958.5 9.3 copy-start.19
  958.5 9.3 copy-start.20
  967.6 135.3 %reduce-scatter.18.cloned.1.call-start = ((), (), s32[]{:S(2)}) async-start(), calls=%async_computation.20 | async-start | bytes 9437184 | tf_op jit(solution)/shard_map/reduce_scatter | solution.py:54
  967.8 14.6 copy-start.26
  986.0 1.9 copy-start.40
  986.0 364.3 %reduce-scatter.24.cloned.1.call-start = ((), (), s32[]{:S(2)}) async-start(), calls=%async_computation.23 | async-start | bytes 26738688 | tf_op jit(solution)/shard_map/reduce_scatter | solution.py:299
  1008.1 1.9 copy-start.2
  1008.1 539.3 %reduce-scatter.20.cloned.1.call-start = ((), (), s32[]{:S(2)}) async-start(), calls=%async_computation.21 | async-start | bytes 20054016 | tf_op jit(solution)/shard_map/reduce_scatter | solution.py:296
  1024.7 1.9 copy-start.39
  1024.8 661.2 %reduce-scatter.26.cloned.1.call-start = ((), (), s32[]{:S(2)}) async-start(), calls=%async_computation.24 | async-start | bytes 13369344 | tf_op jit(solution)/shard_map/reduce_scatter | solution.py:300
  1038.0 1.4 copy-start.22
  1038.0 727.0 %reduce-scatter.22.cloned.1.call-start = ((), (), s32[]{:S(2)}) async-start(), calls=%async_computation.22 | async-start | bytes 5013504 | tf_op jit(solution)/shard_map/reduce_scatter | solution.py:298
  1046.1 56.8 %copy-start = (bf16[512,1536]{1,0:T(8,128)(2,1)S(1)}, bf16[512,1536]{1,0:T(8,128)(2,1)}, u32[]{:S(2)}) copy-start(bf16[512,1536]{1,0:T(8,128)(2,1)} %param.11) | copy-start | bytes 4718596
  1046.1 56.8 %copy-start.34 = (f32[1536]{0:T(1024)S(1)}, f32[1536]{0:T(1024)}, u32[]{:S(2)}) copy-start(f32[1536]{0:T(1024)} %param.12) | copy-start | bytes 18436
  1046.1 56.8 %copy-start.37 = (f32[512]{0:T(512)S(1)}, f32[512]{0:T(512)}, u32[]{:S(2)}) copy-start(f32[512]{0:T(512)} %copy-done.36) | copy-start | bytes 6148
  1046.1 59.6 %copy-start.35 = (f32[1536]{0:T(1024)S(1)}, f32[1536]{0:T(1024)}, u32[]{:S(2)}) copy-start(f32[1536]{0:T(1024)} %get-tuple-element.104) | copy-start | bytes 18436
Sparse Core Ops, SparseCore 0:
  12.8 47.6 all-gather.9
  63.3 80.9 all-gather.11
  146.6 40.7 all-gather.13
  242.5 75.6 reduce-scatter.11
  320.8 100.4 all-gather.17
  423.3 43.1 all-gather.15
  468.6 44.8 all-gather.21
  515.8 61.3 all-gather.19
  616.1 75.8 reduce-scatter.15
  694.1 77.1 reduce-scatter.13
  777.1 44.9 all-gather.23
  967.7 56.7 reduce-scatter.27
  1026.7 76.1 reduce-scatter.17
  1106.9 243.3 reduce-scatter.23
  1354.2 193.1 reduce-scatter.19
  1551.9 133.9 reduce-scatter.25
  1690.2 74.8 reduce-scatter.21
where the time goes:
time: 1780 us; the launch traced here: 1770 us
  waiting for transfers between devices  1250 us (70%)
  matrix products  311 us (17%)
  other arithmetic  102 us (6%)
  blocking collectives  63 us (4%)
  local copies, waits for them, and re-layouts  30.5 us (2%)
    reduce_scatter x1, waiting for transfers between devices, on_device(): lax.psum_scatter(grad_w_mlp, 'dp', scatter_dimension=0, tiled=True)  199 us
    reduce_scatter x1, waiting for transfers between devices, on_device(): lax.psum_scatter(grad_w_attn, 'dp', scatter_dimension=0, tiled=True)  193 us
    reduce_scatter x2, waiting for transfers between devices, branch_sum(): lax.psum_scatter(term_fn(jnp.int32(0), own_rows * lax.axis_size('tensor')...  150 us
    reduce_scatter x1, waiting for transfers between devices, on_device(): lax.psum_scatter(grad_w_down, 'dp', scatter_dimension=1, tiled=True)  135 us
    reduce_scatter x2, waiting for transfers between devices, input_sum(): lax.psum_scatter(term_fn(jnp.int32(0), own_rows * lax.axis_size('tensor')...  119 us
    all_gather x1, waiting for transfers between devices, gather_weights(): lax.all_gather(w_mlp, 'dp', axis=0, tiled=True)  95 us
    reduce_scatter x1, waiting for transfers between devices, on_device(): lax.psum_scatter(grad_w_out, 'dp', scatter_dimension=1, tiled=True)  79.1 us
    all_gather x1, waiting for transfers between devices, gather_weights(): lax.all_gather(w_attn, 'dp', axis=0, tiled=True)  76.3 us
  transfers between devices with their start and end apart: 17, of which 15 were waited for; matrix products, arithmetic and copies ran while one was open for 13% of the time, Pallas kernels for 0%

commit v1 on v0

v1 whole, which is shorter than its diff:
```python
import jax
import jax.numpy as jnp
from jax import lax
from jax.sharding import PartitionSpec as P

HEAD = 64
SLOTS = 1024
EPS = 1e-06
PAD = 128

BF16 = jnp.bfloat16
F32 = jnp.float32


def norm_parts(rows):
    inverse = lax.rsqrt(jnp.mean(rows * rows, axis=-1, keepdims=True) + EPS)
    return (rows * inverse, inverse)


def norm_back(grad_normed, scaled, inverse, gain):
    grad_scaled = grad_normed * gain
    inner_sum = jnp.mean(grad_scaled * scaled, axis=-1, keepdims=True)
    return inverse * (grad_scaled - scaled * inner_sum)


def dot_nn(a, b):
    return lax.dot_general(a, b, (((1,), (0,)), ((), ())), preferred_element_type=F32)


def dot_nt(a, b):
    return lax.dot_general(a, b, (((1,), (1,)), ((), ())), preferred_element_type=F32)


def dot_tn(a, b):
    return lax.dot_general(a, b, (((0,), (0,)), ((), ())), preferred_element_type=F32)


def swap(rows):
    return lax.ppermute(rows, "tensor", [(0, 1), (1, 0)])


def share_rows(own):
    if lax.axis_size("tensor") != 2:
        return lax.all_gather(own, "tensor", axis=0, tiled=True)
    other = swap(own)
    first = lax.axis_index("tensor") == 0
    return jnp.concatenate([jnp.where(first, own, other), jnp.where(first, other, own)], axis=0)


def sum_rows(term_fn, own_rows):
    size = lax.axis_size("tensor")
    if size != 2:
        term = term_fn(jnp.int32(0), own_rows * size).astype(BF16)
        return lax.psum_scatter(term, "tensor", scatter_dimension=0, tiled=True).astype(F32)
    index = lax.axis_index("tensor")
    sent = swap(term_fn((1 - index) * own_rows, own_rows).astype(BF16))
    return term_fn(index * own_rows, own_rows) + sent.astype(F32)


def gather_dp(shard):
    return lax.all_gather(shard, "dp", axis=0, tiled=True)


def scatter_dp(grad):
    return lax.psum_scatter(grad, "dp", scatter_dimension=0, tiled=True)


def block_scores(queries, key_rows, decays, length, block_start, block_rows):
    picked = lax.slice_in_dim(queries, block_start, block_start + block_rows, axis=0)
    scores = jnp.einsum(
        "qhe,khe->hqk", picked, key_rows, preferred_element_type=jnp.float32
    ) * HEAD ** (-0.5)
    scores = (
        scores + decays[block_start : block_start + block_rows].T[:, :, None] - decays.T[:, None, :]
    )
    query_pos = block_start + jnp.arange(block_rows, dtype=jnp.int32)
    key_pos = jnp.arange(SLOTS, dtype=jnp.int32)
    allowed = (key_pos[None, :] <= query_pos[:, None]) & (key_pos[None, :] < length)
    return (picked, jnp.where(allowed[None], scores, -1e30), allowed[None])


def sequence_forward(packed):
    queries, key_rows, value_rows, decays, length = packed
    block_rows = min(512, SLOTS)
    outputs = []
    log_totals = []
    for block_start in range(0, SLOTS, block_rows):
        picked, scores, allowed = block_scores(
            queries, key_rows, decays, length, block_start, block_rows
        )
        row_max = jnp.max(scores, axis=-1, keepdims=True)
        exponent = jnp.exp(scores - row_max)
        totals = jnp.sum(exponent, axis=-1, keepdims=True)
        soft_low = (exponent / totals).astype(jnp.bfloat16)
        outputs.append(
            jnp.einsum("hqk,khe->qhe", soft_low, value_rows, preferred_element_type=jnp.float32)
        )
        log_totals.append((row_max + jnp.log(totals))[:, :, 0])
    return (jnp.concatenate(outputs, axis=0), jnp.concatenate(log_totals, axis=1))


def sequence_backward(packed):
    queries, key_rows, value_rows, decays, length, log_totals, grad_attended = packed
    block_rows = min(512, SLOTS)
    score_scale = HEAD ** (-0.5)
    grad_keys = jnp.zeros(key_rows.shape, jnp.float32)
    grad_values = jnp.zeros(value_rows.shape, jnp.float32)
    column_terms = jnp.zeros((decays.shape[1], decays.shape[0]), jnp.float32)
    query_grads = []
    row_terms = []
    for block_start in range(0, SLOTS, block_rows):
        picked, scores, allowed = block_scores(
            queries, key_rows, decays, length, block_start, block_rows
        )
        shifted = scores - log_totals[:, block_start : block_start + block_rows, None]
        soft = jnp.where(allowed, jnp.exp(shifted), 0.0)
        grad_picked = lax.slice_in_dim(grad_attended, block_start, block_start + block_rows, axis=0)
        grad_soft = jnp.einsum(
            "qhe,khe->hqk", grad_picked, value_rows, preferred_element_type=jnp.float32
        )
        inner_sum = jnp.sum(soft * grad_soft, axis=-1, keepdims=True)
        grad_scores = (soft * (grad_soft - inner_sum)).astype(jnp.bfloat16)
        query_grads.append(
            jnp.einsum("hqk,khe->qhe", grad_scores, key_rows, preferred_element_type=jnp.float32)
            * score_scale
        )
        grad_keys = (
            grad_keys
            + jnp.einsum("hqk,qhe->khe", grad_scores, picked, preferred_element_type=jnp.float32)
            * score_scale
        )
        grad_values = grad_values + jnp.einsum(
            "hqk,qhe->khe",
            soft.astype(jnp.bfloat16),
            grad_picked,
            preferred_element_type=jnp.float32,
        )
        wide_grads = grad_scores.astype(jnp.float32)
        row_terms.append(jnp.sum(wide_grads, axis=2))
        column_terms = column_terms - jnp.sum(wide_grads, axis=1)
    grad_decay = jnp.concatenate(row_terms, axis=1) + column_terms
    grad_forget = jnp.cumsum(grad_decay[:, ::-1], axis=1)[:, ::-1].T
    return (
        jnp.concatenate(query_grads, axis=0).astype(jnp.bfloat16),
        grad_keys.astype(jnp.bfloat16),
        grad_values.astype(jnp.bfloat16),
        grad_forget,
    )


def on_device(
    layer_input,
    gain_attn,
    w_attn,
    w_forget,
    forget_bias,
    w_out,
    gain_mlp,
    w_mlp,
    w_down,
    lengths,
    cotangent,
):
    own_rows, width = layer_input.shape
    group_seqs = lengths.shape[0]
    group_rows = group_seqs * SLOTS
    part = w_attn.shape[2]
    heads_dev = part // HEAD
    units = w_mlp.shape[2]
    own_d = w_attn.shape[0]
    tensor_index = lax.axis_index("tensor")
    bias_own = lax.dynamic_slice_in_dim(forget_bias, tensor_index * heads_dev, heads_dev)
    positions = tensor_index * own_rows + jnp.arange(own_rows, dtype=jnp.int32)
    seq_of_row = positions // SLOTS
    matches = seq_of_row[:, None] == jnp.arange(group_seqs, dtype=jnp.int32)[None, :]
    own_lengths = jnp.sum(jnp.where(matches, lengths[None, :], 0), axis=1)
    valid = (positions % SLOTS < own_lengths).astype(F32)[:, None]

    attn_shard = jnp.concatenate(
        [w_attn.reshape(own_d, 4 * part), jnp.pad(w_forget, ((0, 0), (0, PAD - heads_dev)))], axis=1
    )
    attn_full = gather_dp(attn_shard)
    out_full = gather_dp(w_out.T)
    down_full = gather_dp(w_down.T)
    mlp_full = gather_dp(w_mlp.reshape(own_d, 2 * units))

    input_wide = layer_input.astype(F32)
    scaled_attn, inverse_attn = norm_parts(input_wide)
    normed_all = share_rows((scaled_attn * gain_attn).astype(BF16))
    grad_final = cotangent.astype(F32) * valid
    grad_final_all = share_rows(grad_final.astype(BF16))

    proj = dot_nn(normed_all, attn_full[:, : 3 * part]).astype(BF16)
    gate_logit = dot_nn(normed_all, attn_full[:, 3 * part :])
    out_gate = gate_logit[:, :part]
    logits = gate_logit[:, part : part + heads_dev] + bias_own

    def split_heads(column):
        return proj[:, column * part : (column + 1) * part].reshape(
            group_seqs, SLOTS, heads_dev, HEAD
        )

    queries, key_rows, value_rows = (split_heads(0), split_heads(1), split_heads(2))
    log_forget = jax.nn.log_sigmoid(logits)
    decays = jnp.cumsum(log_forget.reshape(group_seqs, SLOTS, heads_dev), axis=1)
    attended, log_totals = lax.map(
        sequence_forward, (queries, key_rows, value_rows, decays, lengths)
    )
    attended = attended.reshape(group_rows, part)
    gate_sig = jax.nn.sigmoid(out_gate)
    gated = (attended * gate_sig).astype(BF16)

    def attn_term(first_row, row_count):
        return dot_nt(lax.dynamic_slice_in_dim(gated, first_row, row_count), out_full)

    middle = input_wide + sum_rows(attn_term, own_rows)
    scaled_mlp, inverse_mlp = norm_parts(middle)
    normed_mid = share_rows((scaled_mlp * gain_mlp).astype(BF16))
    grad_hidden = dot_nn(grad_final_all, down_full)
    gate_pre = dot_nn(normed_mid, mlp_full[:, :units])
    up_pre = dot_nn(normed_mid, mlp_full[:, units:])
    gate_s = jax.nn.sigmoid(gate_pre)
    silu = gate_pre * gate_s
    hidden = (silu * up_pre).astype(BF16)
    grad_gate = (grad_hidden * up_pre * gate_s * (1.0 + gate_pre * (1.0 - gate_s))).astype(BF16)
    grad_up = (grad_hidden * silu).astype(BF16)
    grad_pair = jnp.concatenate([grad_gate, grad_up], axis=1)

    def mlp_back_term(first_row, row_count):
        return dot_nt(lax.dynamic_slice_in_dim(grad_pair, first_row, row_count), mlp_full)

    grad_normed_mlp = sum_rows(mlp_back_term, own_rows)
    down_part = scatter_dp(dot_tn(grad_final_all, hidden).astype(BF16))
    mlp_part = scatter_dp(dot_tn(normed_mid, grad_pair).astype(BF16))

    gain_mlp_part = jnp.sum(scaled_mlp * grad_normed_mlp, axis=0)
    grad_middle = grad_final + norm_back(grad_normed_mlp, scaled_mlp, inverse_mlp, gain_mlp)
    grad_branch_all = share_rows(grad_middle.astype(BF16))

    def mlp_term(first_row, row_count):
        return dot_nt(lax.dynamic_slice_in_dim(hidden, first_row, row_count), down_full)

    layer_output = (valid * (middle + sum_rows(mlp_term, own_rows))).astype(BF16)

    grad_gated = dot_nn(grad_branch_all, out_full)
    out_part = scatter_dp(dot_tn(grad_branch_all, gated).astype(BF16))
    grad_attended = (grad_gated * gate_sig).astype(BF16)
    grad_out_gate = (grad_gated * attended * gate_sig * (1.0 - gate_sig)).astype(BF16)
    grad_heads = grad_attended.reshape(group_seqs, SLOTS, heads_dev, HEAD)
    grad_queries, grad_keys, grad_values, grad_forget = lax.map(
        sequence_backward, (queries, key_rows, value_rows, decays, lengths, log_totals, grad_heads)
    )
    grad_logit = grad_forget.reshape(group_rows, heads_dev) * jax.nn.sigmoid(-logits)
    bias_part = jnp.sum(grad_logit, axis=0)
    grad_proj = jnp.concatenate(
        [
            grad_queries.reshape(group_rows, part),
            grad_keys.reshape(group_rows, part),
            grad_values.reshape(group_rows, part),
            grad_out_gate,
            jnp.pad(grad_logit.astype(BF16), ((0, 0), (0, PAD - heads_dev))),
        ],
        axis=1,
    )
    attn_part = scatter_dp(dot_tn(normed_all, grad_proj).astype(BF16))

    def attn_back_term(first_row, row_count):
        return dot_nt(lax.dynamic_slice_in_dim(grad_proj, first_row, row_count), attn_full)

    grad_normed_attn = sum_rows(attn_back_term, own_rows)
    gain_attn_part = jnp.sum(scaled_attn * grad_normed_attn, axis=0)
    grad_input = grad_middle + norm_back(grad_normed_attn, scaled_attn, inverse_attn, gain_attn)
    bias_full = lax.dynamic_update_slice_in_dim(
        jnp.zeros(forget_bias.shape, F32), bias_part, tensor_index * heads_dev, 0
    )
    grad_gain_attn, grad_gain_mlp, grad_forget_bias = lax.psum(
        (gain_attn_part, gain_mlp_part, bias_full), ("dp", "tensor")
    )
    attn_part = attn_part.astype(F32)
    return (
        layer_output,
        grad_input,
        grad_gain_attn,
        attn_part[:, : 4 * part].reshape(own_d, 4, part),
        attn_part[:, 4 * part : 4 * part + heads_dev],
        grad_forget_bias,
        out_part.astype(F32).T,
        grad_gain_mlp,
        mlp_part.astype(F32).reshape(own_d, 2, units),
        down_part.astype(F32).T,
    )


def solution(mesh):
    placed = (
        P(("dp", "tensor"), None),
        P(),
        P("dp", None, "tensor"),
        P("dp", "tensor"),
        P(),
        P("tensor", "dp"),
        P(),
        P("dp", None, "tensor"),
        P("tensor", "dp"),
        P("dp"),
        P(("dp", "tensor"), None),
    )
    return jax.shard_map(
        on_device,
        mesh=mesh,
        in_specs=placed,
        out_specs=(
            P(("dp", "tensor"), None),
            P(("dp", "tensor"), None),
            P(),
            P("dp", None, "tensor"),
            P("dp", "tensor"),
            P(),
            P("tensor", "dp"),
            P(),
            P("dp", None, "tensor"),
            P("tensor", "dp"),
        ),
        check_vma=False,
    )
```

time: 1780 us -> 924 us (0.52)
  waiting for transfers between devices: 1250 us -> 374 us
  blocking collectives: 63 us -> 39.5 us
    reduce_scatter x8 -> x4, waiting for transfers between devices: 876 us -> 92.4 us  [scatter_dp(): return lax.psum_scatter(grad, 'dp', scatter_dimension=0, tiled=True)]
    all_gather x8 -> x4, waiting for transfers between devices: 372 us -> 42.9 us  [gather_dp(): return lax.all_gather(shard, 'dp', axis=0, tiled=True)]
    ppermute x0 -> x8, waiting for transfers between devices: none -> 238 us  [swap(): return lax.ppermute(rows, 'tensor', [(0, 1), (1, 0)])]
    all_gather x1 -> x0, blocking collectives: 23.3 us -> none  [gather_weights(): lax.all_gather(w_forget, 'dp', axis=0, tiled=True)]
    dot_general x14 -> x18, matrix products: 176 us -> 184 us  [the longest x8 69.3 us: dot_nt(): lax.dot_general(a, b, (((1,), (1,)), ((), ())), preferred_element_type=F32)]
  transfers between devices with their start and end apart: 17 -> 16, of which waited for: 15 -> 10; matrix products, arithmetic and copies ran while one was open for 13% -> 44% of each run, Pallas kernels for 0% -> 0%
where the time goes in v1:
time: 924 us; the launch traced here: 918 us
  waiting for transfers between devices  374 us (40%)
  matrix products  321 us (35%)
  other arithmetic  113 us (12%)
  local copies, waits for them, and re-layouts  40.8 us (4%)
  blocking collectives  39.5 us (4%)
  between operations  15.8 us (2%)
  starting transfers between devices  13.7 us (1%)
    ppermute x8, waiting for transfers between devices, swap(): return lax.ppermute(rows, 'tensor', [(0, 1), (1, 0)])  238 us
    reduce_scatter x4, waiting for transfers between devices, scatter_dp(): return lax.psum_scatter(grad, 'dp', scatter_dimension=0, tiled=True)  92.4 us
    dot_general x8, matrix products, dot_nt(): lax.dot_general(a, b, (((1,), (1,)), ((), ())), preferred_element_type=F32)  69.3 us
    dot_general x6, matrix products, dot_nn(): lax.dot_general(a, b, (((1,), (0,)), ((), ())), preferred_element_type=F32)  63.7 us
    dot_general x4, matrix products, dot_tn(): lax.dot_general(a, b, (((0,), (0,)), ((), ())), preferred_element_type=F32)  51.1 us
    reduce_sum x2, other arithmetic, sequence_backward(): column_terms = column_terms - jnp.sum(wide_grads, axis=1)  47.8 us
    dot_general x2, matrix products, sequence_backward(): jnp.einsum('qhe,khe->hqk', grad_picked, value_rows, preferred_element_typ...  43.6 us
    all_gather x4, waiting for transfers between devices, gather_dp(): return lax.all_gather(shard, 'dp', axis=0, tiled=True)  42.9 us
  transfers between devices with their start and end apart: 16, of which 10 were waited for; matrix products, arithmetic and copies ran while one was open for 44% of the time, Pallas kernels for 0%

profile of v1, /device:TPU:0, one launch (start us, length us, event | category | flops | bytes accessed | tf_op | source)
XLA Modules:
  0.0 917.7 jit_solution(11367068304897842038)
XLA Ops:
  13.1 3.1 collective-permute-start
  18.5 32.2 %collective-permute-done = bf16[512,1536]{1,0:T(8,128)(2,1)} collective-permute-done((bf16[512,1536]{1,0:T(8,128)(2,1)S(1)}, bf16[512,1536]{1,0:T(8,128)(2,1)}, u32[]{:S(2)}, u32[]{:S(2)}) %collective-permute-start) | collective-permute-done | bytes 1572896 | tf_op jit(solution)/shard_map/ppermute | solution.py:39
  50.7 3.5 broadcast_select_fusion.7
  54.1 42.8 %all-gather.5.cloned.1.call-done = bf16[1536,3200]{1,0:T(8,128)(2,1)} async-done(((bf16[96,3200]{1,0:T(8,128)(2,1)}), bf16[1536,3200]{1,0:T(8,128)(2,1)}) %all-gather.5.cloned.1.call-update) | async-done | bytes 9830416 | tf_op jit(solution)/shard_map/all_gather | solution.py:61
  97.0 5.5 fusion.61
  102.5 1.9 copy-done.24
  104.6 3.7 reduce-window.14
  108.8 10.5 %fusion.23 = bf16[1024,2304]{1,0:T(8,128)(2,1)S(1)} fusion(bf16[1536,3200]{1,0:T(8,128)(2,1)} %all-gather.5.cloned.1.call-done, bf16[512,1536]{1,0:T(8,128)(2,1)S(1)} %copy-done.29, bf16[512,1536]{1,0:T(8,128)(2,1)S(1)} %get-tuple-element.122), kind=kOutput, calls=%fused_computation.49 | convolution fusion | flops 7256408064 | bytes 14942208 | tf_op jit(solution)/shard_map/dot_general | solution.py:27
  122.6 2.9 copy.41
  125.5 2.3 copy.47
  127.8 1.7 copy.40
  129.6 13.4 %fusion.117 = (f32[12,512]{1,0:T(8,128)S(1)}, f32[12,512,1024]{2,1,0:T(8,128)}) fusion(f32[12,1024]{1,0:T(8,128)S(1)} %bitcast.155, f32[12,512]{1,0:T(8,128)S(1)} %get-tuple-element.142, bf16[512,12,64]{0,2,1:T(8,128)(2,1)} %bitcast.135, bf16[1024,12,64]{0,2,1:T(8,128)(2,1)S(1)} %bitcast.125, pred[512,1024]{1,0:T(8,128)(4,1)} %get-tuple-element.129), kind=kOutput, calls=%fused_computation.201 | convolution fusion | flops 836757504 | bytes 28147712 | tf_op jit(solution)/shard_map/while/body/eval_jaxpr/qhe,khe->hqk/dot_general | solution.py:70
  143.0 11.3 %fusion.1 = f32[12,512]{1,0:T(8,128)S(1)} fusion(f32[12,512,1024]{2,1,0:T(8,128)} %get-tuple-element.131, f32[12,512]{1,0:T(8,128)S(1)} %get-tuple-element.130), kind=kLoop, calls=%fused_computation.17 | loop fusion | flops 12576768 | bytes 25214976 | tf_op jit(solution)/shard_map/while/body/eval_jaxpr/reduce_sum | solution.py:93
  154.3 10.5 %fusion.74 = f32[512,12,64]{0,2,1:T(8,128)S(1)} fusion(bf16[1024,12,64]{0,2,1:T(8,128)(2,1)S(1)} %bitcast.121, f32[12,512,1024]{2,1,0:T(8,128)} %get-tuple-element.131, f32[12,512]{1,0:T(8,128)S(1)} %fusion.1, f32[12,512]{1,0:T(8,128)S(1)} %get-tuple-element.130), kind=kOutput, calls=%fused_computation.127 | convolution fusion | flops 824180736 | bytes 28360704 | tf_op jit(solution)/shard_map/while/body/eval_jaxpr/hqk,khe->qhe/dot_general | solution.py:96
  164.9 11.9 %fusion.118 = (f32[12,512]{1,0:T(8,128)S(1)}, f32[12,512,1024]{2,1,0:T(8,128)}) fusion(f32[12,1024]{1,0:T(8,128)S(1)} %bitcast.156, f32[12,512]{1,0:T(8,128)S(1)} %get-tuple-element.143, bf16[512,12,64]{0,2,1:T(8,128)(2,1)S(1)} %bitcast.137, bf16[1024,12,64]{0,2,1:T(8,128)(2,1)S(1)} %bitcast.126, pred[512,1024]{1,0:T(8,128)(4,1)S(1)} %copy-done.12), kind=kOutput, calls=%fused_computation.202 | convolution fusion | flops 836757504 | bytes 28147712 | tf_op jit(solution)/shard_map/while/body/eval_jaxpr/qhe,khe->hqk/dot_general | solution.py:70
  176.8 11.6 %fusion = f32[12,512]{1,0:T(8,128)S(1)} fusion(f32[12,512,1024]{2,1,0:T(8,128)} %get-tuple-element.133, f32[12,512]{1,0:T(8,128)S(1)} %get-tuple-element.132), kind=kLoop, calls=%fused_computation.16 | loop fusion | flops 12576768 | bytes 25214976 | tf_op jit(solution)/shard_map/while/body/eval_jaxpr/reduce_sum | solution.py:93
  188.4 10.5 %fusion.75 = f32[512,12,64]{0,2,1:T(8,128)S(1)} fusion(bf16[1024,12,64]{0,2,1:T(8,128)(2,1)S(1)} %bitcast.122, f32[12,512,1024]{2,1,0:T(8,128)} %get-tuple-element.133, f32[12,512]{1,0:T(8,128)S(1)} %fusion, f32[12,512]{1,0:T(8,128)S(1)} %get-tuple-element.132), kind=kOutput, calls=%fused_computation.128 | convolution fusion | flops 824180736 | bytes 28360704 | tf_op jit(solution)/shard_map/while/body/eval_jaxpr/hqk,khe->qhe/dot_general | solution.py:96
  203.0 4.9 convolution_convert_fusion.5
  207.9 1.8 collective-permute-start.1
  211.5 34.0 %collective-permute-done.1 = bf16[512,1536]{1,0:T(8,128)(2,1)} collective-permute-done((bf16[512,1536]{1,0:T(8,128)(2,1)}, bf16[512,1536]{1,0:T(8,128)(2,1)}, u32[]{:S(2)}, u32[]{:S(2)}) %collective-permute-start.1) | collective-permute-done | bytes 1572896 | tf_op jit(solution)/shard_map/ppermute | solution.py:39
  245.5 4.5 multiply_reduce_fusion.4
  250.4 1.8 collective-permute-start.2
  252.2 27.0 %collective-permute-done.4 = bf16[512,1536]{1,0:T(8,128)(2,1)} collective-permute-done((bf16[512,1536]{1,0:T(8,128)(2,1)}, bf16[512,1536]{1,0:T(8,128)(2,1)}, u32[]{:S(2)}, u32[]{:S(2)}) %collective-permute-start.4) | collective-permute-done | bytes 1572896 | tf_op jit(solution)/shard_map/ppermute | solution.py:39
  279.2 3.8 broadcast_select_fusion.3
  283.0 29.1 %collective-permute-done.2 = bf16[512,1536]{1,0:T(8,128)(2,1)S(1)} collective-permute-done((bf16[512,1536]{1,0:T(8,128)(2,1)S(1)}, bf16[512,1536]{1,0:T(8,128)(2,1)S(1)}, u32[]{:S(2)}, u32[]{:S(2)}) %collective-permute-start.2) | collective-permute-done | bytes 1572896 | tf_op jit(solution)/shard_map/ppermute | solution.py:39
  312.0 2.4 broadcast_select_fusion.5
  314.5 12.6 %fusion.19 = f32[1024,2048]{1,0:T(8,128)} fusion(bf16[1536,4096]{1,0:T(8,128)(2,1)} %all-gather.9.cloned.1.call-done, bf16[512,1536]{1,0:T(8,128)(2,1)} %get-tuple-element.121, bf16[512,1536]{1,0:T(8,128)(2,1)} %get-tuple-element.120), kind=kOutput, calls=%fused_computation.45 | convolution fusion | flops 6448742400 | bytes 17825792 | tf_op jit(solution)/shard_map/dot_general | solution.py:27
  327.1 9.1 fusion.21
  336.2 17.5 %multiply_convert_fusion.2 = (bf16[1024,2048]{1,0:T(8,128)(2,1)}, bf16[1024,2048]{1,0:T(8,128)(2,1)}, bf16[1024,2048]{1,0:T(8,128)(2,1)}) fusion(f32[1024,2048]{1,0:T(8,128)} %fusion.21, f32[1024,2048]{1,0:T(8,128)} %fusion.19, bf16[1536,2048]{1,0:T(8,128)(2,1)} %all-gather.11.cloned.1.call-done, bf16[512,1536]{1,0:T(8,128)(2,1)} %get-tuple-element.119, ...), kind=kOutput, calls=%fused_computation.37 | convolution fusion | flops 6480199680 | bytes 38797312 | tf_op jit(solution)/shard_map/dot_general | solution.py:27
  353.7 10.9 %fusion.58 = bf16[512,1536]{1,0:T(8,128)(2,1)S(1)} fusion(bf16[1536,4096]{1,0:T(8,128)(2,1)} %all-gather.9.cloned.1.call-done, s32[]{:T(128)S(6)} %select_n.122, bf16[1024,2048]{1,0:T(8,128)(2,1)} %get-tuple-element.108, bf16[1024,2048]{1,0:T(8,128)(2,1)} %get-tuple-element.107), kind=kOutput, calls=%fused_computation.104 | convolution fusion | flops 6451625984 | bytes 22544388 | tf_op jit(solution)/shard_map/dot_general | solution.py:31
  364.7 1.7 collective-permute-start.5
  366.4 34.1 %collective-permute-done.5 = bf16[512,1536]{1,0:T(8,128)(2,1)} collective-permute-done((bf16[512,1536]{1,0:T(8,128)(2,1)S(1)}, bf16[512,1536]{1,0:T(8,128)(2,1)}, u32[]{:S(2)}, u32[]{:S(2)}) %collective-permute-start.5) | collective-permute-done | bytes 1572896 | tf_op jit(solution)/shard_map/ppermute | solution.py:39
  400.5 15.0 %multiply_reduce_fusion.2 = (f32[1536]{0:T(1024)}, f32[512]{0:T(512)S(1)}, f32[512,1536]{1,0:T(8,128)}) fusion(f32[512,1536]{1,0:T(8,128)S(1)} %get-tuple-element.135, f32[512]{0:T(512)S(1)} %add_rsqrt_fusion, bf16[512,1536]{1,0:T(8,128)(2,1)} %collective-permute-done.5, f32[1536]{0:T(1024)S(1)} %copy-done.49, ...), kind=kOutput, calls=%fused_computation.88 | convolution fusion | flops 6457128960 | bytes 28852228 | tf_op jit(solution)/shard_map/dot_general | solution.py:31
  415.5 5.7 fusion.112
  422.8 33.2 %collective-permute-done.6 = bf16[512,1536]{1,0:T(8,128)(2,1)S(1)} collective-permute-done((bf16[512,1536]{1,0:T(8,128)(2,1)S(1)}, bf16[512,1536]{1,0:T(8,128)(2,1)S(1)}, u32[]{:S(2)}, u32[]{:S(2)}) %collective-permute-start.6) | collective-permute-done | bytes 1572896 | tf_op jit(solution)/shard_map/ppermute | solution.py:39
  458.1 3.9 convolution_convert_fusion.3
  462.2 10.8 %convolution_convert_fusion.2 = bf16[1536,2048]{1,0:T(8,128)(2,1)} fusion(bf16[1024,2048]{1,0:T(8,128)(2,1)} %get-tuple-element.109, bf16[512,1536]{1,0:T(8,128)(2,1)S(1)} %copy-done.32, bf16[512,1536]{1,0:T(8,128)(2,1)S(1)} %copy-done.31), kind=kOutput, calls=%fused_computation.42 | convolution fusion | flops 6451888128 | bytes 13631488 | tf_op jit(solution)/shard_map/dot_general | solution.py:35
  475.0 8.4 fusion.53
  485.2 21.7 %multiply_reduce_fusion.1 = (f32[12,512]{1,0:T(8,128)}, f32[12,512,1024]{2,1,0:T(8,128)}) fusion(f32[12,512,1024]{2,1,0:T(8,128)} %get-tuple-element.133, f32[12,512]{1,0:T(8,128)S(1)} %log_add_fusion.1, pred[512,1024]{1,0:T(8,128)(4,1)S(1)} %copy-done.13, bf16[512,12,64]{0,2,1:T(8,128)(2,1)S(1)} %bitcast.130, bf16[1024,12,64]{0,2,1:T(8,128)(2,1)S(1)} %bitcast.123), kind=kOutput, calls=%fused_computation.8 | convolution fusion | flops 830466048 | bytes 53264384 | tf_op jit(solution)/shard_map/while/body/eval_jaxpr/qhe,khe->hqk/dot_general | solution.py:118
  506.9 23.7 %convert_reduce_fusion.2 = (f32[12,1024]{1,0:T(8,128)S(1)}, f32[12,512]{1,0:T(8,128)}, bf16[12,512,1024]{2,1,0:T(8,128)(2,1)}) fusion(f32[12,512,1024]{2,1,0:T(8,128)} %get-tuple-element.140, f32[12,512]{1,0:T(8,128)} %get-tuple-element.139, f32[12,512,1024]{2,1,0:T(8,128)} %get-tuple-element.133, f32[12,512]{1,0:T(8,128)S(1)} %log_add_fusion.1, ...), kind=kLoop, calls=%fused_computation.2 | loop fusion | flops 50313216 | bytes 63561728 | tf_op jit(solution)/shard_map/while/body/eval_jaxpr/reduce_sum | solution.py:140
  530.7 21.9 %multiply_reduce_fusion = (f32[12,512]{1,0:T(8,128)S(1)}, f32[12,512,1024]{2,1,0:T(8,128)}) fusion(f32[12,512,1024]{2,1,0:T(8,128)} %get-tuple-element.131, f32[12,512]{1,0:T(8,128)S(1)} %log_add_fusion, pred[512,1024]{1,0:T(8,128)(4,1)S(1)} %copy-done.15, bf16[512,12,64]{0,2,1:T(8,128)(2,1)S(1)} %bitcast.132, bf16[1024,12,64]{0,2,1:T(8,128)(2,1)S(1)} %bitcast.124), kind=kOutput, calls=%fused_computation.5 | convolution fusion | flops 830466048 | bytes 53264384 | tf_op jit(solution)/shard_map/while/body/eval_jaxpr/qhe,khe->hqk/dot_general | solution.py:118
  552.6 24.0 %convert_reduce_fusion = (f32[12,1024]{1,0:T(8,128)S(1)}, f32[12,512]{1,0:T(8,128)S(1)}, bf16[12,512,1024]{2,1,0:T(8,128)(2,1)}) fusion(f32[12,512,1024]{2,1,0:T(8,128)} %get-tuple-element.138, f32[12,512]{1,0:T(8,128)S(1)} %get-tuple-element.137, f32[12,512,1024]{2,1,0:T(8,128)} %get-tuple-element.131, f32[12,512]{1,0:T(8,128)S(1)} %log_add_fusion, ...), kind=kLoop, calls=%fused_computation | loop fusion | flops 50313216 | bytes 63561728 | tf_op jit(solution)/shard_map/while/body/eval_jaxpr/reduce_sum | solution.py:140
  577.3 3.4 reduce-window.16
  581.9 10.1 %multiply_convert_fusion.10 = bf16[12,64,512]{2,1,0:T(8,128)(2,1)} fusion(bf16[1024,12,64]{0,2,1:T(8,128)(2,1)} %bitcast.127, bf16[12,512,1024]{2,1,0:T(8,128)(2,1)} %get-tuple-element.103), kind=kOutput, calls=%fused_computation.118 | convolution fusion | flops 806092800 | bytes 14942208 | tf_op jit(solution)/shard_map/while/body/eval_jaxpr/hqk,khe->qhe/dot_general | solution.py:124
  592.0 6.2 multiply_convert_fusion.9
  598.3 2.8 maximum_dynamic-update-slice_fusion
  601.1 7.0 fusion.119
  608.1 2.3 multiply_convert_fusion.5
  612.4 10.4 %fusion.4 = f32[12,64,1024]{2,1,0:T(8,128)S(1)} fusion(bf16[512,12,64]{0,2,1:T(8,128)(2,1)S(1)} %bitcast.133, f32[12,512,1024]{2,1,0:T(8,128)} %get-tuple-element.131, f32[12,512]{1,0:T(8,128)S(1)} %log_add_fusion, pred[512,1024]{1,0:T(8,128)(4,1)S(1)} %copy-done.16), kind=kOutput, calls=%fused_computation.22 | convolution fusion | flops 824180736 | bytes 29646848 | tf_op jit(solution)/shard_map/while/body/eval_jaxpr/hqk,qhe->khe/dot_general | solution.py:132
  622.8 10.8 %add_convert_fusion = bf16[12,64,1024]{2,1,0:T(8,128)(2,1)S(1)} fusion(f32[12,64,1024]{2,1,0:T(8,128)S(1)} %fusion.4, bf16[512,12,64]{0,2,1:T(8,128)(2,1)S(1)} %bitcast.131, f32[12,512,1024]{2,1,0:T(8,128)} %get-tuple-element.133, f32[12,512]{1,0:T(8,128)S(1)} %log_add_fusion.1, pred[512,1024]{1,0:T(8,128)(4,1)S(1)} %copy-done.14), kind=kOutput, calls=%fused_computation.90 | convolution fusion | flops 825753600 | bytes 31219712 | tf_op jit(solution)/shard_map/while/body/eval_jaxpr/hqk,qhe->khe/dot_general | solution.py:132
  638.7 16.0 %convolution_convert_fusion.1 = bf16[1536,3200]{1,0:T(8,128)(2,1)} fusion(bf16[1024,3200]{0,1:T(8,128)(2,1)} %pad_dynamic-update-slice_fusion, bf16[512,1536]{1,0:T(8,128)(2,1)S(1)} %copy-done.30, bf16[512,1536]{1,0:T(8,128)(2,1)S(1)} %copy-done.28), kind=kOutput, calls=%fused_computation.21 | convolution fusion | flops 10077536256 | bytes 19529728 | tf_op jit(solution)/shard_map/dot_general | solution.py:35
  656.6 20.4 %convolution_convert_fusion = bf16[1536,4096]{1,0:T(8,128)(2,1)} fusion(bf16[1024,2048]{1,0:T(8,128)(2,1)} %get-tuple-element.107, bf16[1024,2048]{1,0:T(8,128)(2,1)} %get-tuple-element.108, bf16[512,1536]{1,0:T(8,128)(2,1)S(1)} %copy-done.38, bf16[512,1536]{1,0:T(8,128)(2,1)S(1)} %copy-done.36), kind=kOutput, calls=%fused_computation.20 | convolution fusion | flops 12914262016 | bytes 24117248 | tf_op jit(solution)/shard_map/dot_general | solution.py:35
  677.0 7.0 convolution_convert_fusion.4
  684.4 11.1 %fusion.55 = bf16[512,1536]{1,0:T(8,128)(2,1)} fusion(bf16[1536,3200]{1,0:T(8,128)(2,1)} %all-gather.5.cloned.1.call-done, bf16[1024,3200]{0,1:T(8,128)(2,1)} %pad_dynamic-update-slice_fusion, s32[]{:T(128)S(6)} %select_n.122), kind=kOutput, calls=%fused_computation.101 | convolution fusion | flops 5033951232 | bytes 14680068 | tf_op jit(solution)/shard_map/dot_general | solution.py:31
  695.5 2.4 collective-permute-start.7
  697.8 23.6 %collective-permute-done.3 = bf16[512,1536]{1,0:T(8,128)(2,1)S(1)} collective-permute-done((bf16[512,1536]{1,0:T(8,128)(2,1)S(1)}, bf16[512,1536]{1,0:T(8,128)(2,1)S(1)}, u32[]{:S(2)}, u32[]{:S(2)}) %collective-permute-start.3) | collective-permute-done | bytes 1572896 | tf_op jit(solution)/shard_map/ppermute | solution.py:39
  721.4 4.7 multiply_convert_fusion.7
  726.3 24.6 %collective-permute-done.7 = bf16[512,1536]{1,0:T(8,128)(2,1)S(1)} collective-permute-done((bf16[512,1536]{1,0:T(8,128)(2,1)}, bf16[512,1536]{1,0:T(8,128)(2,1)S(1)}, u32[]{:S(2)}, u32[]{:S(2)}) %collective-permute-start.7) | collective-permute-done | bytes 1572896 | tf_op jit(solution)/shard_map/ppermute | solution.py:39
  751.0 11.1 %fusion.45 = (f32[1536]{0:T(1024)S(1)}, f32[512]{0:T(512)S(1)}, f32[512,1536]{1,0:T(8,128)}) fusion(bf16[512,1536]{1,0:T(8,128)(2,1)S(1)} %copy-done.4, f32[512]{0:T(512)S(1)} %copy-done.51, bf16[512,1536]{1,0:T(8,128)(2,1)S(1)} %collective-permute-done.7, f32[1536]{0:T(1024)S(1)} %copy-done.48, bf16[1536,3200]{1,0:T(8,128)(2,1)} %all-gather.5.cloned.1.call-done, ...), kind=kOutput, calls=%fused_computation.71 | convolution fusion | flops 5040240640 | bytes 19415044 | tf_op jit(solution)/shard_map/dot_general | solution.py:31
  762.1 39.5 %all-reduce.2 = (f32[1536]{0:T(1024)}, f32[24]{0:T(128)}, f32[1536]{0:T(1024)}) all-reduce(f32[1536]{0:T(1024)S(1)} %get-tuple-element.96, f32[24]{0:T(128)S(1)} %dynamic_update_slice.19, f32[1536]{0:T(1024)S(1)} %copy-done.54), channel_id=1, replica_groups=mesh['dp'=16,'tensor'=2] {'dp','tensor'}, use_global_device_ids=true, to_apply=%region_19.20 | all-reduce | flops 3096 | bytes 24768 | tf_op jit(solution)/shard_map/psum | solution.py:276
  801.6 5.5 fusion.44
  808.8 1.9 convert_bitcast_fusion
  814.9 92.4 %reduce-scatter.9.cloned.1.call-done = bf16[96,4096]{1,0:T(8,128)(2,1)} async-done(((bf16[1536,4096]{1,0:T(8,128)(2,1)}), bf16[96,4096]{1,0:T(8,128)(2,1)}) %reduce-scatter.9.cloned.1.call-update) | async-done | bytes 786448 | tf_op jit(solution)/shard_map/reduce_scatter | solution.py:65
  907.3 3.3 reshape.299
  (213 shorter events, 42.3 us)
Async XLA Ops:
  7.2 3.9 copy-start.41
  7.2 5.1 copy-start.3
  7.2 89.8 %all-gather.5.cloned.1.call-start = ((), (), s32[]{:S(2)}) async-start(), calls=%async_computation.4 | async-start | bytes 10444800 | tf_op jit(solution)/shard_map/all_gather | solution.py:61
  9.3 3.3 copy-start.47
  10.2 192.8 %all-gather.7.cloned.1.call-start = ((), (), s32[]{:S(2)}) async-start(), calls=%async_computation.5 | async-start | bytes 2506752 | tf_op jit(solution)/shard_map/all_gather | solution.py:61
  11.0 303.5 %all-gather.9.cloned.1.call-start = ((), (), s32[]{:S(2)}) async-start(), calls=%async_computation.6 | async-start | bytes 13369344 | tf_op jit(solution)/shard_map/all_gather | solution.py:61
  12.2 4.7 copy-start.58
  12.2 323.9 %all-gather.11.cloned.1.call-start = ((), (), s32[]{:S(2)}) async-start(), calls=%async_computation.7 | async-start | bytes 6684672 | tf_op jit(solution)/shard_map/all_gather | solution.py:61
  12.7 41.5 %copy-start.50 = (f32[512]{0:T(512)}, f32[512]{0:T(512)S(1)}, u32[]{:S(2)}) copy-start(f32[512]{0:T(512)S(1)} %add_rsqrt_fusion.1) | copy-start | bytes 6148
  13.1 37.6 %collective-permute-start = (bf16[512,1536]{1,0:T(8,128)(2,1)S(1)}, bf16[512,1536]{1,0:T(8,128)(2,1)}, u32[]{:S(2)}, u32[]{:S(2)}) collective-permute-start(bf16[512,1536]{1,0:T(8,128)(2,1)S(1)} %fusion.40), channel_id=1, source_target_pairs={{0,1},{1,0},{2,3},{3,2},{4,5},{5,4},{6,7},{7,6},{8,9},{9,8},{10,11... | collective-permute-start | bytes 4718600 | tf_op jit(solution)/shard_map/ppermute | solution.py:39
  16.2 790.9 %reduce-scatter.7.cloned.1.call-start = ((), (), s32[]{:S(2)}) async-start(), calls=%async_computation.9 | async-start | bytes 2506752 | tf_op jit(solution)/shard_map/reduce_scatter | solution.py:65
  17.0 85.5 %copy-start.55 = (f32[12]{0:T(128)}, f32[12]{0:T(128)S(1)}, u32[]{:S(2)}) copy-start(f32[12]{0:T(128)S(1)} %dynamic_slice.57) | copy-start | bytes 148
  54.1 54.6 %copy-start.27 = (bf16[512,1536]{1,0:T(8,128)(2,1)}, bf16[512,1536]{1,0:T(8,128)(2,1)S(1)}, u32[]{:S(2)}) copy-start(bf16[512,1536]{1,0:T(8,128)(2,1)S(1)} %get-tuple-element.122) | copy-start | bytes 4718596
  97.0 11.8 %copy-start.29 = (bf16[512,1536]{1,0:T(8,128)(2,1)S(1)}, bf16[512,1536]{1,0:T(8,128)(2,1)}, u32[]{:S(2)}) copy-start(bf16[512,1536]{1,0:T(8,128)(2,1)} %get-tuple-element.123) | copy-start | bytes 4718596
  122.6 42.2 %copy-start.7 = (bf16[1024,768]{0,1:T(8,128)(2,1)}, bf16[1024,768]{0,1:T(8,128)(2,1)S(1)}, u32[]{:S(2)}) copy-start(bf16[1024,768]{0,1:T(8,128)(2,1)S(1)} %copy.42) | copy-start | bytes 4718596
  129.5 58.8 %copy-start.5 = (bf16[1024,768]{0,1:T(8,128)(2,1)}, bf16[1024,768]{0,1:T(8,128)(2,1)S(1)}, u32[]{:S(2)}) copy-start(bf16[1024,768]{0,1:T(8,128)(2,1)S(1)} %copy.40) | copy-start | bytes 4718596
  143.0 11.3 %copy-start.43 = (f32[12,512]{1,0:T(8,128)}, f32[12,512]{1,0:T(8,128)S(1)}, u32[]{:S(2)}) copy-start(f32[12,512]{1,0:T(8,128)S(1)} %get-tuple-element.130) | copy-start | bytes 73732
  154.3 10.5 %copy-start.45 = (f32[12,512]{1,0:T(8,128)}, f32[12,512]{1,0:T(8,128)S(1)}, u32[]{:S(2)}) copy-start(f32[12,512]{1,0:T(8,128)S(1)} %fusion.1) | copy-start | bytes 73732
  154.3 10.5 %copy-start.12 = (pred[512,1024]{1,0:T(8,128)(4,1)S(1)}, pred[512,1024]{1,0:T(8,128)(4,1)}, u32[]{:S(2)}) copy-start(pred[512,1024]{1,0:T(8,128)(4,1)} %get-tuple-element.128) | copy-start | bytes 1572868
  154.3 10.5 %copy-start.22 = (bf16[512,768]{0,1:T(8,128)(2,1)S(1)}, bf16[512,768]{0,1:T(8,128)(2,1)}, u32[]{:S(2)}) copy-start(bf16[512,768]{0,1:T(8,128)(2,1)} %copy.41) | copy-start | bytes 2359300
  203.0 5.0 copy-start.39
  203.0 6.7 copy-start.8
  207.9 37.6 %collective-permute-start.1 = (bf16[512,1536]{1,0:T(8,128)(2,1)}, bf16[512,1536]{1,0:T(8,128)(2,1)}, u32[]{:S(2)}, u32[]{:S(2)}) collective-permute-start(bf16[512,1536]{1,0:T(8,128)(2,1)} %convolution_convert_fusion.5), channel_id=1, source_target_pairs={{0,1},{1,0},{2,3},{3,2},{4,5},{5,4},{6,7},{7,6},{8,9},{9,8},{10,11... | collective-permute-start | bytes 4718600 | tf_op jit(solution)/shard_map/ppermute | solution.py:39
  209.7 205.8 %copy-start.52 = (f32[512]{0:T(512)}, f32[512]{0:T(512)S(1)}, u32[]{:S(2)}) copy-start(f32[512]{0:T(512)S(1)} %fusion.96) | copy-start | bytes 6148
  211.3 67.9 %collective-permute-start.4 = (bf16[512,1536]{1,0:T(8,128)(2,1)}, bf16[512,1536]{1,0:T(8,128)(2,1)}, u32[]{:S(2)}, u32[]{:S(2)}) collective-permute-start(bf16[512,1536]{1,0:T(8,128)(2,1)} %fusion.54), channel_id=1, source_target_pairs={{0,1},{1,0},{2,3},{3,2},{4,5},{5,4},{6,7},{7,6},{8,9},{9,8},{10,11... | collective-permute-start | bytes 4718600 | tf_op jit(solution)/shard_map/ppermute | solution.py:39
  211.5 38.5 %copy-start.49 = (f32[1536]{0:T(1024)S(1)}, f32[1536]{0:T(1024)}, u32[]{:S(2)}) copy-start(f32[1536]{0:T(1024)} %param.17) | copy-start | bytes 18436
  250.0 165.5 %copy-start.1 = (f32[512,1536]{1,0:T(8,128)}, f32[512,1536]{1,0:T(8,128)S(1)}, u32[]{:S(2)}) copy-start(f32[512,1536]{1,0:T(8,128)S(1)} %get-tuple-element.135) | copy-start | bytes 9437188
  250.0 29.2 %copy-start.9 = (bf16[512,1536]{1,0:T(8,128)(2,1)S(1)}, bf16[512,1536]{1,0:T(8,128)(2,1)}, u32[]{:S(2)}) copy-start(bf16[512,1536]{1,0:T(8,128)(2,1)} %param.21) | copy-start | bytes 4718596
  250.4 61.7 %collective-permute-start.2 = (bf16[512,1536]{1,0:T(8,128)(2,1)S(1)}, bf16[512,1536]{1,0:T(8,128)(2,1)S(1)}, u32[]{:S(2)}, u32[]{:S(2)}) collective-permute-start(bf16[512,1536]{1,0:T(8,128)(2,1)S(1)} %multiply_convert_fusion.8), channel_id=1, source_target_pairs={{0,1},{1,0},{2,3},{3,2},{4,5},{5,4},{6,7},{7,6},{8,9},{9,8},{10,11... | collective-permute-start | bytes 4718600 | tf_op jit(solution)/shard_map/ppermute | solution.py:39
  314.5 12.6 %copy-start.35 = (bf16[512,1536]{1,0:T(8,128)(2,1)S(1)}, bf16[512,1536]{1,0:T(8,128)(2,1)}, u32[]{:S(2)}) copy-start(bf16[512,1536]{1,0:T(8,128)(2,1)} %get-tuple-element.120) | copy-start | bytes 4718596
  314.5 12.6 %copy-start.37 = (bf16[512,1536]{1,0:T(8,128)(2,1)S(1)}, bf16[512,1536]{1,0:T(8,128)(2,1)}, u32[]{:S(2)}) copy-start(bf16[512,1536]{1,0:T(8,128)(2,1)} %get-tuple-element.121) | copy-start | bytes 4718596
  314.5 12.6 %copy-start.57 = (bf16[1536,4096]{1,0:T(8,128)(2,1)S(1)}, bf16[1536,4096]{1,0:T(8,128)(2,1)}, u32[]{:S(2)}) copy-start(bf16[1536,4096]{1,0:T(8,128)(2,1)} %all-gather.9.cloned.1.call-done) | copy-start | bytes 37748740
  364.7 35.8 %collective-permute-start.5 = (bf16[512,1536]{1,0:T(8,128)(2,1)S(1)}, bf16[512,1536]{1,0:T(8,128)(2,1)}, u32[]{:S(2)}, u32[]{:S(2)}) collective-permute-start(bf16[512,1536]{1,0:T(8,128)(2,1)S(1)} %fusion.58), channel_id=1, source_target_pairs={{0,1},{1,0},{2,3},{3,2},{4,5},{5,4},{6,7},{7,6},{8,9},{9,8},{10,11... | collective-permute-start | bytes 4718600 | tf_op jit(solution)/shard_map/ppermute | solution.py:39
  421.2 36.9 %copy-start.40 = (bf16[1024,768]{0,1:T(8,128)(2,1)S(1)}, bf16[1024,768]{0,1:T(8,128)(2,1)}, u32[]{:S(2)}) copy-start(bf16[1024,768]{0,1:T(8,128)(2,1)} %copy-done.39) | copy-start | bytes 4718596
  421.2 34.8 %collective-permute-start.6 = (bf16[512,1536]{1,0:T(8,128)(2,1)S(1)}, bf16[512,1536]{1,0:T(8,128)(2,1)S(1)}, u32[]{:S(2)}, u32[]{:S(2)}) collective-permute-start(bf16[512,1536]{1,0:T(8,128)(2,1)S(1)} %get-tuple-element.105), channel_id=1, source_target_pairs={{0,1},{1,0},{2,3},{3,2},{4,5},{5,4},{6,7},{7,6},{8,9},{9,8},{10,11... | collective-permute-start | bytes 4718600 | tf_op jit(solution)/shard_map/ppermute | solution.py:39
  458.1 4.0 copy-start.44
  458.1 4.0 copy-start.46
  458.1 4.1 copy-start.31
  458.1 4.1 copy-start.32
  462.0 346.7 %reduce-scatter.11.cloned.1.call-start = ((), (), s32[]{:S(2)}) async-start(), calls=%async_computation.11 | async-start | bytes 6684672 | tf_op jit(solution)/shard_map/reduce_scatter | solution.py:65
  473.0 337.7 %reduce-scatter.5.cloned.1.call-start = ((), (), s32[]{:S(2)}) async-start(), calls=%async_computation.8 | async-start | bytes 10444800 | tf_op jit(solution)/shard_map/reduce_scatter | solution.py:65
  484.4 22.5 %copy-start.17 = (bf16[512,768]{0,1:T(8,128)(2,1)}, bf16[512,768]{0,1:T(8,128)(2,1)S(1)}, u32[]{:S(2)}) copy-start(bf16[512,768]{0,1:T(8,128)(2,1)S(1)} %get-tuple-element.124) | copy-start | bytes 2359300
  506.9 23.7 %copy-start.15 = (pred[512,1024]{1,0:T(8,128)(4,1)S(1)}, pred[512,1024]{1,0:T(8,128)(4,1)}, u32[]{:S(2)}) copy-start(pred[512,1024]{1,0:T(8,128)(4,1)} %get-tuple-element.129) | copy-start | bytes 1572868
  506.9 23.7 %copy-start.19 = (bf16[512,768]{0,1:T(8,128)(2,1)S(1)}, bf16[512,768]{0,1:T(8,128)(2,1)}, u32[]{:S(2)}) copy-start(bf16[512,768]{0,1:T(8,128)(2,1)} %get-tuple-element.125) | copy-start | bytes 2359300
  552.6 24.0 %copy-start.42 = (f32[12,512]{1,0:T(8,128)S(1)}, f32[12,512]{1,0:T(8,128)}, u32[]{:S(2)}) copy-start(f32[12,512]{1,0:T(8,128)} %get-tuple-element.91) | copy-start | bytes 73732
  581.9 10.1 %copy-start = (bf16[12,512,1024]{2,1,0:T(8,128)(2,1)S(1)}, bf16[12,512,1024]{2,1,0:T(8,128)(2,1)}, u32[]{:S(2)}) copy-start(bf16[12,512,1024]{2,1,0:T(8,128)(2,1)} %get-tuple-element.104) | copy-start | bytes 37748740
  601.1 7.1 copy-start.21
  612.4 10.5 %copy-start.14 = (pred[512,1024]{1,0:T(8,128)(4,1)S(1)}, pred[512,1024]{1,0:T(8,128)(4,1)}, u32[]{:S(2)}) copy-start(pred[512,1024]{1,0:T(8,128)(4,1)} %get-tuple-element.128) | copy-start | bytes 1572868
  612.4 10.5 %copy-start.18 = (bf16[512,768]{0,1:T(8,128)(2,1)S(1)}, bf16[512,768]{0,1:T(8,128)(2,1)}, u32[]{:S(2)}) copy-start(bf16[512,768]{0,1:T(8,128)(2,1)} %copy-done.17) | copy-start | bytes 2359300
  633.6 3.2 copy-start.56
  633.6 5.0 copy-start.28
  633.6 5.0 copy-start.30
  654.7 252.6 %reduce-scatter.9.cloned.1.call-start = ((), (), s32[]{:S(2)}) async-start(), calls=%async_computation.10 | async-start | bytes 13369344 | tf_op jit(solution)/shard_map/reduce_scatter | solution.py:65
  677.0 44.4 %slice-start = ((s8[6291456]{0:T(1024)(128)(4,1)}), s8[4194304]{0:T(1024)(128)(4,1)S(1)}, s32[]{:S(2)}) async-start(s8[6291456]{0:T(1024)(128)(4,1)} %bitcast.159), calls=%async_computation.12 | async-start | bytes 8388608
  684.0 37.4 %copy-start.2 = (f32[512,1536]{1,0:T(8,128)S(1)}, f32[512,1536]{1,0:T(8,128)}, u32[]{:S(2)}) copy-start(f32[512,1536]{1,0:T(8,128)} %copy-done.1) | copy-start | bytes 9437188
  684.0 37.4 %copy-start.53 = (f32[512]{0:T(512)S(1)}, f32[512]{0:T(512)}, u32[]{:S(2)}) copy-start(f32[512]{0:T(512)} %copy-done.52) | copy-start | bytes 6148
  684.1 37.4 %slice-start.1 = ((s8[6291456]{0:T(1024)(128)(4,1)}), s8[2097152]{0:T(1024)(128)(4,1)S(1)}, s32[]{:S(2)}) async-start(s8[6291456]{0:T(1024)(128)(4,1)} %bitcast.159), calls=%async_computation.13 | async-start | bytes 4194304
  684.1 37.4 %copy-start.59 = (bf16[1024,2048]{1,0:T(8,128)(2,1)S(1)}, bf16[1024,2048]{1,0:T(8,128)(2,1)}, u32[]{:S(2)}) copy-start(bf16[1024,2048]{1,0:T(8,128)(2,1)} %get-tuple-element.109) | copy-start | bytes 12582916
  684.1 37.3 %collective-permute-start.3 = (bf16[512,1536]{1,0:T(8,128)(2,1)S(1)}, bf16[512,1536]{1,0:T(8,128)(2,1)S(1)}, u32[]{:S(2)}, u32[]{:S(2)}) collective-permute-start(bf16[512,1536]{1,0:T(8,128)(2,1)S(1)} %convolution_convert_fusion.4), channel_id=1, source_target_pairs={{0,1},{1,0},{2,3},{3,2},{4,5},{5,4},{6,7},{7,6},{8,9},{9,8},{10,11... | collective-permute-start | bytes 4718600 | tf_op jit(solution)/shard_map/ppermute | solution.py:39
  695.5 55.5 %copy-start.4 = (bf16[512,1536]{1,0:T(8,128)(2,1)S(1)}, bf16[512,1536]{1,0:T(8,128)(2,1)}, u32[]{:S(2)}) copy-start(bf16[512,1536]{1,0:T(8,128)(2,1)} %param.11) | copy-start | bytes 4718596
  695.5 55.5 %copy-start.48 = (f32[1536]{0:T(1024)S(1)}, f32[1536]{0:T(1024)}, u32[]{:S(2)}) copy-start(f32[1536]{0:T(1024)} %param.12) | copy-start | bytes 18436
  695.5 55.5 %copy-start.51 = (f32[512]{0:T(512)S(1)}, f32[512]{0:T(512)}, u32[]{:S(2)}) copy-start(f32[512]{0:T(512)} %copy-done.50) | copy-start | bytes 6148
  695.5 55.5 %collective-permute-start.7 = (bf16[512,1536]{1,0:T(8,128)(2,1)}, bf16[512,1536]{1,0:T(8,128)(2,1)S(1)}, u32[]{:S(2)}, u32[]{:S(2)}) collective-permute-start(bf16[512,1536]{1,0:T(8,128)(2,1)} %fusion.55), channel_id=1, source_target_pairs={{0,1},{1,0},{2,3},{3,2},{4,5},{5,4},{6,7},{7,6},{8,9},{9,8},{10,11... | collective-permute-start | bytes 4718600 | tf_op jit(solution)/shard_map/ppermute | solution.py:39
  726.3 35.8 %copy-start.54 = (f32[1536]{0:T(1024)S(1)}, f32[1536]{0:T(1024)}, u32[]{:S(2)}) copy-start(f32[1536]{0:T(1024)} %get-tuple-element.94) | copy-start | bytes 18436
  (14 other events, 26.3 us)
Sparse Core Ops, SparseCore 0:
  10.9 86.0 all-gather.4
  99.3 40.6 all-gather.6
  142.3 99.1 all-gather.8
  243.6 59.6 all-gather.10
  462.2 62.1 reduce-scatter.6
  528.2 84.1 reduce-scatter.10
  654.9 113.8 reduce-scatter.4
  772.8 134.5 reduce-scatter.8

commit v2 on v1

--- a/solution.py
+++ b/solution.py
@@ -1,12 +1,18 @@
+import functools
+
 import jax
 import jax.numpy as jnp
 from jax import lax
+from jax.experimental import pallas as pl
+from jax.experimental.pallas import tpu as pltpu
 from jax.sharding import PartitionSpec as P
 
 HEAD = 64
 SLOTS = 1024
 EPS = 1e-06
 PAD = 128
+BLOCK = 256
+NEG = -1e30
 
 BF16 = jnp.bfloat16
 F32 = jnp.float32
@@ -65,87 +71,296 @@
     return lax.psum_scatter(grad, "dp", scatter_dimension=0, tiled=True)
 
 
-def block_scores(queries, key_rows, decays, length, block_start, block_rows):
-    picked = lax.slice_in_dim(queries, block_start, block_start + block_rows, axis=0)
-    scores = jnp.einsum(
-        "qhe,khe->hqk", picked, key_rows, preferred_element_type=jnp.float32
-    ) * HEAD ** (-0.5)
-    scores = (
-        scores + decays[block_start : block_start + block_rows].T[:, :, None] - decays.T[:, None, :]
-    )
-    query_pos = block_start + jnp.arange(block_rows, dtype=jnp.int32)
-    key_pos = jnp.arange(SLOTS, dtype=jnp.int32)
-    allowed = (key_pos[None, :] <= query_pos[:, None]) & (key_pos[None, :] < length)
-    return (picked, jnp.where(allowed[None], scores, -1e30), allowed[None])
-
-
-def sequence_forward(packed):
-    queries, key_rows, value_rows, decays, length = packed
-    block_rows = min(512, SLOTS)
-    outputs = []
-    log_totals = []
-    for block_start in range(0, SLOTS, block_rows):
-        picked, scores, allowed = block_scores(
-            queries, key_rows, decays, length, block_start, block_rows
+def head_span(lane, head):
+    return (lane >= head * HEAD) & (lane < (head + 1) * HEAD)
+
+
+def key_side(keys, bias, lane, head, spare):
+    high = bias.astype(BF16).astype(F32)
+    rest = bias - high
+    mid = rest.astype(BF16).astype(F32)
+    extra = jnp.where(
+        lane == spare,
+        high,
+        jnp.where(lane == spare + 1, mid, jnp.where(lane == spare + 2, rest - mid, 0.0)),
+    )
+    return jnp.where(head_span(lane, head), keys, extra).astype(BF16)
+
+
+def query_side(queries, lane, head, spare):
+    ones = jnp.where((lane >= spare) & (lane < spare + 3), 1.0, 0.0)
+    return jnp.where(head_span(lane, head), queries * HEAD ** (-0.5), ones).astype(BF16)
+
+
+def pick_lane(rows, lane, index):
+    return jnp.sum(jnp.where(lane == index, rows, 0.0), axis=1, keepdims=True)
+
+
+def running_sum(rows, reverse):
+    step = 1
+    while step < SLOTS:
+        zeros = jnp.zeros((step, rows.shape[1]), F32)
+        if reverse:
+            moved = jnp.concatenate([rows[step:], zeros], axis=0)
+        else:
+            moved = jnp.concatenate([zeros, rows[:-step]], axis=0)
+        rows = rows + moved
+        step *= 2
+    return rows
+
+
+def causal(block):
+    key = lax.broadcasted_iota(jnp.int32, (block, block), 0)
+    query = lax.broadcasted_iota(jnp.int32, (block, block), 1)
+    return key <= query
+
+
+def attend_body(
+    lengths, q_ref, k_ref, v_ref, gate_ref, logit_ref, bias_ref, gated_ref, att_ref, shift_ref, keyb_ref,
+    *, per_group,
+):
+    seq = pl.program_id(0)
+    group = pl.program_id(1)
+    wide = per_group * HEAD
+
+    @pl.when(group == 0)
+    def _():
+        logit = logit_ref[...] + bias_ref[0:1]
+        forget = jnp.minimum(logit, 0.0) - jnp.log1p(jnp.exp(-jnp.abs(logit)))
+        slot = lax.broadcasted_iota(jnp.int32, (SLOTS, PAD), 0)
+        keyb_ref[...] = jnp.where(slot < lengths[seq], -running_sum(forget, False), NEG)
+
+    lane = lax.broadcasted_iota(jnp.int32, (SLOTS, wide), 1)
+    lane_all = lax.broadcasted_iota(jnp.int32, (SLOTS, PAD), 1)
+    queries = q_ref[...].astype(F32)
+    keys = k_ref[...].astype(F32)
+    values_t = jnp.transpose(v_ref[...].astype(F32)).astype(BF16)
+    allowed = causal(BLOCK)
+    sides = []
+    for head in range(per_group):
+        spare = HEAD if head == 0 else 0
+        bias = pick_lane(keyb_ref[...], lane_all, group * per_group + head)
+        sides.append(
+            (key_side(keys, bias, lane, head, spare), query_side(queries, lane, head, spare))
         )
-        row_max = jnp.max(scores, axis=-1, keepdims=True)
-        exponent = jnp.exp(scores - row_max)
-        totals = jnp.sum(exponent, axis=-1, keepdims=True)
-        soft_low = (exponent / totals).astype(jnp.bfloat16)
-        outputs.append(
-            jnp.einsum("hqk,khe->qhe", soft_low, value_rows, preferred_element_type=jnp.float32)
+    for start in range(0, SLOTS, BLOCK):
+        stop = start + BLOCK
+        outs = []
+        for head in range(per_group):
+            key_aug, query_aug = sides[head]
+            picked = query_aug[start:stop]
+            diag = jnp.where(allowed, dot_nt(key_aug[start:stop], picked), NEG)
+            top = jnp.max(diag, axis=0, keepdims=True)
+            if start:
+                early = dot_nt(key_aug[:start], picked)
+                top = jnp.maximum(top, jnp.max(early, axis=0, keepdims=True))
+            diag = jnp.exp(diag - top)
+            total = jnp.sum(diag, axis=0, keepdims=True)
+            value_rows = values_t[head * HEAD : (head + 1) * HEAD]
+            out = dot_nn(value_rows[:, start:stop], diag.astype(BF16))
+            if start:
+                early = jnp.exp(early - top)
+                total = total + jnp.sum(early, axis=0, keepdims=True)
+                out = out + dot_nn(value_rows[:, :start], early.astype(BF16))
+            outs.append(out / total)
+            shift_ref[pl.ds(group * per_group + head, 1), start:stop] = -(top + jnp.log(total))
+        block = jnp.transpose(jnp.concatenate(outs, axis=0))
+        att_ref[start:stop] = block.astype(BF16)
+        gated_ref[start:stop] = (block * jax.nn.sigmoid(gate_ref[start:stop])).astype(BF16)
+
+
+def attend_back_body(
+    q_ref, k_ref, v_ref, gate_ref, att_ref, grad_ref, logit_ref, bias_ref, shift_ref, keyb_ref,
+    out_ref, bias_out_ref, low_ref, dk_ref, dv_ref, row_ref, col_ref,
+    *, per_group, groups,
+):
+    group = pl.program_id(1)
+    wide = per_group * HEAD
+    part = groups * wide
+
+    def columns(which):
+        if groups == 1:
+            return slice(which * part, which * part + wide)
+        return pl.ds(pl.multiple_of(which * part + group * wide, wide), wide)
+
+    @pl.when(group == 0)
+    def _():
+        row_ref[...] = jnp.zeros(row_ref.shape, F32)
+        col_ref[...] = jnp.zeros(col_ref.shape, F32)
+
+    lane = lax.broadcasted_iota(jnp.int32, (SLOTS, wide), 1)
+    lane_all = lax.broadcasted_iota(jnp.int32, (SLOTS, PAD), 1)
+    sig = jax.nn.sigmoid(gate_ref[...])
+    grad_gated = grad_ref[...].astype(F32)
+    grad_att = grad_gated * sig
+    out_ref[:, columns(3)] = (grad_att * att_ref[...].astype(F32) * (1.0 - sig)).astype(BF16)
+    low_ref[...] = grad_att.astype(BF16)
+    queries = q_ref[...].astype(F32)
+    keys = k_ref[...].astype(F32)
+    keys_t = jnp.transpose(keys).astype(BF16)
+    ones = jnp.ones((16, SLOTS), BF16)
+    allowed = causal(BLOCK)
+    grad_low = low_ref[...].astype(F32)
+    sides = []
+    for head in range(per_group):
+        spare = HEAD if head == 0 else 0
+        bias = pick_lane(keyb_ref[...], lane_all, group * per_group + head)
+        sides.append(
+            (
+                key_side(keys, bias, lane, head, spare),
+                query_side(queries, lane, head, spare),
+                jnp.where(head_span(lane, head), grad_low, 0.0).astype(BF16),
+                jnp.concatenate([keys_t[head * HEAD : (head + 1) * HEAD], ones], axis=0),
+            )
         )
-        log_totals.append((row_max + jnp.log(totals))[:, :, 0])
-    return (jnp.concatenate(outputs, axis=0), jnp.concatenate(log_totals, axis=1))
-
-
-def sequence_backward(packed):
-    queries, key_rows, value_rows, decays, length, log_totals, grad_attended = packed
-    block_rows = min(512, SLOTS)
-    score_scale = HEAD ** (-0.5)
-    grad_keys = jnp.zeros(key_rows.shape, jnp.float32)
-    grad_values = jnp.zeros(value_rows.shape, jnp.float32)
-    column_terms = jnp.zeros((decays.shape[1], decays.shape[0]), jnp.float32)
-    query_grads = []
-    row_terms = []
-    for block_start in range(0, SLOTS, block_rows):
-        picked, scores, allowed = block_scores(
-            queries, key_rows, decays, length, block_start, block_rows
+    for start in reversed(range(0, SLOTS, BLOCK)):
+        stop = start + BLOCK
+        last = stop == SLOTS
+        outs = []
+        for head in range(per_group):
+            key_aug, query_aug, grad_own, key_rows = sides[head]
+            picked = query_aug[start:stop]
+            grads = grad_own[start:stop]
+            shift = shift_ref[pl.ds(group * per_group + head, 1), start:stop]
+            spans = [(start, stop)] + ([(0, start)] if start else [])
+            weights = []
+            inner = jnp.zeros((1, BLOCK), F32)
+            for low, high in spans:
+                score = dot_nt(key_aug[low:high], picked) + shift
+                if low == start:
+                    score = jnp.where(allowed, score, NEG)
+                soft = jnp.exp(score)
+                grad_soft = dot_nt(v_ref[low:high], grads)
+                inner = inner + jnp.sum(soft * grad_soft, axis=0, keepdims=True)
+                weights.append((soft, grad_soft))
+            out = jnp.zeros((HEAD + 16, BLOCK), F32)
+            for (low, high), (soft, grad_soft) in zip(spans, weights):
+                grad_score = (soft * (grad_soft - inner)).astype(BF16)
+                key_part = dot_nn(grad_score, picked)
+                value_part = dot_nn(soft.astype(BF16), grads)
+                if last:
+                    dk_ref[head, low:high] = key_part
+                    if head == 0:
+                        dv_ref[low:high] = value_part
+                    else:
+                        dv_ref[low:high] += value_part
+                else:
+                    dk_ref[head, low:high] += key_part
+                    dv_ref[low:high] += value_part
+                out = out + dot_nn(key_rows[:, low:high], grad_score)
+            outs.append(out[:HEAD] * HEAD ** (-0.5))
+            row_ref[pl.ds(group * per_group + head, 1), start:stop] = out[HEAD : HEAD + 1]
+        out_ref[start:stop, columns(0)] = jnp.transpose(jnp.concatenate(outs, axis=0)).astype(BF16)
+    grad_keys = dk_ref[0]
+    for head in range(per_group):
+        spare = HEAD if head == 0 else 0
+        found = dk_ref[head]
+        if head:
+            grad_keys = jnp.where(head_span(lane, head), found, grad_keys)
+        sums = pick_lane(found, lane, spare)
+        col_ref[...] = jnp.where(lane_all == group * per_group + head, sums, col_ref[...])
+    out_ref[:, columns(1)] = grad_keys.astype(BF16)
+    out_ref[:, columns(2)] = dv_ref[...].astype(BF16)
+
+    @pl.when(group == groups - 1)
+    def _():
+        grad_decay = jnp.transpose(row_ref[...]) - col_ref[...]
+        logit = logit_ref[...] + bias_ref[0:1]
+        grad_logit = running_sum(grad_decay, True) * jax.nn.sigmoid(-logit)
+        out_ref[:, 4 * part :] = grad_logit.astype(BF16)
+        bias_out_ref[...] = jnp.broadcast_to(jnp.sum(grad_logit, axis=0, keepdims=True), (8, PAD))
+
+
+def head_blocks(part):
+    heads = part // HEAD
+    per_group = 2 if heads % 2 == 0 else heads
+    groups = heads // per_group
+    wide = per_group * HEAD
+
+    def of(array, which, count):
+        if part % 128 == 0:
+            return array, pl.BlockSpec((SLOTS, wide), lambda s, g: (s, which * groups + g))
+        return (
+            array[:, which * part : (which + 1) * part],
+            pl.BlockSpec((SLOTS, wide), lambda s, g: (s, g)),
         )
-        shifted = scores - log_totals[:, block_start : block_start + block_rows, None]
-        soft = jnp.where(allowed, jnp.exp(shifted), 0.0)
-        grad_picked = lax.slice_in_dim(grad_attended, block_start, block_start + block_rows, axis=0)
-        grad_soft = jnp.einsum(
-            "qhe,khe->hqk", grad_picked, value_rows, preferred_element_type=jnp.float32
-        )
-        inner_sum = jnp.sum(soft * grad_soft, axis=-1, keepdims=True)
-        grad_scores = (soft * (grad_soft - inner_sum)).astype(jnp.bfloat16)
-        query_grads.append(
-            jnp.einsum("hqk,khe->qhe", grad_scores, key_rows, preferred_element_type=jnp.float32)
-            * score_scale
-        )
-        grad_keys = (
-            grad_keys
-            + jnp.einsum("hqk,qhe->khe", grad_scores, picked, preferred_element_type=jnp.float32)
-            * score_scale
-        )
-        grad_values = grad_values + jnp.einsum(
-            "hqk,qhe->khe",
-            soft.astype(jnp.bfloat16),
-            grad_picked,
-            preferred_element_type=jnp.float32,
-        )
-        wide_grads = grad_scores.astype(jnp.float32)
-        row_terms.append(jnp.sum(wide_grads, axis=2))
-        column_terms = column_terms - jnp.sum(wide_grads, axis=1)
-    grad_decay = jnp.concatenate(row_terms, axis=1) + column_terms
-    grad_forget = jnp.cumsum(grad_decay[:, ::-1], axis=1)[:, ::-1].T
-    return (
-        jnp.concatenate(query_grads, axis=0).astype(jnp.bfloat16),
-        grad_keys.astype(jnp.bfloat16),
-        grad_values.astype(jnp.bfloat16),
-        grad_forget,
-    )
+
+    return per_group, groups, wide, of
+
+
+def logit_block(gate_logit, part):
+    if part % PAD == 0:
+        return gate_logit, pl.BlockSpec((SLOTS, PAD), lambda s, g: (s, part // PAD))
+    return gate_logit[:, part:], pl.BlockSpec((SLOTS, PAD), lambda s, g: (s, 0))
+
+
+def attend(proj, gate_logit, bias_rows, lengths, part):
+    rows = proj.shape[0]
+    seqs = rows // SLOTS
+    per_group, groups, wide, of = head_blocks(part)
+    fix = lambda f: (lambda s, g, lengths: f(s, g))
+    parts = [of(proj, 0, 3), of(proj, 1, 3), of(proj, 2, 3), of(gate_logit, 0, 1)]
+    parts.append(logit_block(gate_logit, part))
+    parts.append((bias_rows, pl.BlockSpec((8, PAD), lambda s, g: (0, 0))))
+    wide_spec = pl.BlockSpec((SLOTS, wide), lambda s, g: (s, g))
+    outs = [
+        (jax.ShapeDtypeStruct((rows, part), BF16), wide_spec),
+        (jax.ShapeDtypeStruct((rows, part), BF16), wide_spec),
+        (jax.ShapeDtypeStruct((seqs * PAD, SLOTS), F32), pl.BlockSpec((PAD, SLOTS), lambda s, g: (s, 0))),
+        (jax.ShapeDtypeStruct((rows, PAD), F32), pl.BlockSpec((SLOTS, PAD), lambda s, g: (s, 0))),
+    ]
+    respec = lambda spec: pl.BlockSpec(spec.block_shape, fix(spec.index_map))
+    return pl.pallas_call(
+        functools.partial(attend_body, per_group=per_group),
+        out_shape=[shape for shape, _ in outs],
+        grid_spec=pltpu.PrefetchScalarGridSpec(
+            num_scalar_prefetch=1,
+            grid=(seqs, groups),
+            in_specs=[respec(spec) for _, spec in parts],
+            out_specs=[respec(spec) for _, spec in outs],
+        ),
+        compiler_params=pltpu.CompilerParams(
+            dimension_semantics=("arbitrary", "arbitrary"), vmem_limit_bytes=48 * 2**20
+        ),
+        name="attend",
+    )(lengths, *[array for array, _ in parts])
+
+
+def attend_back(proj, gate_logit, attended, grad_gated, bias_rows, shift, keyb, part):
+    rows = proj.shape[0]
+    seqs = rows // SLOTS
+    per_group, groups, wide, of = head_blocks(part)
+    parts = [of(proj, 0, 3), of(proj, 1, 3), of(proj, 2, 3), of(gate_logit, 0, 1)]
+    parts += [of(attended, 0, 1), of(grad_gated, 0, 1)]
+    parts.append(logit_block(gate_logit, part))
+    parts.append((bias_rows, pl.BlockSpec((8, PAD), lambda s, g: (0, 0))))
+    parts.append((shift, pl.BlockSpec((PAD, SLOTS), lambda s, g: (s, 0))))
+    parts.append((keyb, pl.BlockSpec((SLOTS, PAD), lambda s, g: (s, 0))))
+    total = 4 * part + PAD
+    return pl.pallas_call(
+        functools.partial(attend_back_body, per_group=per_group, groups=groups),
+        out_shape=[
+            jax.ShapeDtypeStruct((rows, total), BF16),
+            jax.ShapeDtypeStruct((seqs * 8, PAD), F32),
+        ],
+        grid=(seqs, groups),
+        in_specs=[spec for _, spec in parts],
+        out_specs=[
+            pl.BlockSpec((SLOTS, total), lambda s, g: (s, 0)),
+            pl.BlockSpec((8, PAD), lambda s, g: (s, 0)),
+        ],
+        scratch_shapes=[
+            pltpu.VMEM((SLOTS, wide), BF16),
+            pltpu.VMEM((per_group, SLOTS, wide), F32),
+            pltpu.VMEM((SLOTS, wide), F32),
+            pltpu.VMEM((PAD, SLOTS), F32),
+            pltpu.VMEM((SLOTS, PAD), F32),
+        ],
+        compiler_params=pltpu.CompilerParams(
+            dimension_semantics=("arbitrary", "arbitrary"), vmem_limit_bytes=56 * 2**20
+        ),
+        name="attend_back",
+    )(*[array for array, _ in parts])
 
 
 def on_device(
@@ -192,23 +407,8 @@
 
     proj = dot_nn(normed_all, attn_full[:, : 3 * part]).astype(BF16)
     gate_logit = dot_nn(normed_all, attn_full[:, 3 * part :])
-    out_gate = gate_logit[:, :part]
-    logits = gate_logit[:, part : part + heads_dev] + bias_own
-
-    def split_heads(column):
-        return proj[:, column * part : (column + 1) * part].reshape(
-            group_seqs, SLOTS, heads_dev, HEAD
-        )
-
-    queries, key_rows, value_rows = (split_heads(0), split_heads(1), split_heads(2))
-    log_forget = jax.nn.log_sigmoid(logits)
-    decays = jnp.cumsum(log_forget.reshape(group_seqs, SLOTS, heads_dev), axis=1)
-    attended, log_totals = lax.map(
-        sequence_forward, (queries, key_rows, value_rows, decays, lengths)
-    )
-    attended = attended.reshape(group_rows, part)
-    gate_sig = jax.nn.sigmoid(out_gate)
-    gated = (attended * gate_sig).astype(BF16)
+    bias_rows = jnp.broadcast_to(jnp.pad(bias_own, (0, PAD - heads_dev))[None, :], (8, PAD))
+    gated, attended, shift, keyb = attend(proj, gate_logit, bias_rows, lengths, part)
 
     def attn_term(first_row, row_count):
         return dot_nt(lax.dynamic_slice_in_dim(gated, first_row, row_count), out_full)
@@ -242,26 +442,12 @@
 
     layer_output = (valid * (middle + sum_rows(mlp_term, own_rows))).astype(BF16)
 
-    grad_gated = dot_nn(grad_branch_all, out_full)
+    grad_gated = dot_nn(grad_branch_all, out_full).astype(BF16)
     out_part = scatter_dp(dot_tn(grad_branch_all, gated).astype(BF16))
-    grad_attended = (grad_gated * gate_sig).astype(BF16)
-    grad_out_gate = (grad_gated * attended * gate_sig * (1.0 - gate_sig)).astype(BF16)
-    grad_heads = grad_attended.reshape(group_seqs, SLOTS, heads_dev, HEAD)
-    grad_queries, grad_keys, grad_values, grad_forget = lax.map(
-        sequence_backward, (queries, key_rows, value_rows, decays, lengths, log_totals, grad_heads)
-    )
-    grad_logit = grad_forget.reshape(group_rows, heads_dev) * jax.nn.sigmoid(-logits)
-    bias_part = jnp.sum(grad_logit, axis=0)
-    grad_proj = jnp.concatenate(
-        [
-            grad_queries.reshape(group_rows, part),
-            grad_keys.reshape(group_rows, part),
-            grad_values.reshape(group_rows, part),
-            grad_out_gate,
-            jnp.pad(grad_logit.astype(BF16), ((0, 0), (0, PAD - heads_dev))),
-        ],
-        axis=1,
-    )
+    grad_proj, bias_sums = attend_back(
+        proj, gate_logit, attended, grad_gated, bias_rows, shift, keyb, part
+    )
+    bias_part = jnp.sum(bias_sums.reshape(group_seqs, 8, PAD)[:, 0, :heads_dev], axis=0)
     attn_part = scatter_dp(dot_tn(normed_all, grad_proj).astype(BF16))
 
     def attn_back_term(first_row, row_count):

time: 924 us -> 855 us (0.925)
  matrix products: 321 us -> 182 us
  waiting for transfers between devices: 374 us -> 486 us
  other arithmetic: 113 us -> 30.2 us
  Pallas kernels: 0 us -> 63 us
  local copies, waits for them, and re-layouts: 40.8 us -> 20.2 us
    dot_general x12 -> x0, matrix products: 137 us -> none  [the longest x2 43.6 us: sequence_backward(): jnp.einsum('qhe,khe->hqk', grad_picked, value_rows, preferred_element_typ...]
    reduce_scatter x4, waiting for transfers between devices: 92.4 us -> 171 us  [scatter_dp(): return lax.psum_scatter(grad, 'dp', scatter_dimension=0, tiled=True)]
    reduce_sum x5 -> x0, other arithmetic: 71.7 us -> none  [the longest x2 47.8 us: sequence_backward(): column_terms = column_terms - jnp.sum(wide_grads, axis=1)]
    pallas_call x0 -> x2, Pallas kernels: none -> 63 us  [the longest x1 38.1 us: attend_back(): pl.pallas_call(functools.partial(attend_back_body, per_group=per_group, g...]
    all_gather x4, waiting for transfers between devices: 42.9 us -> 72.8 us  [gather_dp(): return lax.all_gather(shard, 'dp', axis=0, tiled=True)]
    slice x8 -> x0, local copies, waits for them, and re-layouts: 11.2 us -> none  [the longest x3 6.41 us: block_scores(): lax.slice_in_dim(queries, block_start, block_start + block_rows, axis=0)]
    unnamed x136 -> x76, local copies, waits for them, and re-layouts: 19.7 us -> 12.5 us
  transfers between devices with their start and end apart: 16 -> 16, of which waited for: 10 -> 12; matrix products, arithmetic and copies ran while one was open for 44% -> 19% of each run, Pallas kernels for 0% -> 7%
where the time goes in v2:
time: 855 us; the launch traced here: 851 us
  waiting for transfers between devices  486 us (57%)
  matrix products  182 us (21%)
  Pallas kernels  63 us (7%)
  blocking collectives  42.8 us (5%)
  other arithmetic  30.2 us (4%)
  local copies, waits for them, and re-layouts  20.2 us (2%)
  between operations  15.4 us (2%)
  starting transfers between devices  11.5 us (1%)
    ppermute x8, waiting for transfers between devices, swap(): return lax.ppermute(rows, 'tensor', [(0, 1), (1, 0)])  241 us
    reduce_scatter x4, waiting for transfers between devices, scatter_dp(): return lax.psum_scatter(grad, 'dp', scatter_dimension=0, tiled=True)  171 us
    all_gather x4, waiting for transfers between devices, gather_dp(): return lax.all_gather(shard, 'dp', axis=0, tiled=True)  72.8 us
    dot_general x8, matrix products, dot_nt(): lax.dot_general(a, b, (((1,), (1,)), ((), ())), preferred_element_type=F32)  68.4 us
    dot_general x6, matrix products, dot_nn(): lax.dot_general(a, b, (((1,), (0,)), ((), ())), preferred_element_type=F32)  62.4 us
    dot_general x4, matrix products, dot_tn(): lax.dot_general(a, b, (((0,), (0,)), ((), ())), preferred_element_type=F32)  51.2 us
    psum x1, blocking collectives, on_device(): lax.psum((gain_attn_part, gain_mlp_part, bias_full), ('dp', 'tensor'))  42.8 us
    pallas_call x1, Pallas kernels, attend_back(): pl.pallas_call(functools.partial(attend_back_body, per_group=per_group, g...  38.1 us
  transfers between devices with their start and end apart: 16, of which 12 were waited for; matrix products, arithmetic and copies ran while one was open for 19% of the time, Pallas kernels for 7%

profile of v2, /device:TPU:0, one launch (start us, length us, event | category | flops | bytes accessed | tf_op | source)
XLA Modules:
  0.0 851.2 jit_solution(4302154311936959995)
XLA Ops:
  7.2 1.3 copy.24
  8.5 0.8 copy.23
  9.4 0.9 fusion.54
  10.3 0.7 all-gather.7.cloned.1.call-update
  11.1 1.1 copy.25
  13.1 3.1 collective-permute-start
  17.0 33.7 %collective-permute-done = bf16[512,1536]{1,0:T(8,128)(2,1)} collective-permute-done((bf16[512,1536]{1,0:T(8,128)(2,1)S(1)}, bf16[512,1536]{1,0:T(8,128)(2,1)}, u32[]{:S(2)}, u32[]{:S(2)}) %collective-permute-start) | collective-permute-done | bytes 1572896 | tf_op jit(solution)/shard_map/ppermute | solution.py:45
  50.7 3.5 broadcast_select_fusion.7
  54.2 42.8 %all-gather.5.cloned.1.call-done = bf16[1536,3200]{1,0:T(8,128)(2,1)} async-done(((bf16[96,3200]{1,0:T(8,128)(2,1)}), bf16[1536,3200]{1,0:T(8,128)(2,1)}) %all-gather.5.cloned.1.call-update) | async-done | bytes 9830416 | tf_op jit(solution)/shard_map/all_gather | solution.py:67
  97.0 7.6 fusion.38.gate_ref.logit_ref
  104.6 9.3 %fusion.7.q_ref.k_ref.v_ref = bf16[1024,2304]{1,0:T(8,128)(2,1)} fusion(bf16[1536,3200]{1,0:T(8,128)(2,1)S(1)} %copy-done.29, bf16[512,1536]{1,0:T(8,128)(2,1)S(1)} %copy-done.11, bf16[512,1536]{1,0:T(8,128)(2,1)S(1)} %get-tuple-element.50), kind=kOutput, calls=%fused_computation.19 | convolution fusion | flops 7256408064 | bytes 14942208 | tf_op jit(solution)/shard_map/dot_general | solution.py:33
  113.9 24.8 %attend.1 = (bf16[1024,768]{1,0:T(8,128)(2,1)S(1)}, bf16[1024,768]{1,0:T(8,128)(2,1)S(1)}, f32[128,1024]{1,0:T(8,128)S(1)}, f32[1024,128]{1,0:T(8,128)S(1)}) custom-call(s32[1]{0:T(128)} %copy.27.lengths, bf16[1024,2304]{1,0:T(8,128)(2,1)} %fusion.7.q_ref.k_ref.v_ref, bf16[1024,2304]{1,0:T(8,128)(2,1)} %fusion.7.q_ref.k_ref.v_ref, ...), custom_call_target="tpu_custom_call" | custom-call | tf_op jit(solution)/shard_map/attend/pallas_call | solution.py:313
  138.7 1.2 copy-done
  139.9 0.8 copy-done.1
  140.7 0.8 copy-done.2
  141.5 4.2 convolution_convert_fusion.5
  145.8 1.5 collective-permute-start.1
  147.2 2.9 fusion.31
  150.7 32.7 %collective-permute-done.1 = bf16[512,1536]{1,0:T(8,128)(2,1)} collective-permute-done((bf16[512,1536]{1,0:T(8,128)(2,1)}, bf16[512,1536]{1,0:T(8,128)(2,1)}, u32[]{:S(2)}, u32[]{:S(2)}) %collective-permute-start.1) | collective-permute-done | bytes 1572896 | tf_op jit(solution)/shard_map/ppermute | solution.py:45
  183.3 5.0 multiply_reduce_fusion.2
  188.7 1.4 collective-permute-start.2
  190.1 26.9 %collective-permute-done.4 = bf16[512,1536]{1,0:T(8,128)(2,1)} collective-permute-done((bf16[512,1536]{1,0:T(8,128)(2,1)}, bf16[512,1536]{1,0:T(8,128)(2,1)}, u32[]{:S(2)}, u32[]{:S(2)}) %collective-permute-start.4) | collective-permute-done | bytes 1572896 | tf_op jit(solution)/shard_map/ppermute | solution.py:45
  217.0 3.8 broadcast_select_fusion.3
  220.9 29.1 %collective-permute-done.2 = bf16[512,1536]{1,0:T(8,128)(2,1)S(1)} collective-permute-done((bf16[512,1536]{1,0:T(8,128)(2,1)S(1)}, bf16[512,1536]{1,0:T(8,128)(2,1)S(1)}, u32[]{:S(2)}, u32[]{:S(2)}) %collective-permute-start.2) | collective-permute-done | bytes 1572896 | tf_op jit(solution)/shard_map/ppermute | solution.py:45
  249.9 2.4 broadcast_select_fusion.5
  252.3 12.6 %fusion.3 = f32[1024,2048]{1,0:T(8,128)} fusion(bf16[1536,4096]{1,0:T(8,128)(2,1)} %all-gather.9.cloned.1.call-done, bf16[512,1536]{1,0:T(8,128)(2,1)} %get-tuple-element.49, bf16[512,1536]{1,0:T(8,128)(2,1)} %get-tuple-element.48), kind=kOutput, calls=%fused_computation.15 | convolution fusion | flops 6448742400 | bytes 17825792 | tf_op jit(solution)/shard_map/dot_general | solution.py:33
  264.9 8.9 %fusion.5 = f32[1024,2048]{1,0:T(8,128)} fusion(bf16[1536,4096]{1,0:T(8,128)(2,1)S(1)} %copy-done.28, bf16[512,1536]{1,0:T(8,128)(2,1)S(1)} %copy-done.20, bf16[512,1536]{1,0:T(8,128)(2,1)S(1)} %copy-done.18), kind=kOutput, calls=%fused_computation.17 | convolution fusion | flops 6448742400 | bytes 17825792 | tf_op jit(solution)/shard_map/dot_general | solution.py:33
  273.9 30.0 %all-gather.11.cloned.1.call-done = bf16[1536,2048]{1,0:T(8,128)(2,1)} async-done(((bf16[96,2048]{1,0:T(8,128)(2,1)}), bf16[1536,2048]{1,0:T(8,128)(2,1)}) %all-gather.11.cloned.1.call-update) | async-done | bytes 6291472 | tf_op jit(solution)/shard_map/all_gather | solution.py:67
  303.8 17.5 %multiply_convert_fusion = (bf16[1024,2048]{1,0:T(8,128)(2,1)}, bf16[1024,2048]{1,0:T(8,128)(2,1)}, bf16[1024,2048]{1,0:T(8,128)(2,1)}) fusion(f32[1024,2048]{1,0:T(8,128)} %fusion.5, f32[1024,2048]{1,0:T(8,128)} %fusion.3, bf16[1536,2048]{1,0:T(8,128)(2,1)} %all-gather.11.cloned.1.call-done, bf16[512,1536]{1,0:T(8,128)(2,1)} %get-tuple-element.47, ...), kind=kOutput, calls=%fused_computation.7 | convolution fusion | flops 6480199680 | bytes 38797312 | tf_op jit(solution)/shard_map/dot_general | solution.py:33
  321.3 11.0 %fusion.35 = bf16[512,1536]{1,0:T(8,128)(2,1)S(1)} fusion(bf16[1536,4096]{1,0:T(8,128)(2,1)} %all-gather.9.cloned.1.call-done, s32[]{:T(128)S(6)} %select_n.93, bf16[1024,2048]{1,0:T(8,128)(2,1)} %get-tuple-element.42, bf16[1024,2048]{1,0:T(8,128)(2,1)} %get-tuple-element.41), kind=kOutput, calls=%fused_computation.60 | convolution fusion | flops 6451625984 | bytes 22544388 | tf_op jit(solution)/shard_map/dot_general | solution.py:37
  332.3 1.5 collective-permute-start.5
  333.8 35.2 %collective-permute-done.5 = bf16[512,1536]{1,0:T(8,128)(2,1)} collective-permute-done((bf16[512,1536]{1,0:T(8,128)(2,1)S(1)}, bf16[512,1536]{1,0:T(8,128)(2,1)}, u32[]{:S(2)}, u32[]{:S(2)}) %collective-permute-start.5) | collective-permute-done | bytes 1572896 | tf_op jit(solution)/shard_map/ppermute | solution.py:45
  369.0 15.1 %multiply_reduce_fusion = (f32[1536]{0:T(1024)S(1)}, f32[512]{0:T(512)S(1)}, f32[512,1536]{1,0:T(8,128)}) fusion(f32[512,1536]{1,0:T(8,128)} %copy-done.4, f32[512]{0:T(512)S(1)} %add_rsqrt_fusion, bf16[512,1536]{1,0:T(8,128)(2,1)} %collective-permute-done.5, f32[1536]{0:T(1024)S(1)} %copy-done.25, bf16[1536,4096]{1,0:T(8,128)(2,1)} %all-gather.9.cloned.1.call-done, ...), kind=kOutput, calls=%fused_computation.47 | convolution fusion | flops 6457128960 | bytes 28852228 | tf_op jit(solution)/shard_map/dot_general | solution.py:37
  384.2 6.1 fusion.80
  390.2 1.5 collective-permute-start.6
  391.7 34.2 %collective-permute-done.6 = bf16[512,1536]{1,0:T(8,128)(2,1)S(1)} collective-permute-done((bf16[512,1536]{1,0:T(8,128)(2,1)S(1)}, bf16[512,1536]{1,0:T(8,128)(2,1)S(1)}, u32[]{:S(2)}, u32[]{:S(2)}) %collective-permute-start.6) | collective-permute-done | bytes 1572896 | tf_op jit(solution)/shard_map/ppermute | solution.py:45
  426.3 1.2 copy-done.14
  428.0 4.0 convolution_convert_fusion.3
  432.1 11.1 %convolution_convert_fusion.2 = bf16[1536,2048]{1,0:T(8,128)(2,1)} fusion(bf16[1024,2048]{1,0:T(8,128)(2,1)} %get-tuple-element.43, bf16[512,1536]{1,0:T(8,128)(2,1)} %get-tuple-element.47, bf16[512,1536]{1,0:T(8,128)(2,1)S(1)} %copy-done.13), kind=kOutput, calls=%fused_computation.12 | convolution fusion | flops 6451888128 | bytes 13631488 | tf_op jit(solution)/shard_map/dot_general | solution.py:41
  443.3 1.4 copy-done.15
  445.2 6.5 fusion.47.grad_ref
  451.7 38.1 %attend_back.1 = (bf16[1024,3200]{1,0:T(8,128)(2,1)}, f32[8,128]{1,0:T(8,128)}) custom-call(bf16[1024,2304]{1,0:T(8,128)(2,1)} %fusion.7.q_ref.k_ref.v_ref, bf16[1024,2304]{1,0:T(8,128)(2,1)} %fusion.7.q_ref.k_ref.v_ref, bf16[1024,2304]{1,0:T(8,128)(2,1)} %fusion.7.q_ref.k_ref.v_ref, f32[1024,896]{1,0:T(8,128)} %fusion.38.gate_ref.logit_ref, ...), custom_call_target="tpu_custom_call" | custom-call | tf_op jit(solution)/shard_map/attend_back/pallas_call | solution.py:340
  489.8 15.9 %convolution_convert_fusion.1 = bf16[1536,3200]{1,0:T(8,128)(2,1)} fusion(bf16[1024,3200]{1,0:T(8,128)(2,1)} %get-tuple-element.20, bf16[512,1536]{1,0:T(8,128)(2,1)S(1)} %copy-done.12, bf16[512,1536]{1,0:T(8,128)(2,1)S(1)} %copy-done.10), kind=kOutput, calls=%fused_computation.1 | convolution fusion | flops 10077536256 | bytes 19529728 | tf_op jit(solution)/shard_map/dot_general | solution.py:41
  505.8 1.4 copy-done.19
  507.9 20.2 %convolution_convert_fusion = bf16[1536,4096]{1,0:T(8,128)(2,1)} fusion(bf16[1024,2048]{1,0:T(8,128)(2,1)} %get-tuple-element.41, bf16[1024,2048]{1,0:T(8,128)(2,1)} %get-tuple-element.42, bf16[512,1536]{1,0:T(8,128)(2,1)S(1)} %copy-done.21, bf16[512,1536]{1,0:T(8,128)(2,1)S(1)} %copy-done.19), kind=kOutput, calls=%fused_computation | convolution fusion | flops 12914262016 | bytes 24117248 | tf_op jit(solution)/shard_map/dot_general | solution.py:41
  528.2 7.0 convolution_convert_fusion.4
  535.2 1.4 collective-permute-start.3
  536.6 8.8 %fusion.32 = bf16[512,1536]{1,0:T(8,128)(2,1)S(1)} fusion(bf16[1536,3200]{1,0:T(8,128)(2,1)} %all-gather.5.cloned.1.call-done, bf16[1024,3200]{1,0:T(8,128)(2,1)S(1)} %bitcast.37, s32[]{:T(128)S(6)} %select_n.93), kind=kOutput, calls=%fused_computation.57 | convolution fusion | flops 5033951232 | bytes 14680068 | tf_op jit(solution)/shard_map/dot_general | solution.py:37
  545.8 26.8 %collective-permute-done.3 = bf16[512,1536]{1,0:T(8,128)(2,1)S(1)} collective-permute-done((bf16[512,1536]{1,0:T(8,128)(2,1)S(1)}, bf16[512,1536]{1,0:T(8,128)(2,1)S(1)}, u32[]{:S(2)}, u32[]{:S(2)}) %collective-permute-start.3) | collective-permute-done | bytes 1572896 | tf_op jit(solution)/shard_map/ppermute | solution.py:45
  572.6 8.2 multiply_convert_fusion.3
  580.8 0.8 bitcast_dynamic-update-slice_fusion
  581.6 22.8 %collective-permute-done.7 = bf16[512,1536]{1,0:T(8,128)(2,1)S(1)} collective-permute-done((bf16[512,1536]{1,0:T(8,128)(2,1)S(1)}, bf16[512,1536]{1,0:T(8,128)(2,1)S(1)}, u32[]{:S(2)}, u32[]{:S(2)}) %collective-permute-start.7) | collective-permute-done | bytes 1572896 | tf_op jit(solution)/shard_map/ppermute | solution.py:45
  604.5 9.1 %fusion.29 = (f32[1536]{0:T(1024)S(1)}, f32[512]{0:T(512)S(1)}, f32[512,1536]{1,0:T(8,128)}) fusion(bf16[512,1536]{1,0:T(8,128)(2,1)S(1)} %copy-done.7, f32[512]{0:T(512)S(1)} %copy-done.27, bf16[512,1536]{1,0:T(8,128)(2,1)S(1)} %collective-permute-done.7, f32[1536]{0:T(1024)S(1)} %copy-done.24, bf16[1536,3200]{1,0:T(8,128)(2,1)S(1)} %bitcast.35, ...), kind=kOutput, calls=%fused_computation.41 | convolution fusion | flops 5040240640 | bytes 19415044 | tf_op jit(solution)/shard_map/dot_general | solution.py:37
  613.5 42.8 %all-reduce.2 = (f32[1536]{0:T(1024)}, f32[24]{0:T(128)}, f32[1536]{0:T(1024)}) all-reduce(f32[1536]{0:T(1024)S(1)} %get-tuple-element.34, f32[24]{0:T(128)S(1)} %bitcast_dynamic-update-slice_fusion, f32[1536]{0:T(1024)S(1)} %get-tuple-element.32), channel_id=1, replica_groups=mesh['dp'=16,'tensor'=2] {'dp','tensor'}, use_global_device_ids=true, to_apply=%region_5.6 | all-reduce | flops 3096 | bytes 24768 | tf_op jit(solution)/shard_map/psum | solution.py:462
  656.3 5.5 fusion.28
  661.9 1.6 convert_bitcast_fusion.1
  663.5 1.9 convert_bitcast_fusion
  665.5 36.7 %reduce-scatter.5.cloned.1.call-done = bf16[96,3200]{1,0:T(8,128)(2,1)} async-done(((bf16[1536,3200]{1,0:T(8,128)(2,1)}), bf16[96,3200]{1,0:T(8,128)(2,1)}) %reduce-scatter.5.cloned.1.call-update) | async-done | bytes 614416 | tf_op jit(solution)/shard_map/reduce_scatter | solution.py:71
  702.1 1.2 slice.32
  703.3 1.6 reshape.110
  704.9 0.7 slice.33
  705.6 0.7 copy.22
  706.3 134.4 %reduce-scatter.9.cloned.1.call-done = bf16[96,4096]{1,0:T(8,128)(2,1)} async-done(((bf16[1536,4096]{1,0:T(8,128)(2,1)}), bf16[96,4096]{1,0:T(8,128)(2,1)}) %reduce-scatter.9.cloned.1.call-update) | async-done | bytes 786448 | tf_op jit(solution)/shard_map/reduce_scatter | solution.py:71
  840.8 3.3 reshape.115
  (102 shorter events, 4.7 us)
Async XLA Ops:
  7.2 3.9 copy-start.22
  7.2 5.1 copy-start.6
  7.2 89.8 %all-gather.5.cloned.1.call-start = ((), (), s32[]{:S(2)}) async-start(), calls=%async_computation.4 | async-start | bytes 10444800 | tf_op jit(solution)/shard_map/all_gather | solution.py:67
  8.5 4.1 copy-start.23
  10.3 131.3 %all-gather.7.cloned.1.call-start = ((), (), s32[]{:S(2)}) async-start(), calls=%async_computation.5 | async-start | bytes 2506752 | tf_op jit(solution)/shard_map/all_gather | solution.py:67
  11.0 241.3 %all-gather.9.cloned.1.call-start = ((), (), s32[]{:S(2)}) async-start(), calls=%async_computation.6 | async-start | bytes 13369344 | tf_op jit(solution)/shard_map/all_gather | solution.py:67
  12.2 4.7 copy-start.30
  12.2 291.6 %all-gather.11.cloned.1.call-start = ((), (), s32[]{:S(2)}) async-start(), calls=%async_computation.7 | async-start | bytes 6684672 | tf_op jit(solution)/shard_map/all_gather | solution.py:67
  12.7 41.5 %copy-start.26 = (f32[512]{0:T(512)}, f32[512]{0:T(512)S(1)}, u32[]{:S(2)}) copy-start(f32[512]{0:T(512)S(1)} %add_rsqrt_fusion.1) | copy-start | bytes 6148
  13.1 37.6 %collective-permute-start = (bf16[512,1536]{1,0:T(8,128)(2,1)S(1)}, bf16[512,1536]{1,0:T(8,128)(2,1)}, u32[]{:S(2)}, u32[]{:S(2)}) collective-permute-start(bf16[512,1536]{1,0:T(8,128)(2,1)S(1)} %fusion.24), channel_id=1, source_target_pairs={{0,1},{1,0},{2,3},{3,2},{4,5},{5,4},{6,7},{7,6},{8,9},{9,8},{10,11... | collective-permute-start | bytes 4718600 | tf_op jit(solution)/shard_map/ppermute | solution.py:45
  16.2 645.7 %reduce-scatter.7.cloned.1.call-start = ((), (), s32[]{:S(2)}) async-start(), calls=%async_computation.9 | async-start | bytes 2506752 | tf_op jit(solution)/shard_map/reduce_scatter | solution.py:71
  54.1 50.4 %copy-start.9 = (bf16[512,1536]{1,0:T(8,128)(2,1)}, bf16[512,1536]{1,0:T(8,128)(2,1)S(1)}, u32[]{:S(2)}) copy-start(bf16[512,1536]{1,0:T(8,128)(2,1)S(1)} %get-tuple-element.50) | copy-start | bytes 4718596
  97.0 7.6 copy-start.11
  97.0 7.6 copy-start.29
  113.9 24.8 %copy-start.3 = (f32[8,128]{1,0:T(8,128)}, f32[8,128]{1,0:T(8,128)S(1)}, u32[]{:S(2)}) copy-start(f32[8,128]{1,0:T(8,128)S(1)} %broadcast_in_dim.16.bias_ref) | copy-start | bytes 12292
  138.7 1.2 copy-start
  139.9 0.8 copy-start.1
  140.7 0.8 copy-start.2
  145.8 37.6 %collective-permute-start.1 = (bf16[512,1536]{1,0:T(8,128)(2,1)}, bf16[512,1536]{1,0:T(8,128)(2,1)}, u32[]{:S(2)}, u32[]{:S(2)}) collective-permute-start(bf16[512,1536]{1,0:T(8,128)(2,1)} %convolution_convert_fusion.5), channel_id=1, source_target_pairs={{0,1},{1,0},{2,3},{3,2},{4,5},{5,4},{6,7},{7,6},{8,9},{9,8},{10,11... | collective-permute-start | bytes 4718600 | tf_op jit(solution)/shard_map/ppermute | solution.py:45
  150.1 66.9 %collective-permute-start.4 = (bf16[512,1536]{1,0:T(8,128)(2,1)}, bf16[512,1536]{1,0:T(8,128)(2,1)}, u32[]{:S(2)}, u32[]{:S(2)}) collective-permute-start(bf16[512,1536]{1,0:T(8,128)(2,1)} %fusion.31), channel_id=1, source_target_pairs={{0,1},{1,0},{2,3},{3,2},{4,5},{5,4},{6,7},{7,6},{8,9},{9,8},{10,11... | collective-permute-start | bytes 4718600 | tf_op jit(solution)/shard_map/ppermute | solution.py:45
  150.7 37.7 %copy-start.25 = (f32[1536]{0:T(1024)S(1)}, f32[1536]{0:T(1024)}, u32[]{:S(2)}) copy-start(f32[1536]{0:T(1024)} %param.17) | copy-start | bytes 18436
  188.3 61.6 %copy-start.4 = (f32[512,1536]{1,0:T(8,128)}, f32[512,1536]{1,0:T(8,128)S(1)}, u32[]{:S(2)}) copy-start(f32[512,1536]{1,0:T(8,128)S(1)} %get-tuple-element.53) | copy-start | bytes 9437188
  188.3 28.7 %copy-start.8 = (bf16[512,1536]{1,0:T(8,128)(2,1)S(1)}, bf16[512,1536]{1,0:T(8,128)(2,1)}, u32[]{:S(2)}) copy-start(bf16[512,1536]{1,0:T(8,128)(2,1)} %param.21) | copy-start | bytes 4718596
  188.7 61.2 %collective-permute-start.2 = (bf16[512,1536]{1,0:T(8,128)(2,1)S(1)}, bf16[512,1536]{1,0:T(8,128)(2,1)S(1)}, u32[]{:S(2)}, u32[]{:S(2)}) collective-permute-start(bf16[512,1536]{1,0:T(8,128)(2,1)S(1)} %multiply_convert_fusion.4), channel_id=1, source_target_pairs={{0,1},{1,0},{2,3},{3,2},{4,5},{5,4},{6,7},{7,6},{8,9},{9,8},{10,11... | collective-permute-start | bytes 4718600 | tf_op jit(solution)/shard_map/ppermute | solution.py:45
  252.3 12.6 %copy-start.18 = (bf16[512,1536]{1,0:T(8,128)(2,1)S(1)}, bf16[512,1536]{1,0:T(8,128)(2,1)}, u32[]{:S(2)}) copy-start(bf16[512,1536]{1,0:T(8,128)(2,1)} %get-tuple-element.48) | copy-start | bytes 4718596
  252.3 12.6 %copy-start.20 = (bf16[512,1536]{1,0:T(8,128)(2,1)S(1)}, bf16[512,1536]{1,0:T(8,128)(2,1)}, u32[]{:S(2)}) copy-start(bf16[512,1536]{1,0:T(8,128)(2,1)} %get-tuple-element.49) | copy-start | bytes 4718596
  252.3 12.6 %copy-start.28 = (bf16[1536,4096]{1,0:T(8,128)(2,1)S(1)}, bf16[1536,4096]{1,0:T(8,128)(2,1)}, u32[]{:S(2)}) copy-start(bf16[1536,4096]{1,0:T(8,128)(2,1)} %all-gather.9.cloned.1.call-done) | copy-start | bytes 37748740
  332.3 36.7 %collective-permute-start.5 = (bf16[512,1536]{1,0:T(8,128)(2,1)S(1)}, bf16[512,1536]{1,0:T(8,128)(2,1)}, u32[]{:S(2)}, u32[]{:S(2)}) collective-permute-start(bf16[512,1536]{1,0:T(8,128)(2,1)S(1)} %fusion.35), channel_id=1, source_target_pairs={{0,1},{1,0},{2,3},{3,2},{4,5},{5,4},{6,7},{7,6},{8,9},{9,8},{10,11... | collective-permute-start | bytes 4718600 | tf_op jit(solution)/shard_map/ppermute | solution.py:45
  390.2 35.7 %collective-permute-start.6 = (bf16[512,1536]{1,0:T(8,128)(2,1)S(1)}, bf16[512,1536]{1,0:T(8,128)(2,1)S(1)}, u32[]{:S(2)}, u32[]{:S(2)}) collective-permute-start(bf16[512,1536]{1,0:T(8,128)(2,1)S(1)} %get-tuple-element.39), channel_id=1, source_target_pairs={{0,1},{1,0},{2,3},{3,2},{4,5},{5,4},{6,7},{7,6},{8,9},{9,8},{10,11... | collective-permute-start | bytes 4718600 | tf_op jit(solution)/shard_map/ppermute | solution.py:45
  426.3 1.2 copy-start.14
  426.3 1.7 copy-start.16
  428.0 4.0 copy-start.13
  432.0 231.5 %reduce-scatter.11.cloned.1.call-start = ((), (), s32[]{:S(2)}) async-start(), calls=%async_computation.11 | async-start | bytes 6684672 | tf_op jit(solution)/shard_map/reduce_scatter | solution.py:71
  443.2 1.5 copy-start.15
  443.2 2.0 copy-start.17
  443.2 258.9 %reduce-scatter.5.cloned.1.call-start = ((), (), s32[]{:S(2)}) async-start(), calls=%async_computation.8 | async-start | bytes 10444800 | tf_op jit(solution)/shard_map/reduce_scatter | solution.py:71
  451.7 38.1 %copy-start.10 = (bf16[512,1536]{1,0:T(8,128)(2,1)S(1)}, bf16[512,1536]{1,0:T(8,128)(2,1)}, u32[]{:S(2)}) copy-start(bf16[512,1536]{1,0:T(8,128)(2,1)} %copy-done.9) | copy-start | bytes 4718596
  451.7 38.1 %copy-start.12 = (bf16[512,1536]{1,0:T(8,128)(2,1)S(1)}, bf16[512,1536]{1,0:T(8,128)(2,1)}, u32[]{:S(2)}) copy-start(bf16[512,1536]{1,0:T(8,128)(2,1)} %get-tuple-element.51) | copy-start | bytes 4718596
  505.8 1.5 copy-start.19
  505.8 2.1 copy-start.21
  505.8 335.0 %reduce-scatter.9.cloned.1.call-start = ((), (), s32[]{:S(2)}) async-start(), calls=%async_computation.10 | async-start | bytes 13369344 | tf_op jit(solution)/shard_map/reduce_scatter | solution.py:71
  528.1 8.5 slice-start.3
  528.1 8.5 slice-start.4
  528.2 76.3 %slice-start = ((s8[9830400]{0:T(1024)(128)(4,1)}), s8[4194304]{0:T(1024)(128)(4,1)S(1)}, s32[]{:S(2)}) async-start(s8[9830400]{0:T(1024)(128)(4,1)} %bitcast.34), calls=%async_computation.12 | async-start | bytes 8388608
  535.2 37.4 %copy-start.5 = (f32[512,1536]{1,0:T(8,128)S(1)}, f32[512,1536]{1,0:T(8,128)}, u32[]{:S(2)}) copy-start(f32[512,1536]{1,0:T(8,128)} %copy-done.4) | copy-start | bytes 9437188
  535.2 69.2 %slice-start.1 = ((s8[9830400]{0:T(1024)(128)(4,1)}), s8[4194304]{0:T(1024)(128)(4,1)S(1)}, s32[]{:S(2)}) async-start(s8[9830400]{0:T(1024)(128)(4,1)} %bitcast.34), calls=%async_computation.13 | async-start | bytes 8388608
  535.2 69.2 %slice-start.2 = ((s8[9830400]{0:T(1024)(128)(4,1)}), s8[1441792]{0:T(1024)(128)(4,1)S(1)}, s32[]{:S(2)}) async-start(s8[9830400]{0:T(1024)(128)(4,1)} %bitcast.34), calls=%async_computation.14 | async-start | bytes 2883584
  535.2 37.3 %collective-permute-start.3 = (bf16[512,1536]{1,0:T(8,128)(2,1)S(1)}, bf16[512,1536]{1,0:T(8,128)(2,1)S(1)}, u32[]{:S(2)}, u32[]{:S(2)}) collective-permute-start(bf16[512,1536]{1,0:T(8,128)(2,1)S(1)} %convolution_convert_fusion.4), channel_id=1, source_target_pairs={{0,1},{1,0},{2,3},{3,2},{4,5},{5,4},{6,7},{7,6},{8,9},{9,8},{10,11... | collective-permute-start | bytes 4718600 | tf_op jit(solution)/shard_map/ppermute | solution.py:45
  545.4 59.0 %copy-start.7 = (bf16[512,1536]{1,0:T(8,128)(2,1)S(1)}, bf16[512,1536]{1,0:T(8,128)(2,1)}, u32[]{:S(2)}) copy-start(bf16[512,1536]{1,0:T(8,128)(2,1)} %param.11) | copy-start | bytes 4718596
  545.5 59.0 %copy-start.24 = (f32[1536]{0:T(1024)S(1)}, f32[1536]{0:T(1024)}, u32[]{:S(2)}) copy-start(f32[1536]{0:T(1024)} %param.12) | copy-start | bytes 18436
  545.5 59.0 %copy-start.27 = (f32[512]{0:T(512)S(1)}, f32[512]{0:T(512)}, u32[]{:S(2)}) copy-start(f32[512]{0:T(512)} %copy-done.26) | copy-start | bytes 6148
  545.5 58.9 %collective-permute-start.7 = (bf16[512,1536]{1,0:T(8,128)(2,1)S(1)}, bf16[512,1536]{1,0:T(8,128)(2,1)S(1)}, u32[]{:S(2)}, u32[]{:S(2)}) collective-permute-start(bf16[512,1536]{1,0:T(8,128)(2,1)S(1)} %fusion.32), channel_id=1, source_target_pairs={{0,1},{1,0},{2,3},{3,2},{4,5},{5,4},{6,7},{7,6},{8,9},{9,8},{10,11... | collective-permute-start | bytes 4718600 | tf_op jit(solution)/shard_map/ppermute | solution.py:45
Sparse Core Ops, SparseCore 0:
  10.9 86.0 all-gather.4
  99.3 40.6 all-gather.6
  142.9 99.1 all-gather.8
  244.2 59.6 all-gather.10
  432.2 61.8 reduce-scatter.6
  497.9 84.0 reduce-scatter.10
  586.2 115.9 reduce-scatter.4
  706.2 134.5 reduce-scatter.8

commit v3 on v2

--- a/solution.py
+++ b/solution.py
@@ -53,14 +53,25 @@
     return jnp.concatenate([jnp.where(first, own, other), jnp.where(first, other, own)], axis=0)
 
 
-def sum_rows(term_fn, own_rows):
+def hold(*values):
+    return lax.optimization_barrier(values)
+
+
+def term_parts(term_fn, own_rows):
     size = lax.axis_size("tensor")
     if size != 2:
-        term = term_fn(jnp.int32(0), own_rows * size).astype(BF16)
-        return lax.psum_scatter(term, "tensor", scatter_dimension=0, tiled=True).astype(F32)
+        return (term_fn(jnp.int32(0), own_rows * size).astype(BF16), jnp.zeros((), F32))
     index = lax.axis_index("tensor")
-    sent = swap(term_fn((1 - index) * own_rows, own_rows).astype(BF16))
-    return term_fn(index * own_rows, own_rows) + sent.astype(F32)
+    return (
+        term_fn((1 - index) * own_rows, own_rows).astype(BF16),
+        term_fn(index * own_rows, own_rows),
+    )
+
+
+def cross(leaving):
+    if lax.axis_size("tensor") != 2:
+        return lax.psum_scatter(leaving, "tensor", scatter_dimension=0, tiled=True)
+    return swap(leaving)
 
 
 def gather_dp(shard):
@@ -394,16 +405,19 @@
     attn_shard = jnp.concatenate(
         [w_attn.reshape(own_d, 4 * part), jnp.pad(w_forget, ((0, 0), (0, PAD - heads_dev)))], axis=1
     )
-    attn_full = gather_dp(attn_shard)
-    out_full = gather_dp(w_out.T)
-    down_full = gather_dp(w_down.T)
-    mlp_full = gather_dp(w_mlp.reshape(own_d, 2 * units))
+    attn_cols = 4 * part + PAD
+    first_full = gather_dp(jnp.concatenate([attn_shard, w_out.T], axis=1))
+    second_shard = jnp.concatenate([w_down.T, w_mlp.reshape(own_d, 2 * units)], axis=1)
+    first_full, second_shard = hold(first_full, second_shard)
+    second_full = gather_dp(second_shard)
+    attn_full, out_full = (first_full[:, :attn_cols], first_full[:, attn_cols:])
+    down_full, mlp_full = (second_full[:, :units], second_full[:, units:])
 
     input_wide = layer_input.astype(F32)
     scaled_attn, inverse_attn = norm_parts(input_wide)
     normed_all = share_rows((scaled_attn * gain_attn).astype(BF16))
     grad_final = cotangent.astype(F32) * valid
-    grad_final_all = share_rows(grad_final.astype(BF16))
+    normed_all, grad_final_all = hold(normed_all, share_rows(grad_final.astype(BF16)))
 
     proj = dot_nn(normed_all, attn_full[:, : 3 * part]).astype(BF16)
     gate_logit = dot_nn(normed_all, attn_full[:, 3 * part :])
@@ -413,7 +427,9 @@
     def attn_term(first_row, row_count):
         return dot_nt(lax.dynamic_slice_in_dim(gated, first_row, row_count), out_full)
 
-    middle = input_wide + sum_rows(attn_term, own_rows)
+    leaving, staying = term_parts(attn_term, own_rows)
+    arrived, staying = hold(cross(leaving), staying)
+    middle = input_wide + (staying + arrived.astype(F32))
     scaled_mlp, inverse_mlp = norm_parts(middle)
     normed_mid = share_rows((scaled_mlp * gain_mlp).astype(BF16))
     grad_hidden = dot_nn(grad_final_all, down_full)
@@ -429,31 +445,42 @@
     def mlp_back_term(first_row, row_count):
         return dot_nt(lax.dynamic_slice_in_dim(grad_pair, first_row, row_count), mlp_full)
 
-    grad_normed_mlp = sum_rows(mlp_back_term, own_rows)
-    down_part = scatter_dp(dot_tn(grad_final_all, hidden).astype(BF16))
-    mlp_part = scatter_dp(dot_tn(normed_mid, grad_pair).astype(BF16))
+    down_grad = dot_tn(grad_final_all, hidden).astype(BF16)
+    down_part = scatter_dp(down_grad)
+    leaving, staying = term_parts(mlp_back_term, own_rows)
+    mlp_grad = dot_tn(normed_mid, grad_pair).astype(BF16)
+    arrived, staying, mlp_grad = hold(cross(leaving), staying, mlp_grad)
+    mlp_part = scatter_dp(mlp_grad)
+    grad_normed_mlp = staying + arrived.astype(F32)
 
     gain_mlp_part = jnp.sum(scaled_mlp * grad_normed_mlp, axis=0)
     grad_middle = grad_final + norm_back(grad_normed_mlp, scaled_mlp, inverse_mlp, gain_mlp)
-    grad_branch_all = share_rows(grad_middle.astype(BF16))
+    grad_middle_low, hidden = hold(grad_middle.astype(BF16), hidden)
 
     def mlp_term(first_row, row_count):
         return dot_nt(lax.dynamic_slice_in_dim(hidden, first_row, row_count), down_full)
 
-    layer_output = (valid * (middle + sum_rows(mlp_term, own_rows))).astype(BF16)
+    leaving, staying = term_parts(mlp_term, own_rows)
+    grad_branch_all, leaving, staying = hold(share_rows(grad_middle_low), leaving, staying)
+    arrived_out = cross(leaving)
 
     grad_gated = dot_nn(grad_branch_all, out_full).astype(BF16)
-    out_part = scatter_dp(dot_tn(grad_branch_all, gated).astype(BF16))
     grad_proj, bias_sums = attend_back(
         proj, gate_logit, attended, grad_gated, bias_rows, shift, keyb, part
     )
+    grad_proj, arrived_out = hold(grad_proj, arrived_out)
+    layer_output = (valid * (middle + (staying + arrived_out.astype(F32)))).astype(BF16)
     bias_part = jnp.sum(bias_sums.reshape(group_seqs, 8, PAD)[:, 0, :heads_dev], axis=0)
-    attn_part = scatter_dp(dot_tn(normed_all, grad_proj).astype(BF16))
-
     def attn_back_term(first_row, row_count):
         return dot_nt(lax.dynamic_slice_in_dim(grad_proj, first_row, row_count), attn_full)
 
-    grad_normed_attn = sum_rows(attn_back_term, own_rows)
+    first_grad = jnp.concatenate(
+        [dot_tn(normed_all, grad_proj), dot_tn(grad_branch_all, gated)], axis=1
+    ).astype(BF16)
+    first_part = scatter_dp(first_grad)
+    leaving, staying = term_parts(attn_back_term, own_rows)
+    grad_normed_attn = staying + cross(leaving).astype(F32)
+    attn_part, out_part = (first_part[:, :attn_cols], first_part[:, attn_cols:])
     gain_attn_part = jnp.sum(scaled_attn * grad_normed_attn, axis=0)
     grad_input = grad_middle + norm_back(grad_normed_attn, scaled_attn, inverse_attn, gain_attn)
     bias_full = lax.dynamic_update_slice_in_dim(

time: 855 us -> 735 us (0.86)
  waiting for transfers between devices: 486 us -> 368 us
  other arithmetic: 30.2 us -> 45 us
  local copies, waits for them, and re-layouts: 20.2 us -> 11.3 us
    reduce_scatter x4 -> x3, waiting for transfers between devices: 171 us -> 97.5 us  [scatter_dp(): return lax.psum_scatter(grad, 'dp', scatter_dimension=0, tiled=True)]
    ppermute x8, waiting for transfers between devices: 241 us -> 171 us  [swap(): return lax.ppermute(rows, 'tensor', [(0, 1), (1, 0)])]
    all_gather x4 -> x2, waiting for transfers between devices: 72.8 us -> 99.4 us  [gather_dp(): return lax.all_gather(shard, 'dp', axis=0, tiled=True)]
    concatenate x1 -> x5, other arithmetic: 0.87 us -> 10.3 us  [the longest x1 5.13 us: on_device(): jnp.concatenate([dot_tn(normed_all, grad_proj), dot_tn(grad_branch_all, g...]
  transfers between devices with their start and end apart: 16 -> 13, of which waited for: 12 -> 8; matrix products, arithmetic and copies ran while one was open for 19% -> 24% of each run, Pallas kernels for 7% -> 9%
where the time goes in v3:
time: 735 us; the launch traced here: 731 us
  waiting for transfers between devices  368 us (50%)
  matrix products  179 us (24%)
  Pallas kernels  63.5 us (9%)
  other arithmetic  45 us (6%)
  blocking collectives  39.5 us (5%)
  between operations  15.2 us (2%)
  local copies, waits for them, and re-layouts  11.3 us (2%)
  starting transfers between devices  9.43 us (1%)
    ppermute x8, waiting for transfers between devices, swap(): return lax.ppermute(rows, 'tensor', [(0, 1), (1, 0)])  171 us
    all_gather x2, waiting for transfers between devices, gather_dp(): return lax.all_gather(shard, 'dp', axis=0, tiled=True)  99.4 us
    reduce_scatter x3, waiting for transfers between devices, scatter_dp(): return lax.psum_scatter(grad, 'dp', scatter_dimension=0, tiled=True)  97.5 us
    dot_general x8, matrix products, dot_nt(): lax.dot_general(a, b, (((1,), (1,)), ((), ())), preferred_element_type=F32)  68.9 us
    dot_general x6, matrix products, dot_nn(): lax.dot_general(a, b, (((1,), (0,)), ((), ())), preferred_element_type=F32)  60.3 us
    dot_general x4, matrix products, dot_tn(): lax.dot_general(a, b, (((0,), (0,)), ((), ())), preferred_element_type=F32)  49.5 us
    psum x1, blocking collectives, on_device(): lax.psum((gain_attn_part, gain_mlp_part, bias_full), ('dp', 'tensor'))  39.5 us
    pallas_call x1, Pallas kernels, attend_back(): pl.pallas_call(functools.partial(attend_back_body, per_group=per_group, g...  38.7 us
  transfers between devices with their start and end apart: 13, of which 8 were waited for; matrix products, arithmetic and copies ran while one was open for 24% of the time, Pallas kernels for 9%

profile of v3, /device:TPU:0, one launch (start us, length us, event | category | flops | bytes accessed | tf_op | source)
XLA Modules:
  0.0 730.7 jit_solution(5567908466064278698)
XLA Ops:
  7.2 1.2 copy.26
  8.5 0.8 copy.25
  9.3 1.8 fusion.75
  11.5 1.1 pad_maximum_fusion.7
  12.6 99.4 %all-gather.3.cloned.1.call-done = bf16[1536,3968]{1,0:T(8,128)(2,1)} async-done(((bf16[96,3968]{1,0:T(8,128)(2,1)}), bf16[1536,3968]{1,0:T(8,128)(2,1)}) %all-gather.3.cloned.1.call-update) | async-done | bytes 12189712 | tf_op jit(solution)/shard_map/all_gather | solution.py:78
  112.8 1.5 fusion.44
  114.3 1.5 collective-permute-start.1
  115.7 0.4 fusion.43
  116.1 1.6 fusion.37
  117.7 0.6 collective-permute-start
  118.3 33.5 %collective-permute-done.1 = bf16[512,1536]{1,0:T(8,128)(2,1)} collective-permute-done((bf16[512,1536]{1,0:T(8,128)(2,1)}, bf16[512,1536]{1,0:T(8,128)(2,1)}, u32[]{:S(2)}, u32[]{:S(2)}) %collective-permute-start.1) | collective-permute-done | bytes 1572896 | tf_op jit(solution)/shard_map/ppermute | solution.py:45
  151.8 2.2 broadcast_select_fusion.5
  154.1 30.7 %collective-permute-done = bf16[512,1536]{1,0:T(8,128)(2,1)} collective-permute-done((bf16[512,1536]{1,0:T(8,128)(2,1)}, bf16[512,1536]{1,0:T(8,128)(2,1)}, u32[]{:S(2)}, u32[]{:S(2)}) %collective-permute-start) | collective-permute-done | bytes 1572896 | tf_op jit(solution)/shard_map/ppermute | solution.py:45
  184.8 2.3 broadcast_select_fusion.7
  187.2 2.1 pad_maximum_fusion.3
  189.3 1.7 slice-done.2
  191.0 5.3 fusion.58.gate_ref.logit_ref
  196.3 9.1 %fusion.15.q_ref.k_ref.v_ref = bf16[1024,2304]{1,0:T(8,128)(2,1)} fusion(bf16[1024,1536]{1,0:T(8,128)(2,1)S(1)} %get-tuple-element.32, bf16[1536,3968]{1,0:T(8,128)(2,1)S(1)} %bitcast.32), kind=kOutput, calls=%fused_computation.28 | convolution fusion | flops 7250116608 | bytes 14942208 | tf_op jit(solution)/shard_map/dot_general | solution.py:33
  205.4 24.8 %attend.1 = (bf16[1024,768]{1,0:T(8,128)(2,1)S(1)}, bf16[1024,768]{1,0:T(8,128)(2,1)S(1)}, f32[128,1024]{1,0:T(8,128)S(1)}, f32[1024,128]{1,0:T(8,128)S(1)}) custom-call(s32[1]{0:T(128)} %copy.29.lengths, bf16[1024,2304]{1,0:T(8,128)(2,1)} %fusion.15.q_ref.k_ref.v_ref, bf16[1024,2304]{1,0:T(8,128)(2,1)} %fusion.15.q_ref.k_ref.v_ref, ...), custom_call_target="tpu_custom_call" | custom-call | tf_op jit(solution)/shard_map/attend/pallas_call | solution.py:324
  230.3 4.6 convolution_convert_fusion.4
  234.9 1.5 collective-permute-start.2
  236.5 3.2 fusion.64
  239.7 31.1 %collective-permute-done.2 = bf16[512,1536]{1,0:T(8,128)(2,1)} collective-permute-done((bf16[512,1536]{1,0:T(8,128)(2,1)S(1)}, bf16[512,1536]{1,0:T(8,128)(2,1)}, u32[]{:S(2)}, u32[]{:S(2)}) %collective-permute-start.2) | collective-permute-done | bytes 1572896 | tf_op jit(solution)/shard_map/ppermute | solution.py:45
  270.8 2.1 multiply_reduce_fusion.2
  273.2 1.5 collective-permute-start.3
  274.8 33.4 %collective-permute-done.3 = bf16[512,1536]{1,0:T(8,128)(2,1)S(1)} collective-permute-done((bf16[512,1536]{1,0:T(8,128)(2,1)S(1)}, bf16[512,1536]{1,0:T(8,128)(2,1)S(1)}, u32[]{:S(2)}, u32[]{:S(2)}) %collective-permute-start.3) | collective-permute-done | bytes 1572896 | tf_op jit(solution)/shard_map/ppermute | solution.py:45
  308.1 2.4 broadcast_select_fusion.3
  310.5 12.0 %fusion.22 = f32[1024,2048]{1,0:T(8,128)} fusion(bf16[1024,1536]{1,0:T(8,128)(2,1)} %get-tuple-element.37, bf16[1536,6144]{1,0:T(8,128)(2,1)} %all-gather.5.cloned.1.call-done), kind=kOutput, calls=%fused_computation.33 | convolution fusion | flops 6442450944 | bytes 17825792 | tf_op jit(solution)/shard_map/dot_general | solution.py:33
  322.5 10.7 %fusion.11 = f32[1024,2048]{1,0:T(8,128)} fusion(bf16[1536,6144]{1,0:T(8,128)(2,1)} %all-gather.5.cloned.1.call-done, bf16[512,1536]{1,0:T(8,128)(2,1)S(1)} %copy-done.17, bf16[512,1536]{1,0:T(8,128)(2,1)S(1)} %copy-done.16), kind=kOutput, calls=%fused_computation.24 | convolution fusion | flops 6448742400 | bytes 17825792 | tf_op jit(solution)/shard_map/dot_general | solution.py:33
  333.3 17.3 %multiply_convert_fusion = (bf16[1024,2048]{1,0:T(8,128)(2,1)}, bf16[1024,2048]{1,0:T(8,128)(2,1)}, bf16[1024,2048]{1,0:T(8,128)(2,1)}) fusion(f32[1024,2048]{1,0:T(8,128)} %fusion.11, f32[1024,2048]{1,0:T(8,128)} %fusion.22, bf16[1536,6144]{1,0:T(8,128)(2,1)} %all-gather.5.cloned.1.call-done, bf16[512,1536]{1,0:T(8,128)(2,1)} %get-tuple-element.81, ...), kind=kOutput, calls=%fused_computation.16 | convolution fusion | flops 6480199680 | bytes 38797312 | tf_op jit(solution)/shard_map/dot_general | solution.py:33
  350.6 11.2 %convolution_convert_fusion.2 = bf16[1536,2048]{1,0:T(8,128)(2,1)} fusion(bf16[1024,1536]{1,0:T(8,128)(2,1)} %get-tuple-element.37, bf16[1024,2048]{1,0:T(8,128)(2,1)} %get-tuple-element.42), kind=kOutput, calls=%fused_computation.21 | convolution fusion | flops 6445596672 | bytes 13631488 | tf_op jit(solution)/shard_map/dot_general | solution.py:41
  361.9 12.6 %fusion.53 = bf16[512,1536]{1,0:T(8,128)(2,1)} fusion(bf16[1536,6144]{1,0:T(8,128)(2,1)} %all-gather.5.cloned.1.call-done, s32[]{:T(128)S(6)} %select_n.94, bf16[1024,2048]{1,0:T(8,128)(2,1)} %get-tuple-element.76, bf16[1024,2048]{1,0:T(8,128)(2,1)} %get-tuple-element.77), kind=kOutput, calls=%fused_computation.71 | convolution fusion | flops 6451625984 | bytes 22544388 | tf_op jit(solution)/shard_map/dot_general | solution.py:37
  374.5 1.4 collective-permute-start.4
  375.9 20.9 %convolution_convert_fusion.1 = bf16[1536,4096]{1,0:T(8,128)(2,1)} fusion(bf16[1024,2048]{1,0:T(8,128)(2,1)} %get-tuple-element.77, bf16[1024,2048]{1,0:T(8,128)(2,1)} %get-tuple-element.76, bf16[512,1536]{1,0:T(8,128)(2,1)} %get-tuple-element.81, bf16[512,1536]{1,0:T(8,128)(2,1)} %get-tuple-element.80), kind=kOutput, calls=%fused_computation.1 | convolution fusion | flops 12914262016 | bytes 24117248 | tf_op jit(solution)/shard_map/dot_general | solution.py:41
  396.8 12.3 %fusion = f32[512,1536]{1,0:T(8,128)} fusion(bf16[1536,6144]{1,0:T(8,128)(2,1)} %all-gather.5.cloned.1.call-done, s32[]{:T(128)S(6)} %select_n.95, bf16[1024,2048]{1,0:T(8,128)(2,1)} %get-tuple-element.76, bf16[1024,2048]{1,0:T(8,128)(2,1)} %get-tuple-element.77), kind=kOutput, calls=%fused_computation.3 | convolution fusion | flops 6450839552 | bytes 24117252 | tf_op jit(solution)/shard_map/dot_general | solution.py:37
  409.2 3.5 multiply_reduce_fusion
  412.7 0.6 copy-done.12
  413.3 4.5 fusion.94
  417.8 0.8 collective-permute-start.5
  418.6 8.0 %fusion.18 = f32[512,1536]{1,0:T(8,128)} fusion(bf16[1536,6144]{1,0:T(8,128)(2,1)} %all-gather.5.cloned.1.call-done, bf16[1024,2048]{1,0:T(8,128)(2,1)S(1)} %copy-done.28, s32[]{:T(128)S(6)} %select_n.95), kind=kOutput, calls=%fused_computation.29 | convolution fusion | flops 3221225472 | bytes 11534340 | tf_op jit(solution)/shard_map/dot_general | solution.py:37
  426.6 8.1 %fusion.45 = bf16[512,1536]{1,0:T(8,128)(2,1)} fusion(bf16[1536,6144]{1,0:T(8,128)(2,1)} %all-gather.5.cloned.1.call-done, bf16[1024,2048]{1,0:T(8,128)(2,1)S(1)} %copy-done.28, s32[]{:T(128)S(6)} %select_n.94), kind=kOutput, calls=%fused_computation.68 | convolution fusion | flops 3222011904 | bytes 9961476 | tf_op jit(solution)/shard_map/dot_general | solution.py:37
  434.7 16.8 %collective-permute-done.5 = bf16[512,1536]{1,0:T(8,128)(2,1)S(1)} collective-permute-done((bf16[512,1536]{1,0:T(8,128)(2,1)S(1)}, bf16[512,1536]{1,0:T(8,128)(2,1)S(1)}, u32[]{:S(2)}, u32[]{:S(2)}) %collective-permute-start.5) | collective-permute-done | bytes 1572896 | tf_op jit(solution)/shard_map/ppermute | solution.py:45
  451.4 0.4 broadcast_select_fusion.1
  452.0 0.9 collective-permute-start.6
  452.9 5.8 fusion.67.grad_ref
  458.7 38.7 %attend_back.1 = (bf16[1024,3200]{1,0:T(8,128)(2,1)}, f32[8,128]{1,0:T(8,128)}) custom-call(bf16[1024,2304]{1,0:T(8,128)(2,1)} %fusion.15.q_ref.k_ref.v_ref, bf16[1024,2304]{1,0:T(8,128)(2,1)} %fusion.15.q_ref.k_ref.v_ref, bf16[1024,2304]{1,0:T(8,128)(2,1)} %fusion.15.q_ref.k_ref.v_ref, f32[1024,896]{1,0:T(8,128)} %fusion.58.gate_ref.logit_ref, ...), custom_call_target="tpu_custom_call" | custom-call | tf_op jit(solution)/shard_map/attend_back/pallas_call | solution.py:351
  497.4 2.9 convolution_convert_fusion.3
  500.4 14.4 %convolution_convert_fusion = bf16[1536,3200]{1,0:T(8,128)(2,1)S(1)} fusion(bf16[1024,1536]{1,0:T(8,128)(2,1)S(1)} %copy-done.15, bf16[1024,3200]{1,0:T(8,128)(2,1)} %get-tuple-element.51), kind=kOutput, calls=%fused_computation | convolution fusion | flops 10071244800 | bytes 19529728 | tf_op jit(solution)/shard_map/dot_general | solution.py:41
  514.8 5.1 pad_maximum_fusion
  520.0 9.3 %fusion.48 = bf16[512,1536]{1,0:T(8,128)(2,1)S(1)} fusion(bf16[1536,3968]{1,0:T(8,128)(2,1)} %all-gather.3.cloned.1.call-done, bf16[1024,3200]{1,0:T(8,128)(2,1)} %get-tuple-element.51, s32[]{:T(128)S(6)} %select_n.94), kind=kOutput, calls=%fused_computation.69 | convolution fusion | flops 5033951232 | bytes 14680068 | tf_op jit(solution)/shard_map/dot_general | solution.py:37
  529.3 1.0 collective-permute-start.7
  530.4 0.8 bitcast_dynamic-update-slice_fusion
  531.2 3.1 multiply_convert_fusion.3
  534.3 25.6 %collective-permute-done.7 = bf16[512,1536]{1,0:T(8,128)(2,1)S(1)} collective-permute-done((bf16[512,1536]{1,0:T(8,128)(2,1)S(1)}, bf16[512,1536]{1,0:T(8,128)(2,1)S(1)}, u32[]{:S(2)}, u32[]{:S(2)}) %collective-permute-start.7) | collective-permute-done | bytes 1572896 | tf_op jit(solution)/shard_map/ppermute | solution.py:45
  560.0 10.8 %fusion.42 = (f32[1536]{0:T(1024)S(1)}, f32[512]{0:T(512)S(1)}, f32[512,1536]{1,0:T(8,128)}) fusion(bf16[512,1536]{1,0:T(8,128)(2,1)S(1)} %copy-done.8, f32[512]{0:T(512)S(1)} %copy-done.26, f32[1536]{0:T(1024)S(1)} %copy-done.22, bf16[512,1536]{1,0:T(8,128)(2,1)S(1)} %collective-permute-done.7, bf16[1536,3968]{1,0:T(8,128)(2,1)} %all-gather.3.cloned.1.call-done, ...), kind=kOutput, calls=%fused_computation.53 | convolution fusion | flops 5040240640 | bytes 19415044 | tf_op jit(solution)/shard_map/dot_general | solution.py:37
  570.8 39.5 %all-reduce.2 = (f32[1536]{0:T(1024)}, f32[24]{0:T(128)}, f32[1536]{0:T(1024)}) all-reduce(f32[1536]{0:T(1024)S(1)} %get-tuple-element.66, f32[24]{0:T(128)S(1)} %bitcast_dynamic-update-slice_fusion, f32[1536]{0:T(1024)S(1)} %get-tuple-element.64), channel_id=1, replica_groups=mesh['dp'=16,'tensor'=2] {'dp','tensor'}, use_global_device_ids=true, to_apply=%region_5.6 | all-reduce | flops 3096 | bytes 24768 | tf_op jit(solution)/shard_map/psum | solution.py:489
  610.3 5.5 fusion.41
  615.8 1.9 convert_bitcast_fusion
  617.8 3.3 reshape.115
  621.1 97.5 %reduce-scatter.4.cloned.1.call-done = bf16[96,3968]{1,0:T(8,128)(2,1)} async-done(((bf16[1536,3968]{1,0:T(8,128)(2,1)}), bf16[96,3968]{1,0:T(8,128)(2,1)}) %reduce-scatter.4.cloned.1.call-update) | async-done | bytes 761872 | tf_op jit(solution)/shard_map/reduce_scatter | solution.py:82
  718.6 1.2 slice_convert_fusion
  719.9 1.6 reshape.110
  721.5 0.7 copy.23
  722.2 1.6 convert_bitcast_fusion.1
  (92 shorter events, 1.5 us)
Async XLA Ops:
  7.2 4.0 copy-start.18
  7.2 4.3 copy-start.19
  7.2 104.8 %all-gather.3.cloned.1.call-start = ((), (), s32[]{:S(2)}) async-start(), calls=%async_computation.3 | async-start | bytes 12951552 | tf_op jit(solution)/shard_map/all_gather | solution.py:78
  11.1 101.7 %copy-start.10 = (bf16[512,1536]{1,0:T(8,128)(2,1)S(1)}, bf16[512,1536]{1,0:T(8,128)(2,1)}, u32[]{:S(2)}) copy-start(bf16[512,1536]{1,0:T(8,128)(2,1)} %param.21) | copy-start | bytes 4718596
  11.1 299.4 %all-gather.5.cloned.1.call-start = ((), (), s32[]{:S(2)}) async-start(), calls=%async_computation.4 | async-start | bytes 20054016 | tf_op jit(solution)/shard_map/all_gather | solution.py:78
  11.5 104.3 %copy-start.6 = (bf16[512,1536]{1,0:T(8,128)(2,1)S(1)}, bf16[512,1536]{1,0:T(8,128)(2,1)}, u32[]{:S(2)}) copy-start(bf16[512,1536]{1,0:T(8,128)(2,1)} %param.11) | copy-start | bytes 4718596
  12.6 103.5 %copy-start.21 = (f32[1536]{0:T(1024)S(1)}, f32[1536]{0:T(1024)}, u32[]{:S(2)}) copy-start(f32[1536]{0:T(1024)} %param.12) | copy-start | bytes 18436
  112.0 503.8 %reduce-scatter.8.cloned.1.call-start = ((), (), s32[]{:S(2)}) async-start(), calls=%async_computation.7 | async-start | bytes 6684672 | tf_op jit(solution)/shard_map/reduce_scatter | solution.py:82
  112.8 39.1 %copy-start.23 = (f32[512]{0:T(512)}, f32[512]{0:T(512)S(1)}, u32[]{:S(2)}) copy-start(f32[512]{0:T(512)S(1)} %fusion.88) | copy-start | bytes 6148
  114.3 4.0 copy-start.27
  114.3 37.6 %collective-permute-start.1 = (bf16[512,1536]{1,0:T(8,128)(2,1)}, bf16[512,1536]{1,0:T(8,128)(2,1)}, u32[]{:S(2)}, u32[]{:S(2)}) collective-permute-start(bf16[512,1536]{1,0:T(8,128)(2,1)} %fusion.44), channel_id=1, source_target_pairs={{0,1},{1,0},{2,3},{3,2},{4,5},{5,4},{6,7},{7,6},{8,9},{9,8},{10,11... | collective-permute-start | bytes 4718600 | tf_op jit(solution)/shard_map/ppermute | solution.py:45
  116.1 68.7 %copy-start.25 = (f32[512]{0:T(512)}, f32[512]{0:T(512)S(1)}, u32[]{:S(2)}) copy-start(f32[512]{0:T(512)S(1)} %add_rsqrt_fusion.1) | copy-start | bytes 6148
  117.7 67.1 %collective-permute-start = (bf16[512,1536]{1,0:T(8,128)(2,1)}, bf16[512,1536]{1,0:T(8,128)(2,1)}, u32[]{:S(2)}, u32[]{:S(2)}) collective-permute-start(bf16[512,1536]{1,0:T(8,128)(2,1)} %fusion.37), channel_id=1, source_target_pairs={{0,1},{1,0},{2,3},{3,2},{4,5},{5,4},{6,7},{7,6},{8,9},{9,8},{10,11... | collective-permute-start | bytes 4718600 | tf_op jit(solution)/shard_map/ppermute | solution.py:45
  151.8 37.4 %slice-start = ((s8[12189696]{0:T(1024)(128)(4,1)}), s8[4194304]{0:T(1024)(128)(4,1)S(1)}, s32[]{:S(2)}) async-start(s8[12189696]{0:T(1024)(128)(4,1)} %bitcast.31), calls=%async_computation.8 | async-start | bytes 8388608
  154.1 35.2 %slice-start.1 = ((s8[12189696]{0:T(1024)(128)(4,1)}), s8[4194304]{0:T(1024)(128)(4,1)S(1)}, s32[]{:S(2)}) async-start(s8[12189696]{0:T(1024)(128)(4,1)} %bitcast.31), calls=%async_computation.9 | async-start | bytes 8388608
  187.2 3.8 slice-start.2
  189.2 7.0 copy-start.14
  205.4 24.8 %copy-start.3 = (f32[8,128]{1,0:T(8,128)}, f32[8,128]{1,0:T(8,128)S(1)}, u32[]{:S(2)}) copy-start(f32[8,128]{1,0:T(8,128)S(1)} %broadcast_in_dim.16.bias_ref) | copy-start | bytes 12292
  230.3 4.6 copy-start
  230.3 4.6 copy-start.1
  230.3 4.6 copy-start.2
  230.3 6.2 copy-start.4
  234.9 35.9 %collective-permute-start.2 = (bf16[512,1536]{1,0:T(8,128)(2,1)S(1)}, bf16[512,1536]{1,0:T(8,128)(2,1)}, u32[]{:S(2)}, u32[]{:S(2)}) collective-permute-start(bf16[512,1536]{1,0:T(8,128)(2,1)S(1)} %convolution_convert_fusion.4), channel_id=1, source_target_pairs={{0,1},{1,0},{2,3},{3,2},{4,5},{5,4},{6,7},{7,6},{8,9},{9,8},{10,11... | collective-permute-start | bytes 4718600 | tf_op jit(solution)/shard_map/ppermute | solution.py:45
  236.4 34.3 %copy-start.7 = (bf16[512,1536]{1,0:T(8,128)(2,1)S(1)}, bf16[512,1536]{1,0:T(8,128)(2,1)}, u32[]{:S(2)}) copy-start(bf16[512,1536]{1,0:T(8,128)(2,1)} %param.11) | copy-start | bytes 4718596
  239.7 33.3 %copy-start.20 = (f32[1536]{0:T(1024)S(1)}, f32[1536]{0:T(1024)}, u32[]{:S(2)}) copy-start(f32[1536]{0:T(1024)} %param.17) | copy-start | bytes 18436
  273.2 34.9 %collective-permute-start.3 = (bf16[512,1536]{1,0:T(8,128)(2,1)S(1)}, bf16[512,1536]{1,0:T(8,128)(2,1)S(1)}, u32[]{:S(2)}, u32[]{:S(2)}) collective-permute-start(bf16[512,1536]{1,0:T(8,128)(2,1)S(1)} %multiply_convert_fusion.4), channel_id=1, source_target_pairs={{0,1},{1,0},{2,3},{3,2},{4,5},{5,4},{6,7},{7,6},{8,9},{9,8},{10,11... | collective-permute-start | bytes 4718600 | tf_op jit(solution)/shard_map/ppermute | solution.py:45
  310.5 12.0 %copy-start.16 = (bf16[512,1536]{1,0:T(8,128)(2,1)S(1)}, bf16[512,1536]{1,0:T(8,128)(2,1)}, u32[]{:S(2)}) copy-start(bf16[512,1536]{1,0:T(8,128)(2,1)} %get-tuple-element.80) | copy-start | bytes 4718596
  310.5 12.0 %copy-start.17 = (bf16[512,1536]{1,0:T(8,128)(2,1)S(1)}, bf16[512,1536]{1,0:T(8,128)(2,1)}, u32[]{:S(2)}) copy-start(bf16[512,1536]{1,0:T(8,128)(2,1)} %get-tuple-element.81) | copy-start | bytes 4718596
  361.8 256.0 %reduce-scatter.6.cloned.1.call-start = ((), (), s32[]{:S(2)}) async-start(), calls=%async_computation.6 | async-start | bytes 13369344 | tf_op jit(solution)/shard_map/reduce_scatter | solution.py:82
  374.5 34.6 %collective-permute-start.4 = (bf16[512,1536]{1,0:T(8,128)(2,1)}, bf16[512,1536]{1,0:T(8,128)(2,1)}, u32[]{:S(2)}, u32[]{:S(2)}) collective-permute-start(bf16[512,1536]{1,0:T(8,128)(2,1)} %fusion.53), channel_id=1, source_target_pairs={{0,1},{1,0},{2,3},{3,2},{4,5},{5,4},{6,7},{7,6},{8,9},{9,8},{10,11... | collective-permute-start | bytes 4718600 | tf_op jit(solution)/shard_map/ppermute | solution.py:45
  409.1 3.6 copy-start.24
  409.1 309.5 %reduce-scatter.4.cloned.1.call-start = ((), (), s32[]{:S(2)}) async-start(), calls=%async_computation.5 | async-start | bytes 12951552 | tf_op jit(solution)/shard_map/reduce_scatter | solution.py:82
  409.2 3.5 copy-start.11
  409.2 4.1 copy-start.12
  413.3 5.3 copy-start.28
  417.8 33.7 %collective-permute-start.5 = (bf16[512,1536]{1,0:T(8,128)(2,1)S(1)}, bf16[512,1536]{1,0:T(8,128)(2,1)S(1)}, u32[]{:S(2)}, u32[]{:S(2)}) collective-permute-start(bf16[512,1536]{1,0:T(8,128)(2,1)S(1)} %get-tuple-element.41), channel_id=1, source_target_pairs={{0,1},{1,0},{2,3},{3,2},{4,5},{5,4},{6,7},{7,6},{8,9},{9,8},{10,11... | collective-permute-start | bytes 4718600 | tf_op jit(solution)/shard_map/ppermute | solution.py:45
  452.0 48.3 %collective-permute-start.6 = (bf16[512,1536]{1,0:T(8,128)(2,1)}, bf16[512,1536]{1,0:T(8,128)(2,1)}, u32[]{:S(2)}, u32[]{:S(2)}) collective-permute-start(bf16[512,1536]{1,0:T(8,128)(2,1)} %fusion.45), channel_id=1, source_target_pairs={{0,1},{1,0},{2,3},{3,2},{4,5},{5,4},{6,7},{7,6},{8,9},{9,8},{10,11... | collective-permute-start | bytes 4718600 | tf_op jit(solution)/shard_map/ppermute | solution.py:45
  458.7 38.7 %copy-start.5 = (bf16[1024,768]{1,0:T(8,128)(2,1)S(1)}, bf16[1024,768]{1,0:T(8,128)(2,1)}, u32[]{:S(2)}) copy-start(bf16[1024,768]{1,0:T(8,128)(2,1)} %copy-done.4) | copy-start | bytes 4718596
  497.4 3.0 copy-start.15
  520.0 11.2 %copy-start.13 = (f32[512,1536]{1,0:T(8,128)S(1)}, f32[512,1536]{1,0:T(8,128)}, u32[]{:S(2)}) copy-start(f32[512,1536]{1,0:T(8,128)} %fusion.18) | copy-start | bytes 9437188
  529.3 30.6 %collective-permute-start.7 = (bf16[512,1536]{1,0:T(8,128)(2,1)S(1)}, bf16[512,1536]{1,0:T(8,128)(2,1)S(1)}, u32[]{:S(2)}, u32[]{:S(2)}) collective-permute-start(bf16[512,1536]{1,0:T(8,128)(2,1)S(1)} %fusion.48), channel_id=1, source_target_pairs={{0,1},{1,0},{2,3},{3,2},{4,5},{5,4},{6,7},{7,6},{8,9},{9,8},{10,11... | collective-permute-start | bytes 4718600 | tf_op jit(solution)/shard_map/ppermute | solution.py:45
  531.1 28.8 %copy-start.8 = (bf16[512,1536]{1,0:T(8,128)(2,1)S(1)}, bf16[512,1536]{1,0:T(8,128)(2,1)}, u32[]{:S(2)}) copy-start(bf16[512,1536]{1,0:T(8,128)(2,1)} %param.11) | copy-start | bytes 4718596
  531.1 28.8 %copy-start.22 = (f32[1536]{0:T(1024)S(1)}, f32[1536]{0:T(1024)}, u32[]{:S(2)}) copy-start(f32[1536]{0:T(1024)} %param.12) | copy-start | bytes 18436
  531.2 28.8 %copy-start.26 = (f32[512]{0:T(512)S(1)}, f32[512]{0:T(512)}, u32[]{:S(2)}) copy-start(f32[512]{0:T(512)} %copy-done.25) | copy-start | bytes 6148
  534.3 76.0 %copy-start.9 = (bf16[512,1536]{1,0:T(8,128)(2,1)S(1)}, bf16[512,1536]{1,0:T(8,128)(2,1)}, u32[]{:S(2)}) copy-start(bf16[512,1536]{1,0:T(8,128)(2,1)} %param.11) | copy-start | bytes 4718596
Sparse Core Ops, SparseCore 0:
  11.3 100.7 all-gather.2
  114.2 97.1 all-gather.4
  361.9 83.3 reduce-scatter.7
  449.2 134.1 reduce-scatter.5
  587.4 131.2 reduce-scatter.3

commit v4 on v3

--- a/solution.py
+++ b/solution.py
@@ -80,6 +80,60 @@
 
 def scatter_dp(grad):
     return lax.psum_scatter(grad, "dp", scatter_dimension=0, tiled=True)
+
+
+def trade(value, axis, mask):
+    size = lax.axis_size(axis)
+    return lax.ppermute(value, axis, [(i, i ^ mask) for i in range(size)])
+
+
+def take(array, axis, index):
+    return lax.dynamic_index_in_dim(array, index, axis, keepdims=False)
+
+
+def scatter_links(first, second, beside):
+    size = lax.axis_size("dp")
+    if size % 4 or size & (size - 1):
+        return (scatter_dp(first).astype(F32), scatter_dp(second).astype(F32), beside)
+    layers = size // 4
+    index = lax.axis_index("dp")
+    core, side, layer = (index % 2, index // 2 % 2, index // 4)
+
+    def over_core(grad):
+        grad = grad.reshape(layers, 2, 2, grad.shape[0] // size, grad.shape[1])
+        arrived = trade(take(grad, 2, 1 - core), "dp", 1)
+        return (take(grad, 2, core).astype(F32) + arrived.astype(F32)).astype(BF16)
+
+    def side_pieces(grad, axis):
+        return [take(grad, axis, side), trade(take(grad, axis, 1 - side), "dp", 2)]
+
+    def layer_pieces(grad):
+        sent = [trade(take(grad, 0, layer ^ k), "dp", 4 * k) for k in range(1, layers)]
+        return [take(grad, 0, layer), *sent]
+
+    def total(pieces):
+        result = pieces[0].astype(F32)
+        for piece in pieces[1:]:
+            result = result + piece.astype(F32)
+        return result
+
+    first, second = hold(over_core(first), over_core(second))
+    first, second, beside = hold(side_pieces(first, 1), layer_pieces(second), beside)
+    first, second = hold(total(first).astype(BF16), total(second).astype(BF16))
+    return (total(layer_pieces(first)), total(side_pieces(second, 0)), beside)
+
+
+def sum_all(value):
+    for axis in ("dp", "tensor"):
+        size = lax.axis_size(axis)
+        if size & (size - 1):
+            value = lax.psum(value, axis)
+            continue
+        step = 1
+        while step < size:
+            value = value + trade(value, axis, step)
+            step *= 2
+    return value
 
 
 def head_span(lane, head):
@@ -190,9 +244,10 @@
     part = groups * wide
 
     def columns(which):
+        first = which * part + (PAD if which == 3 else 0)
         if groups == 1:
-            return slice(which * part, which * part + wide)
-        return pl.ds(pl.multiple_of(which * part + group * wide, wide), wide)
+            return slice(first, first + wide)
+        return pl.ds(pl.multiple_of(first + group * wide, wide), wide)
 
     @pl.when(group == 0)
     def _():
@@ -278,7 +333,7 @@
         grad_decay = jnp.transpose(row_ref[...]) - col_ref[...]
         logit = logit_ref[...] + bias_ref[0:1]
         grad_logit = running_sum(grad_decay, True) * jax.nn.sigmoid(-logit)
-        out_ref[:, 4 * part :] = grad_logit.astype(BF16)
+        out_ref[:, 3 * part : 3 * part + PAD] = grad_logit.astype(BF16)
         bias_out_ref[...] = jnp.broadcast_to(jnp.sum(grad_logit, axis=0, keepdims=True), (8, PAD))
 
 
@@ -299,10 +354,14 @@
     return per_group, groups, wide, of
 
 
-def logit_block(gate_logit, part):
-    if part % PAD == 0:
-        return gate_logit, pl.BlockSpec((SLOTS, PAD), lambda s, g: (s, part // PAD))
-    return gate_logit[:, part:], pl.BlockSpec((SLOTS, PAD), lambda s, g: (s, 0))
+def logit_block(gate_logit):
+    return gate_logit, pl.BlockSpec((SLOTS, PAD), lambda s, g: (s, 0))
+
+
+def gate_block(gate_logit, part, wide):
+    if part % 128 == 0:
+        return gate_logit, pl.BlockSpec((SLOTS, wide), lambda s, g: (s, g + PAD // wide))
+    return gate_logit[:, PAD:], pl.BlockSpec((SLOTS, wide), lambda s, g: (s, g))
 
 
 def attend(proj, gate_logit, bias_rows, lengths, part):
@@ -310,8 +369,8 @@
     seqs = rows // SLOTS
     per_group, groups, wide, of = head_blocks(part)
     fix = lambda f: (lambda s, g, lengths: f(s, g))
-    parts = [of(proj, 0, 3), of(proj, 1, 3), of(proj, 2, 3), of(gate_logit, 0, 1)]
-    parts.append(logit_block(gate_logit, part))
+    parts = [of(proj, 0, 3), of(proj, 1, 3), of(proj, 2, 3), gate_block(gate_logit, part, wide)]
+    parts.append(logit_block(gate_logit))
     parts.append((bias_rows, pl.BlockSpec((8, PAD), lambda s, g: (0, 0))))
     wide_spec = pl.BlockSpec((SLOTS, wide), lambda s, g: (s, g))
     outs = [
@@ -341,9 +400,9 @@
     rows = proj.shape[0]
     seqs = rows // SLOTS
     per_group, groups, wide, of = head_blocks(part)
-    parts = [of(proj, 0, 3), of(proj, 1, 3), of(proj, 2, 3), of(gate_logit, 0, 1)]
+    parts = [of(proj, 0, 3), of(proj, 1, 3), of(proj, 2, 3), gate_block(gate_logit, part, wide)]
     parts += [of(attended, 0, 1), of(grad_gated, 0, 1)]
-    parts.append(logit_block(gate_logit, part))
+    parts.append(logit_block(gate_logit))
     parts.append((bias_rows, pl.BlockSpec((8, PAD), lambda s, g: (0, 0))))
     parts.append((shift, pl.BlockSpec((PAD, SLOTS), lambda s, g: (s, 0))))
     parts.append((keyb, pl.BlockSpec((SLOTS, PAD), lambda s, g: (s, 0))))
@@ -403,21 +462,27 @@
     valid = (positions % SLOTS < own_lengths).astype(F32)[:, None]
 
     attn_shard = jnp.concatenate(
-        [w_attn.reshape(own_d, 4 * part), jnp.pad(w_forget, ((0, 0), (0, PAD - heads_dev)))], axis=1
+        [
+            w_attn[:, :3].reshape(own_d, 3 * part),
+            jnp.pad(w_forget, ((0, 0), (0, PAD - heads_dev))),
+            w_attn[:, 3],
+        ],
+        axis=1,
     )
     attn_cols = 4 * part + PAD
     first_full = gather_dp(jnp.concatenate([attn_shard, w_out.T], axis=1))
     second_shard = jnp.concatenate([w_down.T, w_mlp.reshape(own_d, 2 * units)], axis=1)
-    first_full, second_shard = hold(first_full, second_shard)
-    second_full = gather_dp(second_shard)
-    attn_full, out_full = (first_full[:, :attn_cols], first_full[:, attn_cols:])
-    down_full, mlp_full = (second_full[:, :units], second_full[:, units:])
-
     input_wide = layer_input.astype(F32)
     scaled_attn, inverse_attn = norm_parts(input_wide)
     normed_all = share_rows((scaled_attn * gain_attn).astype(BF16))
     grad_final = cotangent.astype(F32) * valid
-    normed_all, grad_final_all = hold(normed_all, share_rows(grad_final.astype(BF16)))
+    grad_final_all = share_rows(grad_final.astype(BF16))
+    first_full, second_shard, normed_all, grad_final_all = hold(
+        first_full, second_shard, normed_all, grad_final_all
+    )
+    second_full = gather_dp(second_shard)
+    attn_full, out_full = (first_full[:, :attn_cols], first_full[:, attn_cols:])
+    down_full, mlp_full = (second_full[:, :units], second_full[:, units:])
 
     proj = dot_nn(normed_all, attn_full[:, : 3 * part]).astype(BF16)
     gate_logit = dot_nn(normed_all, attn_full[:, 3 * part :])
@@ -474,31 +539,40 @@
     def attn_back_term(first_row, row_count):
         return dot_nt(lax.dynamic_slice_in_dim(grad_proj, first_row, row_count), attn_full)
 
-    first_grad = jnp.concatenate(
-        [dot_tn(normed_all, grad_proj), dot_tn(grad_branch_all, gated)], axis=1
-    ).astype(BF16)
-    first_part = scatter_dp(first_grad)
     leaving, staying = term_parts(attn_back_term, own_rows)
-    grad_normed_attn = staying + cross(leaving).astype(F32)
-    attn_part, out_part = (first_part[:, :attn_cols], first_part[:, attn_cols:])
+    arrived_back = cross(leaving)
+    main_grad = dot_tn(normed_all, grad_proj[:, : 3 * part + PAD]).astype(BF16)
+    rest_grad = jnp.concatenate(
+        [
+            dot_tn(normed_all, grad_proj[:, 3 * part + PAD :]).astype(BF16),
+            dot_tn(grad_branch_all, gated).astype(BF16),
+        ],
+        axis=1,
+    )
+    main_part, rest_part, arrived_back = scatter_links(main_grad, rest_grad, arrived_back)
+    grad_normed_attn = staying + arrived_back.astype(F32)
     gain_attn_part = jnp.sum(scaled_attn * grad_normed_attn, axis=0)
     grad_input = grad_middle + norm_back(grad_normed_attn, scaled_attn, inverse_attn, gain_attn)
     bias_full = lax.dynamic_update_slice_in_dim(
         jnp.zeros(forget_bias.shape, F32), bias_part, tensor_index * heads_dev, 0
     )
-    grad_gain_attn, grad_gain_mlp, grad_forget_bias = lax.psum(
-        (gain_attn_part, gain_mlp_part, bias_full), ("dp", "tensor")
-    )
-    attn_part = attn_part.astype(F32)
+    heads = forget_bias.shape[0]
+    sums = sum_all(
+        jnp.concatenate(
+            [gain_attn_part, gain_mlp_part, jnp.pad(bias_full, (0, -heads % 128))]
+        ).reshape(-1, 128)
+    ).reshape(-1)
     return (
         layer_output,
         grad_input,
-        grad_gain_attn,
-        attn_part[:, : 4 * part].reshape(own_d, 4, part),
-        attn_part[:, 4 * part : 4 * part + heads_dev],
-        grad_forget_bias,
-        out_part.astype(F32).T,
-        grad_gain_mlp,
+        sums[:width],
+        jnp.concatenate([main_part[:, : 3 * part], rest_part[:, :part]], axis=1).reshape(
+            own_d, 4, part
+        ),
+        main_part[:, 3 * part : 3 * part + heads_dev],
+        sums[2 * width : 2 * width + heads],
+        rest_part[:, part:].T,
+        sums[width : 2 * width],
         mlp_part.astype(F32).reshape(own_d, 2, units),
         down_part.astype(F32).T,
     )

time: 735 us -> 650 us (0.88)
  waiting for transfers between devices: 368 us -> 264 us
  blocking collectives: 39.5 us -> 0 us
  starting transfers between devices: 9.43 us -> 38.2 us
  local copies, waits for them, and re-layouts: 11.3 us -> 32.7 us
    reduce_scatter x3 -> x2, waiting for transfers between devices: 97.5 us -> 0.01 us  [scatter_dp(): return lax.psum_scatter(grad, 'dp', scatter_dimension=0, tiled=True)]
    all_gather x2, waiting for transfers between devices: 99.4 us -> 23.1 us  [gather_dp(): return lax.all_gather(shard, 'dp', axis=0, tiled=True)]
    ppermute x0 -> x15, waiting for transfers between devices: none -> 70.5 us  [trade(): return lax.ppermute(value, axis, [(i, i ^ mask) for i in range(size)])]
    psum x1 -> x0, blocking collectives: 39.5 us -> none  [on_device(): lax.psum((gain_attn_part, gain_mlp_part, bias_full), ('dp', 'tensor'))]
    ppermute x0 -> x15, starting transfers between devices: none -> 27.1 us  [trade(): return lax.ppermute(value, axis, [(i, i ^ mask) for i in range(size)])]
    convert_element_type x2 -> x5, other arithmetic: 2.62 us -> 13 us  [the longest x2 7.59 us: over_core(): return (take(grad, 2, core).astype(F32) + arrived.astype(F32)).astype(BF16)]
    squeeze x0 -> x6, local copies, waits for them, and re-layouts: none -> 9.69 us  [take(): return lax.dynamic_index_in_dim(array, index, axis, keepdims=False)]
    dot_general x4 -> x5, matrix products: 49.5 us -> 52.3 us  [dot_tn(): lax.dot_general(a, b, (((0,), (0,)), ((), ())), preferred_element_type=F32)]
  transfers between devices with their start and end apart: 13 -> 27, of which waited for: 8 -> 13; matrix products, arithmetic and copies ran while one was open for 24% -> 31% of each run, Pallas kernels for 9% -> 10%
where the time goes in v4:
time: 650 us; the launch traced here: 644 us
  waiting for transfers between devices  264 us (41%)
  matrix products  181 us (28%)
  Pallas kernels  63.8 us (10%)
  other arithmetic  49.1 us (8%)
  starting transfers between devices  38.2 us (6%)
  local copies, waits for them, and re-layouts  32.7 us (5%)
  between operations  15.2 us (2%)
    ppermute x8, waiting for transfers between devices, swap(): return lax.ppermute(rows, 'tensor', [(0, 1), (1, 0)])  171 us
    ppermute x15, waiting for transfers between devices, trade(): return lax.ppermute(value, axis, [(i, i ^ mask) for i in range(size)])  70.5 us
    dot_general x8, matrix products, dot_nt(): lax.dot_general(a, b, (((1,), (1,)), ((), ())), preferred_element_type=F32)  65.6 us
    dot_general x6, matrix products, dot_nn(): lax.dot_general(a, b, (((1,), (0,)), ((), ())), preferred_element_type=F32)  63.2 us
    dot_general x5, matrix products, dot_tn(): lax.dot_general(a, b, (((0,), (0,)), ((), ())), preferred_element_type=F32)  52.3 us
    pallas_call x1, Pallas kernels, attend_back(): pl.pallas_call(functools.partial(attend_back_body, per_group=per_group, g...  38.8 us
    ppermute x15, starting transfers between devices, trade(): return lax.ppermute(value, axis, [(i, i ^ mask) for i in range(size)])  27.1 us
    pallas_call x1, Pallas kernels, attend(): pl.pallas_call(functools.partial(attend_body, per_group=per_group), out_s...  25 us
  transfers between devices with their start and end apart: 27, of which 13 were waited for; matrix products, arithmetic and copies ran while one was open for 31% of the time, Pallas kernels for 10%

profile of v4, /device:TPU:0, one launch (start us, length us, event | category | flops | bytes accessed | tf_op | source)
XLA Modules:
  0.0 644.2 jit_solution(3604252977753201153)
XLA Ops:
  8.7 1.9 copy.41
  11.6 2.0 fusion.82
  15.8 3.0 collective-permute-start.1
  23.3 31.1 %collective-permute-done.1 = bf16[512,1536]{1,0:T(8,128)(2,1)} collective-permute-done((bf16[512,1536]{1,0:T(8,128)(2,1)}, bf16[512,1536]{1,0:T(8,128)(2,1)}, u32[]{:S(2)}, u32[]{:S(2)}) %collective-permute-start.1) | collective-permute-done | bytes 1572896 | tf_op jit(solution)/shard_map/ppermute | solution.py:45
  54.4 2.1 broadcast_select_fusion.5
  56.5 30.7 %collective-permute-done = bf16[512,1536]{1,0:T(8,128)(2,1)} collective-permute-done((bf16[512,1536]{1,0:T(8,128)(2,1)}, bf16[512,1536]{1,0:T(8,128)(2,1)}, u32[]{:S(2)}, u32[]{:S(2)}) %collective-permute-start) | collective-permute-done | bytes 1572896 | tf_op jit(solution)/shard_map/ppermute | solution.py:45
  87.2 2.2 broadcast_select_fusion.7
  89.5 1.9 pad_maximum_fusion.3
  91.4 23.1 %all-gather.3.cloned.1.call-done = bf16[1536,3968]{1,0:T(8,128)(2,1)} async-done(((bf16[96,3968]{1,0:T(8,128)(2,1)}), bf16[1536,3968]{1,0:T(8,128)(2,1)}) %all-gather.3.cloned.1.call-update) | async-done | bytes 12189712 | tf_op jit(solution)/shard_map/all_gather | solution.py:78
  114.7 7.2 %fusion.61.gate_ref.logit_ref = f32[1024,896]{1,0:T(8,128)} fusion(bf16[1024,1536]{1,0:T(8,128)(2,1)S(1)} %get-tuple-element.43, bf16[1536,3968]{1,0:T(8,128)(2,1)} %all-gather.3.cloned.1.call-done), kind=kOutput, calls=%fused_computation.80 | convolution fusion | flops 2818572288 | bytes 9568256 | tf_op jit(solution)/shard_map/dot_general | solution.py:33
  121.9 9.2 %fusion.16.q_ref.k_ref.v_ref = bf16[1024,2304]{1,0:T(8,128)(2,1)} fusion(bf16[1024,1536]{1,0:T(8,128)(2,1)S(1)} %get-tuple-element.43, bf16[1536,3968]{1,0:T(8,128)(2,1)S(1)} %copy-done.30), kind=kOutput, calls=%fused_computation.29 | convolution fusion | flops 7250116608 | bytes 14942208 | tf_op jit(solution)/shard_map/dot_general | solution.py:33
  131.1 25.0 %attend.1 = (bf16[1024,768]{1,0:T(8,128)(2,1)S(1)}, bf16[1024,768]{1,0:T(8,128)(2,1)S(1)}, f32[128,1024]{1,0:T(8,128)S(1)}, f32[1024,128]{1,0:T(8,128)S(1)}) custom-call(s32[1]{0:T(128)} %copy.46.lengths, bf16[1024,2304]{1,0:T(8,128)(2,1)} %fusion.16.q_ref.k_ref.v_ref, bf16[1024,2304]{1,0:T(8,128)(2,1)} %fusion.16.q_ref.k_ref.v_ref, ...), custom_call_target="tpu_custom_call" | custom-call | tf_op jit(solution)/shard_map/attend/pallas_call | solution.py:383
  156.1 4.6 convolution_convert_fusion.5
  162.3 3.2 fusion.67
  165.6 31.9 %collective-permute-done.2 = bf16[512,1536]{1,0:T(8,128)(2,1)} collective-permute-done((bf16[512,1536]{1,0:T(8,128)(2,1)S(1)}, bf16[512,1536]{1,0:T(8,128)(2,1)}, u32[]{:S(2)}, u32[]{:S(2)}) %collective-permute-start.2) | collective-permute-done | bytes 1572896 | tf_op jit(solution)/shard_map/ppermute | solution.py:45
  197.5 2.2 multiply_reduce_fusion.2
  201.6 34.2 %collective-permute-done.3 = bf16[512,1536]{1,0:T(8,128)(2,1)S(1)} collective-permute-done((bf16[512,1536]{1,0:T(8,128)(2,1)S(1)}, bf16[512,1536]{1,0:T(8,128)(2,1)S(1)}, u32[]{:S(2)}, u32[]{:S(2)}) %collective-permute-start.3) | collective-permute-done | bytes 1572896 | tf_op jit(solution)/shard_map/ppermute | solution.py:45
  235.8 2.4 broadcast_select_fusion.3
  238.2 11.9 %fusion.24 = f32[1024,2048]{1,0:T(8,128)} fusion(bf16[1024,1536]{1,0:T(8,128)(2,1)} %get-tuple-element.48, bf16[1536,6144]{1,0:T(8,128)(2,1)} %all-gather.5.cloned.1.call-done), kind=kOutput, calls=%fused_computation.35 | convolution fusion | flops 6442450944 | bytes 17825792 | tf_op jit(solution)/shard_map/dot_general | solution.py:33
  250.1 11.1 %fusion.12 = f32[1024,2048]{1,0:T(8,128)} fusion(bf16[1536,6144]{1,0:T(8,128)(2,1)} %all-gather.5.cloned.1.call-done, bf16[512,1536]{1,0:T(8,128)(2,1)S(1)} %copy-done.21, bf16[512,1536]{1,0:T(8,128)(2,1)S(1)} %copy-done.20), kind=kOutput, calls=%fused_computation.25 | convolution fusion | flops 6448742400 | bytes 17825792 | tf_op jit(solution)/shard_map/dot_general | solution.py:33
  261.1 17.3 %multiply_convert_fusion = (bf16[1024,2048]{1,0:T(8,128)(2,1)}, bf16[1024,2048]{1,0:T(8,128)(2,1)}, bf16[1024,2048]{1,0:T(8,128)(2,1)}) fusion(f32[1024,2048]{1,0:T(8,128)} %fusion.12, f32[1024,2048]{1,0:T(8,128)} %fusion.24, bf16[1536,6144]{1,0:T(8,128)(2,1)} %all-gather.5.cloned.1.call-done, bf16[512,1536]{1,0:T(8,128)(2,1)} %get-tuple-element.102, ...), kind=kOutput, calls=%fused_computation.15 | convolution fusion | flops 6480199680 | bytes 38797312 | tf_op jit(solution)/shard_map/dot_general | solution.py:33
  278.4 11.3 %convolution_convert_fusion.2 = bf16[1536,2048]{1,0:T(8,128)(2,1)} fusion(bf16[1024,1536]{1,0:T(8,128)(2,1)} %get-tuple-element.48, bf16[1024,2048]{1,0:T(8,128)(2,1)} %get-tuple-element.53), kind=kOutput, calls=%fused_computation.20 | convolution fusion | flops 6445596672 | bytes 13631488 | tf_op jit(solution)/shard_map/dot_general | solution.py:41
  289.8 12.5 %fusion.56 = bf16[512,1536]{1,0:T(8,128)(2,1)} fusion(bf16[1536,6144]{1,0:T(8,128)(2,1)} %all-gather.5.cloned.1.call-done, s32[]{:T(128)S(6)} %select_n.149, bf16[1024,2048]{1,0:T(8,128)(2,1)} %get-tuple-element.95, bf16[1024,2048]{1,0:T(8,128)(2,1)} %get-tuple-element.96), kind=kOutput, calls=%fused_computation.79 | convolution fusion | flops 6451625984 | bytes 22544388 | tf_op jit(solution)/shard_map/dot_general | solution.py:37
  303.6 20.8 %convolution_convert_fusion = bf16[1536,4096]{1,0:T(8,128)(2,1)} fusion(bf16[1024,2048]{1,0:T(8,128)(2,1)} %get-tuple-element.96, bf16[1024,2048]{1,0:T(8,128)(2,1)} %get-tuple-element.95, bf16[512,1536]{1,0:T(8,128)(2,1)} %get-tuple-element.102, bf16[512,1536]{1,0:T(8,128)(2,1)} %get-tuple-element.101), kind=kOutput, calls=%fused_computation | convolution fusion | flops 12914262016 | bytes 24117248 | tf_op jit(solution)/shard_map/dot_general | solution.py:41
  324.4 11.2 %fusion = f32[512,1536]{1,0:T(8,128)S(1)} fusion(bf16[1536,6144]{1,0:T(8,128)(2,1)} %all-gather.5.cloned.1.call-done, s32[]{:T(128)S(6)} %select_n.150, bf16[1024,2048]{1,0:T(8,128)(2,1)} %get-tuple-element.95, bf16[1024,2048]{1,0:T(8,128)(2,1)} %get-tuple-element.96), kind=kOutput, calls=%fused_computation.2 | convolution fusion | flops 6450839552 | bytes 24117252 | tf_op jit(solution)/shard_map/dot_general | solution.py:37
  337.2 2.5 multiply_reduce_fusion
  339.7 4.5 fusion.102
  345.7 8.0 %fusion.20 = f32[512,1536]{1,0:T(8,128)} fusion(bf16[1536,6144]{1,0:T(8,128)(2,1)} %all-gather.5.cloned.1.call-done, bf16[1024,2048]{1,0:T(8,128)(2,1)S(1)} %copy-done.32, s32[]{:T(128)S(6)} %select_n.150), kind=kOutput, calls=%fused_computation.31 | convolution fusion | flops 3221225472 | bytes 11534340 | tf_op jit(solution)/shard_map/dot_general | solution.py:37
  353.7 7.6 %fusion.48 = bf16[512,1536]{1,0:T(8,128)(2,1)} fusion(bf16[1536,6144]{1,0:T(8,128)(2,1)} %all-gather.5.cloned.1.call-done, bf16[1024,2048]{1,0:T(8,128)(2,1)S(1)} %copy-done.32, s32[]{:T(128)S(6)} %select_n.149), kind=kOutput, calls=%fused_computation.76 | convolution fusion | flops 3222011904 | bytes 9961476 | tf_op jit(solution)/shard_map/dot_general | solution.py:37
  361.3 16.6 %collective-permute-done.5 = bf16[512,1536]{1,0:T(8,128)(2,1)S(1)} collective-permute-done((bf16[512,1536]{1,0:T(8,128)(2,1)S(1)}, bf16[512,1536]{1,0:T(8,128)(2,1)S(1)}, u32[]{:S(2)}, u32[]{:S(2)}) %collective-permute-start.5) | collective-permute-done | bytes 1572896 | tf_op jit(solution)/shard_map/ppermute | solution.py:45
  378.3 1.9 pad_maximum_fusion.6
  380.2 1.7 collective-permute-start.6
  381.9 6.5 %fusion.70.grad_ref = bf16[1024,768]{1,0:T(8,128)(2,1)} fusion(bf16[1024,1536]{1,0:T(8,128)(2,1)} %pad_maximum_fusion.6, bf16[1536,3968]{1,0:T(8,128)(2,1)} %all-gather.3.cloned.1.call-done), kind=kOutput, calls=%fused_computation.94 | convolution fusion | flops 2416705536 | bytes 7077888 | tf_op jit(solution)/shard_map/dot_general | solution.py:33
  388.4 4.4 convolution_convert_fusion.3
  392.7 38.8 %attend_back.1 = (bf16[1024,3200]{1,0:T(8,128)(2,1)}, f32[8,128]{1,0:T(8,128)}) custom-call(bf16[1024,2304]{1,0:T(8,128)(2,1)} %fusion.16.q_ref.k_ref.v_ref, bf16[1024,2304]{1,0:T(8,128)(2,1)} %fusion.16.q_ref.k_ref.v_ref, bf16[1024,2304]{1,0:T(8,128)(2,1)} %fusion.16.q_ref.k_ref.v_ref, f32[1024,896]{1,0:T(8,128)} %fusion.61.gate_ref.logit_ref, ...), custom_call_target="tpu_custom_call" | custom-call | tf_op jit(solution)/shard_map/attend_back/pallas_call | solution.py:410
  431.6 11.3 %convolution_convert_fusion.1 = bf16[1536,2432]{1,0:T(8,128)(2,1)S(1)} fusion(bf16[1024,1536]{1,0:T(8,128)(2,1)S(1)} %copy-done.17, bf16[1024,3200]{1,0:T(8,128)(2,1)} %get-tuple-element.62), kind=kOutput, calls=%fused_computation.1 | convolution fusion | flops 7654146048 | bytes 15597568 | tf_op jit(solution)/shard_map/dot_general | solution.py:41
  442.9 2.3 dynamic-slice_bitcast_fusion
  445.2 1.7 copy-done.12
  446.9 4.5 convolution_convert_fusion.4
  451.4 2.5 pad_maximum_fusion.2
  454.0 6.8 %copy.38 = bf16[1536,1536]{1,0:T(8,128)(2,1)} copy(bf16[1536,1536]{0,1:T(8,128)(2,1)} %pad_maximum_fusion.2) | data formatting | bytes 9437184 | tf_op jit(solution)/shard_map/concatenate | solution.py:545
  460.7 3.4 dynamic-slice_bitcast_fusion.1
  464.5 4.5 collective-permute-done.8
  469.0 3.4 fusion.30
  472.4 4.2 fusion.9
  476.7 2.3 dynamic-slice_bitcast_fusion.2
  479.4 8.0 %fusion.51 = bf16[512,1536]{1,0:T(8,128)(2,1)} fusion(bf16[1536,3968]{1,0:T(8,128)(2,1)S(1)} %bitcast.91, bf16[1024,3200]{1,0:T(8,128)(2,1)} %get-tuple-element.62, s32[]{:T(128)S(6)} %select_n.149), kind=kOutput, calls=%fused_computation.77 | convolution fusion | flops 5033951232 | bytes 14680068 | tf_op jit(solution)/shard_map/dot_general | solution.py:37
  492.8 1.8 collective-permute-start.12
  494.6 3.2 multiply_convert_fusion.3
  497.8 1.9 convert_bitcast_fusion
  499.7 24.4 %collective-permute-done.13 = bf16[512,1536]{1,0:T(8,128)(2,1)} collective-permute-done((bf16[512,1536]{1,0:T(8,128)(2,1)}, bf16[512,1536]{1,0:T(8,128)(2,1)}, u32[]{:S(2)}, u32[]{:S(2)}) %collective-permute-start.13) | collective-permute-done | bytes 1572896 | tf_op jit(solution)/shard_map/ppermute | solution.py:45
  524.1 13.1 %collective-permute-done.10 = bf16[2,96,1536]{2,1,0:T(8,128)(2,1)} collective-permute-done((bf16[2,96,1536]{2,1,0:T(8,128)(2,1)}, bf16[2,96,1536]{2,1,0:T(8,128)(2,1)}, u32[]{:S(2)}, u32[]{:S(2)}) %collective-permute-start.10) | collective-permute-done | bytes 589856 | tf_op jit(solution)/shard_map/ppermute | solution.py:87
  537.3 15.4 %collective-permute-done.12 = bf16[2,96,1536]{2,1,0:T(8,128)(2,1)} collective-permute-done((bf16[2,96,1536]{2,1,0:T(8,128)(2,1)}, bf16[2,96,1536]{2,1,0:T(8,128)(2,1)}, u32[]{:S(2)}, u32[]{:S(2)}) %collective-permute-start.12) | collective-permute-done | bytes 589856 | tf_op jit(solution)/shard_map/ppermute | solution.py:87
  552.7 10.6 %fusion.45 = (f32[1536]{0:T(1024)S(1)}, f32[512]{0:T(512)S(1)}, f32[512,1536]{1,0:T(8,128)S(1)}) fusion(bf16[512,1536]{1,0:T(8,128)(2,1)} %param.11, f32[512]{0:T(512)S(1)} %copy-done.29, f32[1536]{0:T(1024)S(1)} %copy-done.25, bf16[512,1536]{1,0:T(8,128)(2,1)} %collective-permute-done.13, bf16[1536,3968]{1,0:T(8,128)(2,1)} %all-gather.3.cloned.1.call-done, ...), kind=kOutput, calls=%fused_computation.61 | convolution fusion | flops 5040240640 | bytes 19415044 | tf_op jit(solution)/shard_map/dot_general | solution.py:37
  563.4 2.0 add_convert_fusion
  565.4 1.9 add_convert_fusion.1
  569.0 12.3 %collective-permute-start.19 = (bf16[96,2432]{1,0:T(8,128)(2,1)S(1)}, bf16[96,2432]{1,0:T(8,128)(2,1)S(1)}, u32[]{:S(2)}, u32[]{:S(2)}) collective-permute-start(bf16[96,2432]{1,0:T(8,128)(2,1)S(1)} %get-tuple-element.111), channel_id=1, source_target_pairs={{0,8},{2,10},{4,12},{6,14},{8,0},{10,2},{12,4},{14,6},{16,24},{18,... | collective-permute-start | bytes 1400840 | tf_op jit(solution)/shard_map/ppermute | solution.py:87
  581.3 2.4 collective-permute-start.21
  585.5 26.4 %collective-permute-done.16 = f32[25,128]{1,0:T(8,128)S(1)} collective-permute-done((f32[25,128]{1,0:T(8,128)S(1)}, f32[25,128]{1,0:T(8,128)S(1)}, u32[]{:S(2)}, u32[]{:S(2)}) %collective-permute-start.16) | collective-permute-done | bytes 12832 | tf_op jit(solution)/shard_map/ppermute | solution.py:87
  612.0 2.4 collective-permute-start.17
  614.4 11.0 %collective-permute-done.17 = f32[25,128]{1,0:T(8,128)S(1)} collective-permute-done((f32[25,128]{1,0:T(8,128)S(1)}, f32[25,128]{1,0:T(8,128)S(1)}, u32[]{:S(2)}, u32[]{:S(2)}) %collective-permute-start.17) | collective-permute-done | bytes 12832 | tf_op jit(solution)/shard_map/ppermute | solution.py:87
  626.9 2.5 fusion.44
  631.9 1.6 reshape.136
  634.2 3.3 reshape.145
  (150 shorter events, 31.3 us)
Async XLA Ops:
  7.2 7.2 %copy-start.9 = (bf16[512,1536]{1,0:T(8,128)(2,1)S(1)}, bf16[512,1536]{1,0:T(8,128)(2,1)}, u32[]{:S(2)}) copy-start(bf16[512,1536]{1,0:T(8,128)(2,1)} %param.21) | copy-start | bytes 4718596
  7.2 107.3 %all-gather.3.cloned.1.call-start = ((), (), s32[]{:S(2)}) async-start(), calls=%async_computation.2 | async-start | bytes 12951552 | tf_op jit(solution)/shard_map/all_gather | solution.py:78
  10.6 8.2 %copy-start.6 = (bf16[512,1536]{1,0:T(8,128)(2,1)S(1)}, bf16[512,1536]{1,0:T(8,128)(2,1)}, u32[]{:S(2)}) copy-start(bf16[512,1536]{1,0:T(8,128)(2,1)} %param.11) | copy-start | bytes 4718596
  11.6 7.7 %copy-start.24 = (f32[1536]{0:T(1024)S(1)}, f32[1536]{0:T(1024)}, u32[]{:S(2)}) copy-start(f32[1536]{0:T(1024)} %param.12) | copy-start | bytes 18436
  13.6 224.6 %all-gather.5.cloned.1.call-start = ((), (), s32[]{:S(2)}) async-start(), calls=%async_computation.3 | async-start | bytes 20054016 | tf_op jit(solution)/shard_map/all_gather | solution.py:78
  14.4 40.0 %copy-start.26 = (f32[512]{0:T(512)}, f32[512]{0:T(512)S(1)}, u32[]{:S(2)}) copy-start(f32[512]{0:T(512)S(1)} %fusion.96) | copy-start | bytes 6148
  15.8 6.4 copy-start.22
  15.8 38.6 %collective-permute-start.1 = (bf16[512,1536]{1,0:T(8,128)(2,1)}, bf16[512,1536]{1,0:T(8,128)(2,1)}, u32[]{:S(2)}, u32[]{:S(2)}) collective-permute-start(bf16[512,1536]{1,0:T(8,128)(2,1)} %fusion.47), channel_id=1, source_target_pairs={{0,1},{1,0},{2,3},{3,2},{4,5},{5,4},{6,7},{7,6},{8,9},{9,8},{10,11... | collective-permute-start | bytes 4718600 | tf_op jit(solution)/shard_map/ppermute | solution.py:45
  19.2 68.0 %copy-start.28 = (f32[512]{0:T(512)}, f32[512]{0:T(512)S(1)}, u32[]{:S(2)}) copy-start(f32[512]{0:T(512)S(1)} %add_rsqrt_fusion.1) | copy-start | bytes 6148
  20.8 66.4 %collective-permute-start = (bf16[512,1536]{1,0:T(8,128)(2,1)}, bf16[512,1536]{1,0:T(8,128)(2,1)}, u32[]{:S(2)}, u32[]{:S(2)}) collective-permute-start(bf16[512,1536]{1,0:T(8,128)(2,1)} %fusion.40), channel_id=1, source_target_pairs={{0,1},{1,0},{2,3},{3,2},{4,5},{5,4},{6,7},{7,6},{8,9},{9,8},{10,11... | collective-permute-start | bytes 4718600 | tf_op jit(solution)/shard_map/ppermute | solution.py:45
  89.5 25.1 %copy-start.31 = (f32[24]{0:T(128)S(1)}, f32[24]{0:T(128)}, u32[]{:S(2)}) copy-start(f32[24]{0:T(128)} %param.15) | copy-start | bytes 292
  91.4 30.5 %copy-start.16 = (bf16[1024,1536]{1,0:T(8,128)(2,1)}, bf16[1024,1536]{1,0:T(8,128)(2,1)S(1)}, u32[]{:S(2)}) copy-start(bf16[1024,1536]{1,0:T(8,128)(2,1)S(1)} %get-tuple-element.43) | copy-start | bytes 9437188
  114.5 383.3 %reduce-scatter.5.cloned.1.call-start = ((), (), s32[]{:S(2)}) async-start(), calls=%async_computation.5 | async-start | bytes 6684672 | tf_op jit(solution)/shard_map/reduce_scatter | solution.py:82
  114.7 7.2 %copy-start.30 = (bf16[1536,3968]{1,0:T(8,128)(2,1)S(1)}, bf16[1536,3968]{1,0:T(8,128)(2,1)}, u32[]{:S(2)}) copy-start(bf16[1536,3968]{1,0:T(8,128)(2,1)} %all-gather.3.cloned.1.call-done) | copy-start | bytes 36569092
  131.1 25.0 %copy-start.3 = (f32[8,128]{1,0:T(8,128)}, f32[8,128]{1,0:T(8,128)S(1)}, u32[]{:S(2)}) copy-start(f32[8,128]{1,0:T(8,128)S(1)} %broadcast_in_dim.16.bias_ref) | copy-start | bytes 12292
  156.1 4.6 copy-start
  156.1 4.6 copy-start.1
  156.1 4.6 copy-start.2
  156.1 6.2 copy-start.4
  160.8 36.7 %collective-permute-start.2 = (bf16[512,1536]{1,0:T(8,128)(2,1)S(1)}, bf16[512,1536]{1,0:T(8,128)(2,1)}, u32[]{:S(2)}, u32[]{:S(2)}) collective-permute-start(bf16[512,1536]{1,0:T(8,128)(2,1)S(1)} %convolution_convert_fusion.5), channel_id=1, source_target_pairs={{0,1},{1,0},{2,3},{3,2},{4,5},{5,4},{6,7},{7,6},{8,9},{9,8},{10,11... | collective-permute-start | bytes 4718600 | tf_op jit(solution)/shard_map/ppermute | solution.py:45
  162.3 35.2 %copy-start.7 = (bf16[512,1536]{1,0:T(8,128)(2,1)S(1)}, bf16[512,1536]{1,0:T(8,128)(2,1)}, u32[]{:S(2)}) copy-start(bf16[512,1536]{1,0:T(8,128)(2,1)} %param.11) | copy-start | bytes 4718596
  165.6 34.1 %copy-start.23 = (f32[1536]{0:T(1024)S(1)}, f32[1536]{0:T(1024)}, u32[]{:S(2)}) copy-start(f32[1536]{0:T(1024)} %param.17) | copy-start | bytes 18436
  200.0 35.8 %collective-permute-start.3 = (bf16[512,1536]{1,0:T(8,128)(2,1)S(1)}, bf16[512,1536]{1,0:T(8,128)(2,1)S(1)}, u32[]{:S(2)}, u32[]{:S(2)}) collective-permute-start(bf16[512,1536]{1,0:T(8,128)(2,1)S(1)} %multiply_convert_fusion.4), channel_id=1, source_target_pairs={{0,1},{1,0},{2,3},{3,2},{4,5},{5,4},{6,7},{7,6},{8,9},{9,8},{10,11... | collective-permute-start | bytes 4718600 | tf_op jit(solution)/shard_map/ppermute | solution.py:45
  238.2 11.9 %copy-start.20 = (bf16[512,1536]{1,0:T(8,128)(2,1)S(1)}, bf16[512,1536]{1,0:T(8,128)(2,1)}, u32[]{:S(2)}) copy-start(bf16[512,1536]{1,0:T(8,128)(2,1)} %get-tuple-element.101) | copy-start | bytes 4718596
  238.2 11.9 %copy-start.21 = (bf16[512,1536]{1,0:T(8,128)(2,1)S(1)}, bf16[512,1536]{1,0:T(8,128)(2,1)}, u32[]{:S(2)}) copy-start(bf16[512,1536]{1,0:T(8,128)(2,1)} %get-tuple-element.102) | copy-start | bytes 4718596
  289.7 344.4 %reduce-scatter.3.cloned.1.call-start = ((), (), s32[]{:S(2)}) async-start(), calls=%async_computation.4 | async-start | bytes 13369344 | tf_op jit(solution)/shard_map/reduce_scatter | solution.py:82
  302.3 34.9 %collective-permute-start.4 = (bf16[512,1536]{1,0:T(8,128)(2,1)}, bf16[512,1536]{1,0:T(8,128)(2,1)}, u32[]{:S(2)}, u32[]{:S(2)}) collective-permute-start(bf16[512,1536]{1,0:T(8,128)(2,1)} %fusion.56), channel_id=1, source_target_pairs={{0,1},{1,0},{2,3},{3,2},{4,5},{5,4},{6,7},{7,6},{8,9},{9,8},{10,11... | collective-permute-start | bytes 4718600 | tf_op jit(solution)/shard_map/ppermute | solution.py:45
  335.6 4.1 copy-start.10
  335.6 4.1 copy-start.27
  339.7 6.0 copy-start.32
  344.2 33.7 %collective-permute-start.5 = (bf16[512,1536]{1,0:T(8,128)(2,1)S(1)}, bf16[512,1536]{1,0:T(8,128)(2,1)S(1)}, u32[]{:S(2)}, u32[]{:S(2)}) collective-permute-start(bf16[512,1536]{1,0:T(8,128)(2,1)S(1)} %get-tuple-element.52), channel_id=1, source_target_pairs={{0,1},{1,0},{2,3},{3,2},{4,5},{5,4},{6,7},{7,6},{8,9},{9,8},{10,11... | collective-permute-start | bytes 4718600 | tf_op jit(solution)/shard_map/ppermute | solution.py:45
  380.2 51.4 %collective-permute-start.6 = (bf16[512,1536]{1,0:T(8,128)(2,1)}, bf16[512,1536]{1,0:T(8,128)(2,1)}, u32[]{:S(2)}, u32[]{:S(2)}) collective-permute-start(bf16[512,1536]{1,0:T(8,128)(2,1)} %fusion.48), channel_id=1, source_target_pairs={{0,1},{1,0},{2,3},{3,2},{4,5},{5,4},{6,7},{7,6},{8,9},{9,8},{10,11... | collective-permute-start | bytes 4718600 | tf_op jit(solution)/shard_map/ppermute | solution.py:45
  381.8 6.5 %copy-start.5 = (bf16[1024,768]{1,0:T(8,128)(2,1)S(1)}, bf16[1024,768]{1,0:T(8,128)(2,1)}, u32[]{:S(2)}) copy-start(bf16[1024,768]{1,0:T(8,128)(2,1)} %copy-done.4) | copy-start | bytes 4718596
  381.8 6.5 %copy-start.15 = (bf16[1024,1536]{1,0:T(8,128)(2,1)S(1)}, bf16[1024,1536]{1,0:T(8,128)(2,1)}, u32[]{:S(2)}) copy-start(bf16[1024,1536]{1,0:T(8,128)(2,1)} %pad_maximum_fusion.6) | copy-start | bytes 9437188
  392.7 38.8 %copy-start.17 = (bf16[1024,1536]{1,0:T(8,128)(2,1)S(1)}, bf16[1024,1536]{1,0:T(8,128)(2,1)}, u32[]{:S(2)}) copy-start(bf16[1024,1536]{1,0:T(8,128)(2,1)} %copy-done.16) | copy-start | bytes 9437188
  442.9 4.1 copy-start.12
  446.9 4.5 copy-start.18
  446.9 25.5 %collective-permute-start.7 = (bf16[4,2,96,2432]{3,2,1,0:T(8,128)(2,1)}, bf16[4,2,96,2432]{3,2,1,0:T(8,128)(2,1)}, u32[]{:S(2)}, u32[]{:S(2)}) collective-permute-start(bf16[4,2,96,2432]{3,2,1,0:T(8,128)(2,1)} %dynamic-slice_bitcast_fusion), channel_id=1, source_target_pairs={{0,2},{2,0},{4,6},{6,4},{8,10},{10,8},{12,14},{14,12},{16,18},{18,... | collective-permute-start | bytes 11206664 | tf_op jit(solution)/shard_map/ppermute | solution.py:87
  464.1 4.9 collective-permute-start.8
  469.0 10.3 %slice-start = ((s8[12189696]{0:T(1024)(128)(4,1)}), s8[4194304]{0:T(1024)(128)(4,1)S(1)}, s32[]{:S(2)}) async-start(s8[12189696]{0:T(1024)(128)(4,1)} %bitcast.90), calls=%async_computation.6 | async-start | bytes 8388608
  472.4 6.9 %slice-start.1 = ((s8[12189696]{0:T(1024)(128)(4,1)}), s8[4194304]{0:T(1024)(128)(4,1)S(1)}, s32[]{:S(2)}) async-start(s8[12189696]{0:T(1024)(128)(4,1)} %bitcast.90), calls=%async_computation.7 | async-start | bytes 8388608
  472.4 6.9 %slice-start.2 = ((s8[12189696]{0:T(1024)(128)(4,1)}), s8[3801088]{0:T(1024)(128)(4,1)S(1)}, s32[]{:S(2)}) async-start(s8[12189696]{0:T(1024)(128)(4,1)} %bitcast.90), calls=%async_computation.8 | async-start | bytes 7602176
  479.0 73.7 %collective-permute-start.9 = (bf16[4,96,2432]{2,1,0:T(8,128)(2,1)}, bf16[4,96,2432]{2,1,0:T(8,128)(2,1)}, u32[]{:S(2)}, u32[]{:S(2)}) collective-permute-start(bf16[4,96,2432]{2,1,0:T(8,128)(2,1)} %get-tuple-element.97), channel_id=1, source_target_pairs={{0,4},{2,6},{4,0},{6,2},{8,12},{10,14},{12,8},{14,10},{16,20},{18,... | collective-permute-start | bytes 5603336 | tf_op jit(solution)/shard_map/ppermute | solution.py:87
  487.4 7.3 %copy-start.14 = (f32[512,1536]{1,0:T(8,128)S(1)}, f32[512,1536]{1,0:T(8,128)}, u32[]{:S(2)}) copy-start(f32[512,1536]{1,0:T(8,128)} %fusion.20) | copy-start | bytes 9437188
  487.4 36.8 %collective-permute-start.13 = (bf16[512,1536]{1,0:T(8,128)(2,1)}, bf16[512,1536]{1,0:T(8,128)(2,1)}, u32[]{:S(2)}, u32[]{:S(2)}) collective-permute-start(bf16[512,1536]{1,0:T(8,128)(2,1)} %fusion.51), channel_id=1, source_target_pairs={{0,1},{1,0},{2,3},{3,2},{4,5},{5,4},{6,7},{7,6},{8,9},{9,8},{10,11... | collective-permute-start | bytes 4718600 | tf_op jit(solution)/shard_map/ppermute | solution.py:45
  490.2 47.0 %collective-permute-start.10 = (bf16[2,96,1536]{2,1,0:T(8,128)(2,1)}, bf16[2,96,1536]{2,1,0:T(8,128)(2,1)}, u32[]{:S(2)}, u32[]{:S(2)}) collective-permute-start(bf16[2,96,1536]{2,1,0:T(8,128)(2,1)} %get-tuple-element.109), channel_id=1, source_target_pairs={{0,8},{2,10},{4,12},{6,14},{8,0},{10,2},{12,4},{14,6},{16,24},{18,... | collective-permute-start | bytes 1769480 | tf_op jit(solution)/shard_map/ppermute | solution.py:87
  491.3 46.0 %collective-permute-start.11 = (bf16[2,96,1536]{2,1,0:T(8,128)(2,1)}, bf16[2,96,1536]{2,1,0:T(8,128)(2,1)}, u32[]{:S(2)}, u32[]{:S(2)}) collective-permute-start(bf16[2,96,1536]{2,1,0:T(8,128)(2,1)} %get-tuple-element.108), channel_id=1, source_target_pairs={{0,16},{2,18},{4,20},{6,22},{8,24},{10,26},{12,28},{14,30},{16,0},... | collective-permute-start | bytes 1769480 | tf_op jit(solution)/shard_map/ppermute | solution.py:87
  492.8 59.8 %copy-start.25 = (f32[1536]{0:T(1024)S(1)}, f32[1536]{0:T(1024)}, u32[]{:S(2)}) copy-start(f32[1536]{0:T(1024)} %param.12) | copy-start | bytes 18436
  492.8 59.8 %copy-start.29 = (f32[512]{0:T(512)S(1)}, f32[512]{0:T(512)}, u32[]{:S(2)}) copy-start(f32[512]{0:T(512)} %copy-done.28) | copy-start | bytes 6148
  492.8 59.8 %collective-permute-start.12 = (bf16[2,96,1536]{2,1,0:T(8,128)(2,1)}, bf16[2,96,1536]{2,1,0:T(8,128)(2,1)}, u32[]{:S(2)}, u32[]{:S(2)}) collective-permute-start(bf16[2,96,1536]{2,1,0:T(8,128)(2,1)} %get-tuple-element.107), channel_id=1, source_target_pairs={{0,24},{2,26},{4,28},{6,30},{8,16},{10,18},{12,20},{14,22},{16,8},... | collective-permute-start | bytes 1769480 | tf_op jit(solution)/shard_map/ppermute | solution.py:87
  552.7 10.7 %copy-start.13 = (bf16[4,96,2432]{2,1,0:T(8,128)(2,1)S(1)}, bf16[4,96,2432]{2,1,0:T(8,128)(2,1)}, u32[]{:S(2)}) copy-start(bf16[4,96,2432]{2,1,0:T(8,128)(2,1)} %get-tuple-element.67) | copy-start | bytes 5603332
  563.2 2.2 copy-start.19
  563.3 4.0 collective-permute-start.14
  565.4 61.5 %copy-start.8 = (bf16[512,1536]{1,0:T(8,128)(2,1)S(1)}, bf16[512,1536]{1,0:T(8,128)(2,1)}, u32[]{:S(2)}) copy-start(bf16[512,1536]{1,0:T(8,128)(2,1)} %param.11) | copy-start | bytes 4718596
  565.4 61.5 %copy-start.11 = (f32[512,1536]{1,0:T(8,128)S(1)}, f32[512,1536]{1,0:T(8,128)}, u32[]{:S(2)}) copy-start(f32[512,1536]{1,0:T(8,128)} %get-tuple-element.91) | copy-start | bytes 9437188
  567.3 16.4 %collective-permute-start.15 = (f32[25,128]{1,0:T(8,128)S(1)}, f32[25,128]{1,0:T(8,128)S(1)}, u32[]{:S(2)}, u32[]{:S(2)}) collective-permute-start(f32[25,128]{1,0:T(8,128)S(1)} %fusion.113), channel_id=1, source_target_pairs={{0,4},{2,6},{4,0},{6,2},{8,12},{10,14},{12,8},{14,10},{16,20},{18,... | collective-permute-start | bytes 38408 | tf_op jit(solution)/shard_map/ppermute | solution.py:87
  569.0 62.4 %collective-permute-start.19 = (bf16[96,2432]{1,0:T(8,128)(2,1)S(1)}, bf16[96,2432]{1,0:T(8,128)(2,1)S(1)}, u32[]{:S(2)}, u32[]{:S(2)}) collective-permute-start(bf16[96,2432]{1,0:T(8,128)(2,1)S(1)} %get-tuple-element.111), channel_id=1, source_target_pairs={{0,8},{2,10},{4,12},{6,14},{8,0},{10,2},{12,4},{14,6},{16,24},{18,... | collective-permute-start | bytes 1400840 | tf_op jit(solution)/shard_map/ppermute | solution.py:87
  581.3 50.1 %collective-permute-start.20 = (bf16[96,2432]{1,0:T(8,128)(2,1)S(1)}, bf16[96,2432]{1,0:T(8,128)(2,1)S(1)}, u32[]{:S(2)}, u32[]{:S(2)}) collective-permute-start(bf16[96,2432]{1,0:T(8,128)(2,1)S(1)} %get-tuple-element.113), channel_id=1, source_target_pairs={{0,16},{2,18},{4,20},{6,22},{8,24},{10,26},{12,28},{14,30},{16,0},... | collective-permute-start | bytes 1400840 | tf_op jit(solution)/shard_map/ppermute | solution.py:87
  581.3 50.1 %collective-permute-start.21 = (bf16[96,2432]{1,0:T(8,128)(2,1)S(1)}, bf16[96,2432]{1,0:T(8,128)(2,1)S(1)}, u32[]{:S(2)}, u32[]{:S(2)}) collective-permute-start(bf16[96,2432]{1,0:T(8,128)(2,1)S(1)} %get-tuple-element.112), channel_id=1, source_target_pairs={{0,24},{2,26},{4,28},{6,30},{8,16},{10,18},{12,20},{14,22},{16,8},... | collective-permute-start | bytes 1400840 | tf_op jit(solution)/shard_map/ppermute | solution.py:87
  583.7 28.2 %collective-permute-start.16 = (f32[25,128]{1,0:T(8,128)S(1)}, f32[25,128]{1,0:T(8,128)S(1)}, u32[]{:S(2)}, u32[]{:S(2)}) collective-permute-start(f32[25,128]{1,0:T(8,128)S(1)} %fusion.114), channel_id=1, source_target_pairs={{0,8},{2,10},{4,12},{6,14},{8,0},{10,2},{12,4},{14,6},{16,24},{18,... | collective-permute-start | bytes 38408 | tf_op jit(solution)/shard_map/ppermute | solution.py:87
  584.9 45.7 %collective-permute-start.22 = (bf16[96,1536]{1,0:T(8,128)(2,1)S(1)}, bf16[96,1536]{1,0:T(8,128)(2,1)S(1)}, u32[]{:S(2)}, u32[]{:S(2)}) collective-permute-start(bf16[96,1536]{1,0:T(8,128)(2,1)S(1)} %dynamic-slice_bitcast_fusion.11), channel_id=1, source_target_pairs={{0,4},{2,6},{4,0},{6,2},{8,12},{10,14},{12,8},{14,10},{16,20},{18,... | collective-permute-start | bytes 884744 | tf_op jit(solution)/shard_map/ppermute | solution.py:87
  612.0 13.5 %collective-permute-start.17 = (f32[25,128]{1,0:T(8,128)S(1)}, f32[25,128]{1,0:T(8,128)S(1)}, u32[]{:S(2)}, u32[]{:S(2)}) collective-permute-start(f32[25,128]{1,0:T(8,128)S(1)} %add.228), channel_id=1, source_target_pairs={{0,16},{2,18},{4,20},{6,22},{8,24},{10,26},{12,28},{14,30},{16,0},... | collective-permute-start | bytes 38408 | tf_op jit(solution)/shard_map/ppermute | solution.py:87
  625.4 4.0 collective-permute-start.18
Sparse Core Ops, SparseCore 0:
  13.7 100.7 all-gather.2
  116.7 97.1 all-gather.4
  289.8 83.4 reduce-scatter.4
  382.0 174.1 reduce-scatter.2

commit v5 on v4

--- a/solution.py
+++ b/solution.py
@@ -91,49 +91,40 @@
     return lax.dynamic_index_in_dim(array, index, axis, keepdims=False)
 
 
-def scatter_links(first, second, beside):
+def over_core(grad):
     size = lax.axis_size("dp")
-    if size % 4 or size & (size - 1):
-        return (scatter_dp(first).astype(F32), scatter_dp(second).astype(F32), beside)
-    layers = size // 4
-    index = lax.axis_index("dp")
-    core, side, layer = (index % 2, index // 2 % 2, index // 4)
-
-    def over_core(grad):
-        grad = grad.reshape(layers, 2, 2, grad.shape[0] // size, grad.shape[1])
-        arrived = trade(take(grad, 2, 1 - core), "dp", 1)
-        return (take(grad, 2, core).astype(F32) + arrived.astype(F32)).astype(BF16)
-
-    def side_pieces(grad, axis):
-        return [take(grad, axis, side), trade(take(grad, axis, 1 - side), "dp", 2)]
-
-    def layer_pieces(grad):
-        sent = [trade(take(grad, 0, layer ^ k), "dp", 4 * k) for k in range(1, layers)]
-        return [take(grad, 0, layer), *sent]
-
-    def total(pieces):
-        result = pieces[0].astype(F32)
-        for piece in pieces[1:]:
-            result = result + piece.astype(F32)
-        return result
-
-    first, second = hold(over_core(first), over_core(second))
-    first, second, beside = hold(side_pieces(first, 1), layer_pieces(second), beside)
-    first, second = hold(total(first).astype(BF16), total(second).astype(BF16))
-    return (total(layer_pieces(first)), total(side_pieces(second, 0)), beside)
-
-
-def sum_all(value):
-    for axis in ("dp", "tensor"):
-        size = lax.axis_size(axis)
-        if size & (size - 1):
-            value = lax.psum(value, axis)
-            continue
-        step = 1
-        while step < size:
-            value = value + trade(value, axis, step)
-            step *= 2
+    core = lax.axis_index("dp") % 2
+    grad = grad.reshape(size // 4, 2, 2, grad.shape[0] // size, grad.shape[1])
+    arrived = trade(take(grad, 2, 1 - core), "dp", 1)
+    return (take(grad, 2, core).astype(F32) + arrived.astype(F32)).astype(BF16)
+
+
+def side_pieces(grad, axis):
+    side = lax.axis_index("dp") // 2 % 2
+    return [take(grad, axis, side), trade(take(grad, axis, 1 - side), "dp", 2)]
+
+
+def layer_pieces(grad):
+    layer = lax.axis_index("dp") // 4
+    sent = [trade(take(grad, 0, layer ^ k), "dp", 4 * k) for k in range(1, grad.shape[0])]
+    return [take(grad, 0, layer), *sent]
+
+
+def total(pieces):
+    result = pieces[0].astype(F32)
+    for piece in pieces[1:]:
+        result = result + piece.astype(F32)
+    return result
+
+
+def add_traded(value, axis, masks):
+    for mask in masks:
+        value = value + trade(value, axis, mask)
     return value
+
+
+def masks_of(size):
+    return [1 << k for k in range(size.bit_length() - 1)]
 
 
 def head_span(lane, head):
@@ -448,7 +439,6 @@
 ):
     own_rows, width = layer_input.shape
     group_seqs = lengths.shape[0]
-    group_rows = group_seqs * SLOTS
     part = w_attn.shape[2]
     heads_dev = part // HEAD
     units = w_mlp.shape[2]
@@ -498,6 +488,7 @@
     scaled_mlp, inverse_mlp = norm_parts(middle)
     normed_mid = share_rows((scaled_mlp * gain_mlp).astype(BF16))
     grad_hidden = dot_nn(grad_final_all, down_full)
+    normed_mid, grad_hidden = hold(normed_mid, grad_hidden)
     gate_pre = dot_nn(normed_mid, mlp_full[:, :units])
     up_pre = dot_nn(normed_mid, mlp_full[:, units:])
     gate_s = jax.nn.sigmoid(gate_pre)
@@ -536,42 +527,62 @@
     grad_proj, arrived_out = hold(grad_proj, arrived_out)
     layer_output = (valid * (middle + (staying + arrived_out.astype(F32)))).astype(BF16)
     bias_part = jnp.sum(bias_sums.reshape(group_seqs, 8, PAD)[:, 0, :heads_dev], axis=0)
+
     def attn_back_term(first_row, row_count):
         return dot_nt(lax.dynamic_slice_in_dim(grad_proj, first_row, row_count), attn_full)
 
-    leaving, staying = term_parts(attn_back_term, own_rows)
-    arrived_back = cross(leaving)
-    main_grad = dot_tn(normed_all, grad_proj[:, : 3 * part + PAD]).astype(BF16)
-    rest_grad = jnp.concatenate(
-        [
-            dot_tn(normed_all, grad_proj[:, 3 * part + PAD :]).astype(BF16),
-            dot_tn(grad_branch_all, gated).astype(BF16),
-        ],
-        axis=1,
-    )
-    main_part, rest_part, arrived_back = scatter_links(main_grad, rest_grad, arrived_back)
-    grad_normed_attn = staying + arrived_back.astype(F32)
-    gain_attn_part = jnp.sum(scaled_attn * grad_normed_attn, axis=0)
-    grad_input = grad_middle + norm_back(grad_normed_attn, scaled_attn, inverse_attn, gain_attn)
     bias_full = lax.dynamic_update_slice_in_dim(
         jnp.zeros(forget_bias.shape, F32), bias_part, tensor_index * heads_dev, 0
     )
     heads = forget_bias.shape[0]
-    sums = sum_all(
-        jnp.concatenate(
-            [gain_attn_part, gain_mlp_part, jnp.pad(bias_full, (0, -heads % 128))]
-        ).reshape(-1, 128)
-    ).reshape(-1)
+
+    def finish(arrived):
+        grad_normed_attn = staying + arrived.astype(F32)
+        grad_input = grad_middle + norm_back(grad_normed_attn, scaled_attn, inverse_attn, gain_attn)
+        terms = [jnp.sum(scaled_attn * grad_normed_attn, axis=0), gain_mlp_part]
+        terms.append(jnp.pad(bias_full, (0, -heads % 128)))
+        return grad_input, jnp.concatenate(terms).reshape(-1, 128)
+
+    leaving, staying = term_parts(attn_back_term, own_rows)
+    leaving, grad_later = hold(leaving, grad_proj)
+    arrived_back = cross(leaving)
+    main_grad = dot_tn(normed_all, grad_later[:, : 3 * part + PAD]).astype(BF16)
+    gate_grad = dot_tn(normed_all, grad_later[:, 3 * part + PAD :]).astype(BF16)
+    size = lax.axis_size("dp")
+    tensor_size = lax.axis_size("tensor")
+    if size % 4 or size & (size - 1) or tensor_size & (tensor_size - 1):
+        main_part, gate_part = (scatter_dp(main_grad).astype(F32), scatter_dp(gate_grad).astype(F32))
+        out_part = scatter_dp(dot_tn(grad_branch_all, gated).astype(BF16))
+        grad_input, sums = finish(arrived_back)
+        sums = lax.psum(sums, ("dp", "tensor"))
+    else:
+        out_grad = dot_tn(grad_branch_all, gated).astype(BF16)
+        main_half, gate_half, out_half, arrived_back = hold(
+            over_core(main_grad), over_core(gate_grad), over_core(out_grad), arrived_back
+        )
+        rest_half = jnp.concatenate([gate_half, out_half], axis=-1)
+        grad_input, sums = finish(arrived_back)
+        sums = add_traded(sums, "dp", [1])
+        sums = add_traded(sums, "tensor", masks_of(tensor_size))
+        main_half, rest_half, sums = hold(side_pieces(main_half, 1), layer_pieces(rest_half), sums)
+        sums = add_traded(sums, "dp", masks_of(size)[2:])
+        main_half, rest_half, sums = hold(
+            total(main_half).astype(BF16), total(rest_half).astype(BF16), sums
+        )
+        main_part, rest_part = (total(layer_pieces(main_half)), total(side_pieces(rest_half, 0)))
+        gate_part, out_part = (rest_part[:, :part], rest_part[:, part:])
+        sums = add_traded(sums, "dp", [2])
+    sums = sums.reshape(-1)
     return (
         layer_output,
         grad_input,
         sums[:width],
-        jnp.concatenate([main_part[:, : 3 * part], rest_part[:, :part]], axis=1).reshape(
+        jnp.concatenate([main_part[:, : 3 * part], gate_part], axis=1).reshape(
             own_d, 4, part
         ),
         main_part[:, 3 * part : 3 * part + heads_dev],
         sums[2 * width : 2 * width + heads],
-        rest_part[:, part:].T,
+        out_part.astype(F32).T,
         sums[width : 2 * width],
         mlp_part.astype(F32).reshape(own_d, 2, units),
         down_part.astype(F32).T,
@@ -592,6 +603,7 @@
         P("dp"),
         P(("dp", "tensor"), None),
     )
+
     return jax.shard_map(
         on_device,
         mesh=mesh,

time: 650 us -> 639 us (0.983)
    concatenate x1, local copies, waits for them, and re-layouts: 6.77 us -> 0.08 us  [on_device(): rest_half = jnp.concatenate([gate_half, out_half], axis=-1)]
    ppermute x15 -> x16, starting transfers between devices: 27.1 us -> 22.1 us  [trade(): return lax.ppermute(value, axis, [(i, i ^ mask) for i in range(size)])]
    ppermute x15 -> x16, waiting for transfers between devices: 70.5 us -> 67.2 us  [trade(): return lax.ppermute(value, axis, [(i, i ^ mask) for i in range(size)])]
  transfers between devices with their start and end apart: 27 -> 28, of which waited for: 13 -> 16; matrix products, arithmetic and copies ran while one was open for 31% -> 30% of each run, Pallas kernels for 10% -> 10%
where the time goes in v5:
time: 639 us; the launch traced here: 631 us
  waiting for transfers between devices  265 us (41%)
  matrix products  180 us (28%)
  Pallas kernels  63.8 us (10%)
  other arithmetic  46.7 us (7%)
  starting transfers between devices  33.3 us (5%)
  local copies, waits for them, and re-layouts  26.3 us (4%)
  between operations  15.3 us (2%)
    ppermute x8, waiting for transfers between devices, swap(): return lax.ppermute(rows, 'tensor', [(0, 1), (1, 0)])  175 us
    dot_general x8, matrix products, dot_nt(): lax.dot_general(a, b, (((1,), (1,)), ((), ())), preferred_element_type=F32)  67.4 us
    ppermute x16, waiting for transfers between devices, trade(): return lax.ppermute(value, axis, [(i, i ^ mask) for i in range(size)])  67.2 us
    dot_general x6, matrix products, dot_nn(): lax.dot_general(a, b, (((1,), (0,)), ((), ())), preferred_element_type=F32)  64.7 us
    dot_general x5, matrix products, dot_tn(): lax.dot_general(a, b, (((0,), (0,)), ((), ())), preferred_element_type=F32)  48.2 us
    pallas_call x1, Pallas kernels, attend_back(): pl.pallas_call(functools.partial(attend_back_body, per_group=per_group, g...  38.8 us
    pallas_call x1, Pallas kernels, attend(): pl.pallas_call(functools.partial(attend_body, per_group=per_group), out_s...  25 us
    all_gather x2, waiting for transfers between devices, gather_dp(): return lax.all_gather(shard, 'dp', axis=0, tiled=True)  23.1 us
  transfers between devices with their start and end apart: 28, of which 16 were waited for; matrix products, arithmetic and copies ran while one was open for 30% of the time, Pallas kernels for 10%

profile of v5, /device:TPU:0, one launch (start us, length us, event | category | flops | bytes accessed | tf_op | source)
XLA Modules:
  0.0 631.0 jit_solution(9951027868307380831)
XLA Ops:
  8.7 1.9 copy.39
  11.6 2.0 fusion.83
  15.8 3.0 collective-permute-start.1
  19.2 1.6 fusion.39
  23.3 31.1 %collective-permute-done.1 = bf16[512,1536]{1,0:T(8,128)(2,1)} collective-permute-done((bf16[512,1536]{1,0:T(8,128)(2,1)}, bf16[512,1536]{1,0:T(8,128)(2,1)}, u32[]{:S(2)}, u32[]{:S(2)}) %collective-permute-start.1) | collective-permute-done | bytes 1572896 | tf_op jit(solution)/shard_map/ppermute | solution.py:45
  54.4 2.1 broadcast_select_fusion.5
  56.5 30.7 %collective-permute-done = bf16[512,1536]{1,0:T(8,128)(2,1)} collective-permute-done((bf16[512,1536]{1,0:T(8,128)(2,1)}, bf16[512,1536]{1,0:T(8,128)(2,1)}, u32[]{:S(2)}, u32[]{:S(2)}) %collective-permute-start) | collective-permute-done | bytes 1572896 | tf_op jit(solution)/shard_map/ppermute | solution.py:45
  87.2 2.2 broadcast_select_fusion.7
  89.5 1.9 pad_maximum_fusion.2
  91.4 23.1 %all-gather.3.cloned.1.call-done = bf16[1536,3968]{1,0:T(8,128)(2,1)} async-done(((bf16[96,3968]{1,0:T(8,128)(2,1)}), bf16[1536,3968]{1,0:T(8,128)(2,1)}) %all-gather.3.cloned.1.call-update) | async-done | bytes 12189712 | tf_op jit(solution)/shard_map/all_gather | solution.py:78
  114.7 7.2 %fusion.60.gate_ref.logit_ref = f32[1024,896]{1,0:T(8,128)} fusion(bf16[1024,1536]{1,0:T(8,128)(2,1)S(1)} %get-tuple-element.50, bf16[1536,3968]{1,0:T(8,128)(2,1)} %all-gather.3.cloned.1.call-done), kind=kOutput, calls=%fused_computation.77 | convolution fusion | flops 2818572288 | bytes 9568256 | tf_op jit(solution)/shard_map/dot_general | solution.py:33
  121.9 9.5 %fusion.16.q_ref.k_ref.v_ref = bf16[1024,2304]{1,0:T(8,128)(2,1)} fusion(bf16[1024,1536]{1,0:T(8,128)(2,1)S(1)} %get-tuple-element.50, bf16[1536,3968]{1,0:T(8,128)(2,1)S(1)} %copy-done.30), kind=kOutput, calls=%fused_computation.29 | convolution fusion | flops 7250116608 | bytes 14942208 | tf_op jit(solution)/shard_map/dot_general | solution.py:33
  131.4 25.0 %attend.1 = (bf16[1024,768]{1,0:T(8,128)(2,1)S(1)}, bf16[1024,768]{1,0:T(8,128)(2,1)S(1)}, f32[128,1024]{1,0:T(8,128)S(1)}, f32[1024,128]{1,0:T(8,128)S(1)}) custom-call(s32[1]{0:T(128)} %copy.45.lengths, bf16[1024,2304]{1,0:T(8,128)(2,1)} %fusion.16.q_ref.k_ref.v_ref, bf16[1024,2304]{1,0:T(8,128)(2,1)} %fusion.16.q_ref.k_ref.v_ref, ...), custom_call_target="tpu_custom_call" | custom-call | tf_op jit(solution)/shard_map/attend/pallas_call | solution.py:374
  156.5 4.6 convolution_convert_fusion.5
  162.6 3.2 fusion.68
  165.9 31.9 %collective-permute-done.2 = bf16[512,1536]{1,0:T(8,128)(2,1)} collective-permute-done((bf16[512,1536]{1,0:T(8,128)(2,1)S(1)}, bf16[512,1536]{1,0:T(8,128)(2,1)}, u32[]{:S(2)}, u32[]{:S(2)}) %collective-permute-start.2) | collective-permute-done | bytes 1572896 | tf_op jit(solution)/shard_map/ppermute | solution.py:45
  197.8 2.2 multiply_reduce_fusion.2
  201.8 34.2 %collective-permute-done.3 = bf16[512,1536]{1,0:T(8,128)(2,1)S(1)} collective-permute-done((bf16[512,1536]{1,0:T(8,128)(2,1)S(1)}, bf16[512,1536]{1,0:T(8,128)(2,1)S(1)}, u32[]{:S(2)}, u32[]{:S(2)}) %collective-permute-start.3) | collective-permute-done | bytes 1572896 | tf_op jit(solution)/shard_map/ppermute | solution.py:45
  236.8 1.9 pad_maximum_fusion.4
  238.7 11.9 %fusion.24 = f32[1024,2048]{1,0:T(8,128)} fusion(bf16[1024,1536]{1,0:T(8,128)(2,1)} %get-tuple-element.55, bf16[1536,6144]{1,0:T(8,128)(2,1)} %all-gather.5.cloned.1.call-done), kind=kOutput, calls=%fused_computation.35 | convolution fusion | flops 6442450944 | bytes 17825792 | tf_op jit(solution)/shard_map/dot_general | solution.py:33
  250.6 10.9 %fusion.12 = f32[1024,2048]{1,0:T(8,128)} fusion(bf16[1024,1536]{1,0:T(8,128)(2,1)S(1)} %copy-done.15, bf16[1536,6144]{1,0:T(8,128)(2,1)} %all-gather.5.cloned.1.call-done), kind=kOutput, calls=%fused_computation.25 | convolution fusion | flops 6442450944 | bytes 17825792 | tf_op jit(solution)/shard_map/dot_general | solution.py:33
  261.5 18.0 %multiply_convert_fusion = (bf16[1024,2048]{1,0:T(8,128)(2,1)}, bf16[1024,2048]{1,0:T(8,128)(2,1)}, bf16[1024,2048]{1,0:T(8,128)(2,1)}) fusion(f32[1024,2048]{1,0:T(8,128)} %fusion.12, f32[1024,2048]{1,0:T(8,128)} %fusion.24, bf16[1024,1536]{1,0:T(8,128)(2,1)S(1)} %copy-done.15, bf16[1536,6144]{1,0:T(8,128)(2,1)} %all-gather.5.cloned.1.call-done), kind=kOutput, calls=%fused_computation.15 | convolution fusion | flops 6473908224 | bytes 38797312 | tf_op jit(solution)/shard_map/dot_general | solution.py:33
  279.5 10.9 %convolution_convert_fusion.2 = bf16[1536,2048]{1,0:T(8,128)(2,1)} fusion(bf16[1024,1536]{1,0:T(8,128)(2,1)S(1)} %copy-done.19, bf16[1024,2048]{1,0:T(8,128)(2,1)} %get-tuple-element.62), kind=kOutput, calls=%fused_computation.20 | convolution fusion | flops 6445596672 | bytes 13631488 | tf_op jit(solution)/shard_map/dot_general | solution.py:41
  290.5 12.4 %fusion.55 = bf16[512,1536]{1,0:T(8,128)(2,1)} fusion(bf16[1536,6144]{1,0:T(8,128)(2,1)} %all-gather.5.cloned.1.call-done, s32[]{:T(128)S(6)} %select_n.159, bf16[1024,2048]{1,0:T(8,128)(2,1)} %get-tuple-element.109, bf16[1024,2048]{1,0:T(8,128)(2,1)} %get-tuple-element.110), kind=kOutput, calls=%fused_computation.76 | convolution fusion | flops 6451625984 | bytes 22544388 | tf_op jit(solution)/shard_map/dot_general | solution.py:37
  304.2 19.8 %convolution_convert_fusion = bf16[1536,4096]{1,0:T(8,128)(2,1)} fusion(bf16[1024,1536]{1,0:T(8,128)(2,1)S(1)} %copy-done.16, bf16[1024,2048]{1,0:T(8,128)(2,1)} %get-tuple-element.110, bf16[1024,2048]{1,0:T(8,128)(2,1)} %get-tuple-element.109), kind=kOutput, calls=%fused_computation | convolution fusion | flops 12907970560 | bytes 24117248 | tf_op jit(solution)/shard_map/dot_general | solution.py:41
  324.0 11.4 %fusion = f32[512,1536]{1,0:T(8,128)S(1)} fusion(bf16[1536,6144]{1,0:T(8,128)(2,1)} %all-gather.5.cloned.1.call-done, s32[]{:T(128)S(6)} %select_n.160, bf16[1024,2048]{1,0:T(8,128)(2,1)} %get-tuple-element.109, bf16[1024,2048]{1,0:T(8,128)(2,1)} %get-tuple-element.110), kind=kOutput, calls=%fused_computation.2 | convolution fusion | flops 6450839552 | bytes 24117252 | tf_op jit(solution)/shard_map/dot_general | solution.py:37
  335.4 2.4 collective-permute-done.4
  337.8 2.5 multiply_reduce_fusion
  340.3 5.0 fusion.101
  346.8 8.7 %fusion.20 = f32[512,1536]{1,0:T(8,128)} fusion(bf16[1536,6144]{1,0:T(8,128)(2,1)} %all-gather.5.cloned.1.call-done, bf16[1024,2048]{1,0:T(8,128)(2,1)} %get-tuple-element.62, s32[]{:T(128)S(6)} %select_n.160), kind=kOutput, calls=%fused_computation.31 | convolution fusion | flops 3221225472 | bytes 11534340 | tf_op jit(solution)/shard_map/dot_general | solution.py:37
  355.5 7.8 %fusion.47 = bf16[512,1536]{1,0:T(8,128)(2,1)} fusion(bf16[1536,6144]{1,0:T(8,128)(2,1)} %all-gather.5.cloned.1.call-done, bf16[1024,2048]{1,0:T(8,128)(2,1)S(1)} %copy-done.34, s32[]{:T(128)S(6)} %select_n.159), kind=kOutput, calls=%fused_computation.73 | convolution fusion | flops 3222011904 | bytes 9961476 | tf_op jit(solution)/shard_map/dot_general | solution.py:37
  363.4 15.8 %collective-permute-done.5 = bf16[512,1536]{1,0:T(8,128)(2,1)} collective-permute-done((bf16[512,1536]{1,0:T(8,128)(2,1)}, bf16[512,1536]{1,0:T(8,128)(2,1)}, u32[]{:S(2)}, u32[]{:S(2)}) %collective-permute-start.5) | collective-permute-done | bytes 1572896 | tf_op jit(solution)/shard_map/ppermute | solution.py:45
  379.2 2.1 broadcast_select_fusion.1
  381.3 1.9 pad_maximum_fusion.5
  383.2 1.7 collective-permute-start.6
  384.9 7.2 %fusion.71.grad_ref = bf16[1024,768]{1,0:T(8,128)(2,1)} fusion(bf16[1024,1536]{1,0:T(8,128)(2,1)} %pad_maximum_fusion.5, bf16[1536,3968]{1,0:T(8,128)(2,1)} %all-gather.3.cloned.1.call-done), kind=kOutput, calls=%fused_computation.94 | convolution fusion | flops 2416705536 | bytes 7077888 | tf_op jit(solution)/shard_map/dot_general | solution.py:33
  392.1 38.8 %attend_back.1 = (bf16[1024,3200]{1,0:T(8,128)(2,1)}, f32[8,128]{1,0:T(8,128)}) custom-call(bf16[1024,2304]{1,0:T(8,128)(2,1)} %fusion.16.q_ref.k_ref.v_ref, bf16[1024,2304]{1,0:T(8,128)(2,1)} %fusion.16.q_ref.k_ref.v_ref, bf16[1024,2304]{1,0:T(8,128)(2,1)} %fusion.16.q_ref.k_ref.v_ref, f32[1024,896]{1,0:T(8,128)} %fusion.60.gate_ref.logit_ref, ...), custom_call_target="tpu_custom_call" | custom-call | tf_op jit(solution)/shard_map/attend_back/pallas_call | solution.py:401
  430.9 10.2 %fusion.50 = bf16[512,1536]{1,0:T(8,128)(2,1)} fusion(bf16[1536,3968]{1,0:T(8,128)(2,1)} %all-gather.3.cloned.1.call-done, bf16[1024,3200]{1,0:T(8,128)(2,1)} %get-tuple-element.72, s32[]{:T(128)S(6)} %select_n.159), kind=kOutput, calls=%fused_computation.74 | convolution fusion | flops 5033951232 | bytes 14680068 | tf_op jit(solution)/shard_map/dot_general | solution.py:37
  441.1 9.0 %convolution_convert_fusion.1 = bf16[1536,2432]{1,0:T(8,128)(2,1)S(1)} fusion(bf16[1024,1536]{1,0:T(8,128)(2,1)S(1)} %copy-done.18, bf16[1024,3200]{1,0:T(8,128)(2,1)S(1)} %copy-done.31), kind=kOutput, calls=%fused_computation.1 | convolution fusion | flops 7654146048 | bytes 15597568 | tf_op jit(solution)/shard_map/dot_general | solution.py:41
  450.1 2.2 dynamic-slice_bitcast_fusion
  452.3 3.1 copy-done.12
  456.0 3.2 convolution_convert_fusion.3
  461.7 5.4 convolution_convert_fusion.4
  468.7 1.7 fusion.62
  470.9 3.4 multiply_convert_fusion.3
  474.7 3.5 fusion.9
  478.2 28.8 %collective-permute-done.10 = bf16[512,1536]{1,0:T(8,128)(2,1)} collective-permute-done((bf16[512,1536]{1,0:T(8,128)(2,1)S(1)}, bf16[512,1536]{1,0:T(8,128)(2,1)}, u32[]{:S(2)}, u32[]{:S(2)}) %collective-permute-start.10) | collective-permute-done | bytes 1572896 | tf_op jit(solution)/shard_map/ppermute | solution.py:45
  507.0 9.0 %fusion.44 = (f32[1536]{0:T(1024)S(1)}, f32[512]{0:T(512)S(1)}, f32[512,1536]{1,0:T(8,128)S(1)}) fusion(bf16[512,1536]{1,0:T(8,128)(2,1)S(1)} %copy-done.8, f32[512]{0:T(512)S(1)} %copy-done.29, f32[1536]{0:T(1024)S(1)} %copy-done.25, bf16[512,1536]{1,0:T(8,128)(2,1)} %collective-permute-done.10, bf16[1536,3968]{1,0:T(8,128)(2,1)} %all-gather.3.cloned.1.call-done, ...), kind=kOutput, calls=%fused_computation.58 | convolution fusion | flops 5040240640 | bytes 19417092 | tf_op jit(solution)/shard_map/dot_general | solution.py:37
  517.7 2.3 collective-permute-start.13
  520.0 1.9 collective-permute-start.14
  521.9 1.7 dynamic-slice_bitcast_fusion.1
  524.6 2.5 fusion.43
  528.1 1.9 convert_bitcast_fusion
  530.0 15.7 %collective-permute-done.12 = bf16[2,96,1536]{2,1,0:T(8,128)(2,1)S(1)} collective-permute-done((bf16[2,96,1536]{2,1,0:T(8,128)(2,1)}, bf16[2,96,1536]{2,1,0:T(8,128)(2,1)S(1)}, u32[]{:S(2)}, u32[]{:S(2)}) %collective-permute-start.12) | collective-permute-done | bytes 589856 | tf_op jit(solution)/shard_map/ppermute | solution.py:87
  545.8 14.7 %collective-permute-done.13 = bf16[2,96,1536]{2,1,0:T(8,128)(2,1)} collective-permute-done((bf16[2,96,1536]{2,1,0:T(8,128)(2,1)}, bf16[2,96,1536]{2,1,0:T(8,128)(2,1)}, u32[]{:S(2)}, u32[]{:S(2)}) %collective-permute-start.13) | collective-permute-done | bytes 589856 | tf_op jit(solution)/shard_map/ppermute | solution.py:87
  560.5 5.8 collective-permute-done.11
  566.2 6.8 %collective-permute-start.17 = (f32[25,128]{1,0:T(8,128)S(1)}, f32[25,128]{1,0:T(8,128)S(1)}, u32[]{:S(2)}, u32[]{:S(2)}) collective-permute-start(f32[25,128]{1,0:T(8,128)S(1)} %fusion.116), channel_id=1, source_target_pairs={{0,8},{2,10},{4,12},{6,14},{8,0},{10,2},{12,4},{14,6},{16,24},{18,... | collective-permute-start | bytes 38408 | tf_op jit(solution)/shard_map/ppermute | solution.py:87
  573.0 1.9 add_convert_fusion
  575.0 2.9 collective-permute-start.18
  582.0 1.8 collective-permute-start.20
  589.0 11.4 %collective-permute-done.20 = bf16[96,2432]{1,0:T(8,128)(2,1)S(1)} collective-permute-done((bf16[96,2432]{1,0:T(8,128)(2,1)S(1)}, bf16[96,2432]{1,0:T(8,128)(2,1)S(1)}, u32[]{:S(2)}, u32[]{:S(2)}) %collective-permute-start.20) | collective-permute-done | bytes 466976 | tf_op jit(solution)/shard_map/ppermute | solution.py:87
  600.4 17.8 %collective-permute-done.21 = bf16[96,2432]{1,0:T(8,128)(2,1)S(1)} collective-permute-done((bf16[96,2432]{1,0:T(8,128)(2,1)S(1)}, bf16[96,2432]{1,0:T(8,128)(2,1)S(1)}, u32[]{:S(2)}, u32[]{:S(2)}) %collective-permute-start.21) | collective-permute-done | bytes 466976 | tf_op jit(solution)/shard_map/ppermute | solution.py:87
  618.7 1.6 reshape.142
  620.9 3.3 reshape.152
  (162 shorter events, 33.7 us)
Async XLA Ops:
  7.2 7.2 %copy-start.9 = (bf16[512,1536]{1,0:T(8,128)(2,1)S(1)}, bf16[512,1536]{1,0:T(8,128)(2,1)}, u32[]{:S(2)}) copy-start(bf16[512,1536]{1,0:T(8,128)(2,1)} %param.21) | copy-start | bytes 4718596
  7.2 107.3 %all-gather.3.cloned.1.call-start = ((), (), s32[]{:S(2)}) async-start(), calls=%async_computation.2 | async-start | bytes 12951552 | tf_op jit(solution)/shard_map/all_gather | solution.py:78
  10.6 8.2 %copy-start.6 = (bf16[512,1536]{1,0:T(8,128)(2,1)S(1)}, bf16[512,1536]{1,0:T(8,128)(2,1)}, u32[]{:S(2)}) copy-start(bf16[512,1536]{1,0:T(8,128)(2,1)} %param.11) | copy-start | bytes 4718596
  11.6 7.7 %copy-start.24 = (f32[1536]{0:T(1024)S(1)}, f32[1536]{0:T(1024)}, u32[]{:S(2)}) copy-start(f32[1536]{0:T(1024)} %param.12) | copy-start | bytes 18436
  13.6 225.1 %all-gather.5.cloned.1.call-start = ((), (), s32[]{:S(2)}) async-start(), calls=%async_computation.3 | async-start | bytes 20054016 | tf_op jit(solution)/shard_map/all_gather | solution.py:78
  14.4 40.0 %copy-start.26 = (f32[512]{0:T(512)}, f32[512]{0:T(512)S(1)}, u32[]{:S(2)}) copy-start(f32[512]{0:T(512)S(1)} %fusion.97) | copy-start | bytes 6148
  15.8 6.4 %copy-start.22 = (bf16[2048,96]{0,1:T(8,128)(2,1)S(1)}, bf16[2048,96]{0,1:T(8,128)(2,1)}, u32[]{:S(2)}) copy-start(bf16[2048,96]{0,1:T(8,128)(2,1)} %param.19) | copy-start | bytes 1179652
  15.8 38.6 %collective-permute-start.1 = (bf16[512,1536]{1,0:T(8,128)(2,1)}, bf16[512,1536]{1,0:T(8,128)(2,1)}, u32[]{:S(2)}, u32[]{:S(2)}) collective-permute-start(bf16[512,1536]{1,0:T(8,128)(2,1)} %fusion.46), channel_id=1, source_target_pairs={{0,1},{1,0},{2,3},{3,2},{4,5},{5,4},{6,7},{7,6},{8,9},{9,8},{10,11... | collective-permute-start | bytes 4718600 | tf_op jit(solution)/shard_map/ppermute | solution.py:45
  19.2 68.0 %copy-start.28 = (f32[512]{0:T(512)}, f32[512]{0:T(512)S(1)}, u32[]{:S(2)}) copy-start(f32[512]{0:T(512)S(1)} %add_rsqrt_fusion.1) | copy-start | bytes 6148
  20.8 66.4 %collective-permute-start = (bf16[512,1536]{1,0:T(8,128)(2,1)}, bf16[512,1536]{1,0:T(8,128)(2,1)}, u32[]{:S(2)}, u32[]{:S(2)}) collective-permute-start(bf16[512,1536]{1,0:T(8,128)(2,1)} %fusion.39), channel_id=1, source_target_pairs={{0,1},{1,0},{2,3},{3,2},{4,5},{5,4},{6,7},{7,6},{8,9},{9,8},{10,11... | collective-permute-start | bytes 4718600 | tf_op jit(solution)/shard_map/ppermute | solution.py:45
  89.5 25.1 %copy-start.33 = (f32[24]{0:T(128)S(1)}, f32[24]{0:T(128)}, u32[]{:S(2)}) copy-start(f32[24]{0:T(128)} %param.15) | copy-start | bytes 292
  91.4 30.5 %copy-start.17 = (bf16[1024,1536]{1,0:T(8,128)(2,1)}, bf16[1024,1536]{1,0:T(8,128)(2,1)S(1)}, u32[]{:S(2)}) copy-start(bf16[1024,1536]{1,0:T(8,128)(2,1)S(1)} %get-tuple-element.50) | copy-start | bytes 9437188
  114.5 413.6 %reduce-scatter.5.cloned.1.call-start = ((), (), s32[]{:S(2)}) async-start(), calls=%async_computation.5 | async-start | bytes 6684672 | tf_op jit(solution)/shard_map/reduce_scatter | solution.py:82
  114.7 7.2 %copy-start.30 = (bf16[1536,3968]{1,0:T(8,128)(2,1)S(1)}, bf16[1536,3968]{1,0:T(8,128)(2,1)}, u32[]{:S(2)}) copy-start(bf16[1536,3968]{1,0:T(8,128)(2,1)} %all-gather.3.cloned.1.call-done) | copy-start | bytes 36569092
  131.4 25.0 %copy-start.3 = (f32[8,128]{1,0:T(8,128)}, f32[8,128]{1,0:T(8,128)S(1)}, u32[]{:S(2)}) copy-start(f32[8,128]{1,0:T(8,128)S(1)} %broadcast_in_dim.16.bias_ref) | copy-start | bytes 12292
  156.4 4.6 copy-start
  156.4 4.6 copy-start.1
  156.4 4.6 copy-start.2
  156.4 6.2 copy-start.4
  161.1 36.7 %collective-permute-start.2 = (bf16[512,1536]{1,0:T(8,128)(2,1)S(1)}, bf16[512,1536]{1,0:T(8,128)(2,1)}, u32[]{:S(2)}, u32[]{:S(2)}) collective-permute-start(bf16[512,1536]{1,0:T(8,128)(2,1)S(1)} %convolution_convert_fusion.5), channel_id=1, source_target_pairs={{0,1},{1,0},{2,3},{3,2},{4,5},{5,4},{6,7},{7,6},{8,9},{9,8},{10,11... | collective-permute-start | bytes 4718600 | tf_op jit(solution)/shard_map/ppermute | solution.py:45
  162.6 35.2 %copy-start.7 = (bf16[512,1536]{1,0:T(8,128)(2,1)S(1)}, bf16[512,1536]{1,0:T(8,128)(2,1)}, u32[]{:S(2)}) copy-start(bf16[512,1536]{1,0:T(8,128)(2,1)} %param.11) | copy-start | bytes 4718596
  165.9 34.1 %copy-start.23 = (f32[1536]{0:T(1024)S(1)}, f32[1536]{0:T(1024)}, u32[]{:S(2)}) copy-start(f32[1536]{0:T(1024)} %param.17) | copy-start | bytes 18436
  200.3 35.7 %collective-permute-start.3 = (bf16[512,1536]{1,0:T(8,128)(2,1)S(1)}, bf16[512,1536]{1,0:T(8,128)(2,1)S(1)}, u32[]{:S(2)}, u32[]{:S(2)}) collective-permute-start(bf16[512,1536]{1,0:T(8,128)(2,1)S(1)} %multiply_convert_fusion.4), channel_id=1, source_target_pairs={{0,1},{1,0},{2,3},{3,2},{4,5},{5,4},{6,7},{7,6},{8,9},{9,8},{10,11... | collective-permute-start | bytes 4718600 | tf_op jit(solution)/shard_map/ppermute | solution.py:45
  238.7 11.9 %copy-start.15 = (bf16[1024,1536]{1,0:T(8,128)(2,1)S(1)}, bf16[1024,1536]{1,0:T(8,128)(2,1)}, u32[]{:S(2)}) copy-start(bf16[1024,1536]{1,0:T(8,128)(2,1)} %pad_maximum_fusion.4) | copy-start | bytes 9437188
  261.5 18.0 %copy-start.19 = (bf16[1024,1536]{1,0:T(8,128)(2,1)S(1)}, bf16[1024,1536]{1,0:T(8,128)(2,1)}, u32[]{:S(2)}) copy-start(bf16[1024,1536]{1,0:T(8,128)(2,1)} %get-tuple-element.55) | copy-start | bytes 9437188
  290.4 330.5 %reduce-scatter.3.cloned.1.call-start = ((), (), s32[]{:S(2)}) async-start(), calls=%async_computation.4 | async-start | bytes 13369344 | tf_op jit(solution)/shard_map/reduce_scatter | solution.py:82
  290.5 13.7 %copy-start.16 = (bf16[1024,1536]{1,0:T(8,128)(2,1)S(1)}, bf16[1024,1536]{1,0:T(8,128)(2,1)}, u32[]{:S(2)}) copy-start(bf16[1024,1536]{1,0:T(8,128)(2,1)} %pad_maximum_fusion.4) | copy-start | bytes 9437188
  302.9 34.9 %collective-permute-start.4 = (bf16[512,1536]{1,0:T(8,128)(2,1)}, bf16[512,1536]{1,0:T(8,128)(2,1)}, u32[]{:S(2)}, u32[]{:S(2)}) collective-permute-start(bf16[512,1536]{1,0:T(8,128)(2,1)} %fusion.55), channel_id=1, source_target_pairs={{0,1},{1,0},{2,3},{3,2},{4,5},{5,4},{6,7},{7,6},{8,9},{9,8},{10,11... | collective-permute-start | bytes 4718600 | tf_op jit(solution)/shard_map/ppermute | solution.py:45
  335.4 4.9 copy-start.10
  335.4 4.9 copy-start.27
  345.3 33.9 %collective-permute-start.5 = (bf16[512,1536]{1,0:T(8,128)(2,1)}, bf16[512,1536]{1,0:T(8,128)(2,1)}, u32[]{:S(2)}, u32[]{:S(2)}) collective-permute-start(bf16[512,1536]{1,0:T(8,128)(2,1)} %get-tuple-element.61), channel_id=1, source_target_pairs={{0,1},{1,0},{2,3},{3,2},{4,5},{5,4},{6,7},{7,6},{8,9},{9,8},{10,11... | collective-permute-start | bytes 4718600 | tf_op jit(solution)/shard_map/ppermute | solution.py:45
  346.8 8.7 %copy-start.34 = (bf16[1024,2048]{1,0:T(8,128)(2,1)S(1)}, bf16[1024,2048]{1,0:T(8,128)(2,1)}, u32[]{:S(2)}) copy-start(bf16[1024,2048]{1,0:T(8,128)(2,1)} %get-tuple-element.62) | copy-start | bytes 12582916
  383.2 47.7 %collective-permute-start.6 = (bf16[512,1536]{1,0:T(8,128)(2,1)}, bf16[512,1536]{1,0:T(8,128)(2,1)}, u32[]{:S(2)}, u32[]{:S(2)}) collective-permute-start(bf16[512,1536]{1,0:T(8,128)(2,1)} %fusion.47), channel_id=1, source_target_pairs={{0,1},{1,0},{2,3},{3,2},{4,5},{5,4},{6,7},{7,6},{8,9},{9,8},{10,11... | collective-permute-start | bytes 4718600 | tf_op jit(solution)/shard_map/ppermute | solution.py:45
  430.9 10.2 %copy-start.18 = (bf16[1024,1536]{1,0:T(8,128)(2,1)S(1)}, bf16[1024,1536]{1,0:T(8,128)(2,1)}, u32[]{:S(2)}) copy-start(bf16[1024,1536]{1,0:T(8,128)(2,1)} %copy-done.17) | copy-start | bytes 9437188
  430.9 10.2 %copy-start.31 = (bf16[1024,3200]{1,0:T(8,128)(2,1)S(1)}, bf16[1024,3200]{1,0:T(8,128)(2,1)}, u32[]{:S(2)}) copy-start(bf16[1024,3200]{1,0:T(8,128)(2,1)} %get-tuple-element.72) | copy-start | bytes 19660804
  450.1 5.4 copy-start.12
  450.1 5.4 copy-start.5
  450.1 5.9 copy-start.14
  455.5 19.2 %collective-permute-start.7 = (bf16[4,2,96,2432]{3,2,1,0:T(8,128)(2,1)}, bf16[4,2,96,2432]{3,2,1,0:T(8,128)(2,1)}, u32[]{:S(2)}, u32[]{:S(2)}) collective-permute-start(bf16[4,2,96,2432]{3,2,1,0:T(8,128)(2,1)} %dynamic-slice_bitcast_fusion), channel_id=1, source_target_pairs={{0,2},{2,0},{4,6},{6,4},{8,10},{10,8},{12,14},{14,12},{16,18},{18,... | collective-permute-start | bytes 11206664 | tf_op jit(solution)/shard_map/ppermute | solution.py:87
  461.7 7.1 %collective-permute-start.9 = (bf16[4,2,96,768]{3,2,1,0:T(8,128)(2,1)}, bf16[4,2,96,768]{3,2,1,0:T(8,128)(2,1)}, u32[]{:S(2)}, u32[]{:S(2)}) collective-permute-start(bf16[4,2,96,768]{3,2,1,0:T(8,128)(2,1)} %dynamic-slice_bitcast_fusion.3), channel_id=1, source_target_pairs={{0,2},{2,0},{4,6},{6,4},{8,10},{10,8},{12,14},{14,12},{16,18},{18,... | collective-permute-start | bytes 3538952 | tf_op jit(solution)/shard_map/ppermute | solution.py:87
  461.7 7.1 %copy-start.21 = (bf16[1536,768]{1,0:T(8,128)(2,1)S(1)}, bf16[1536,768]{1,0:T(8,128)(2,1)}, u32[]{:S(2)}) copy-start(bf16[1536,768]{1,0:T(8,128)(2,1)} %copy-done.20) | copy-start | bytes 7077892
  467.2 7.1 %collective-permute-start.8 = (bf16[4,2,96,768]{3,2,1,0:T(8,128)(2,1)S(1)}, bf16[4,2,96,768]{3,2,1,0:T(8,128)(2,1)S(1)}, u32[]{:S(2)}, u32[]{:S(2)}) collective-permute-start(bf16[4,2,96,768]{3,2,1,0:T(8,128)(2,1)S(1)} %dynamic-slice_bitcast_fusion.4), channel_id=1, source_target_pairs={{0,2},{2,0},{4,6},{6,4},{8,10},{10,8},{12,14},{14,12},{16,18},{18,... | collective-permute-start | bytes 3538952 | tf_op jit(solution)/shard_map/ppermute | solution.py:87
  468.7 6.0 slice-start
  470.5 4.2 slice-start.1
  470.5 36.5 %collective-permute-start.10 = (bf16[512,1536]{1,0:T(8,128)(2,1)S(1)}, bf16[512,1536]{1,0:T(8,128)(2,1)}, u32[]{:S(2)}, u32[]{:S(2)}) collective-permute-start(bf16[512,1536]{1,0:T(8,128)(2,1)S(1)} %copy-done.32), channel_id=1, source_target_pairs={{0,1},{1,0},{2,3},{3,2},{4,5},{5,4},{6,7},{7,6},{8,9},{9,8},{10,11... | collective-permute-start | bytes 4718600 | tf_op jit(solution)/shard_map/ppermute | solution.py:45
  474.3 32.7 %slice-start.2 = ((s8[6553600]{0:T(1024)(128)(4,1)}), s8[2359296]{0:T(1024)(128)(4,1)S(1)}, s32[]{:S(2)}) async-start(s8[6553600]{0:T(1024)(128)(4,1)} %bitcast.105), calls=%async_computation.8 | async-start | bytes 4718592
  474.6 32.3 %copy-start.8 = (bf16[512,1536]{1,0:T(8,128)(2,1)S(1)}, bf16[512,1536]{1,0:T(8,128)(2,1)}, u32[]{:S(2)}) copy-start(bf16[512,1536]{1,0:T(8,128)(2,1)} %param.11) | copy-start | bytes 4718596
  474.6 32.3 %copy-start.25 = (f32[1536]{0:T(1024)S(1)}, f32[1536]{0:T(1024)}, u32[]{:S(2)}) copy-start(f32[1536]{0:T(1024)} %param.12) | copy-start | bytes 18436
  474.6 32.3 %copy-start.29 = (f32[512]{0:T(512)S(1)}, f32[512]{0:T(512)}, u32[]{:S(2)}) copy-start(f32[512]{0:T(512)} %copy-done.28) | copy-start | bytes 6148
  474.7 32.3 %slice-start.3 = ((s8[6553600]{0:T(1024)(128)(4,1)}), s8[4194304]{0:T(1024)(128)(4,1)S(1)}, s32[]{:S(2)}) async-start(s8[6553600]{0:T(1024)(128)(4,1)} %bitcast.105), calls=%async_computation.9 | async-start | bytes 8388608
  516.0 8.2 %collective-permute-start.15 = (f32[25,128]{1,0:T(8,128)S(1)}, f32[25,128]{1,0:T(8,128)S(1)}, u32[]{:S(2)}, u32[]{:S(2)}) collective-permute-start(f32[25,128]{1,0:T(8,128)S(1)} %fusion.84), channel_id=1, source_target_pairs={{0,2},{2,0},{4,6},{6,4},{8,10},{10,8},{12,14},{14,12},{16,18},{18,... | collective-permute-start | bytes 38408 | tf_op jit(solution)/shard_map/ppermute | solution.py:87
  517.5 28.2 %collective-permute-start.12 = (bf16[2,96,1536]{2,1,0:T(8,128)(2,1)}, bf16[2,96,1536]{2,1,0:T(8,128)(2,1)S(1)}, u32[]{:S(2)}, u32[]{:S(2)}) collective-permute-start(bf16[2,96,1536]{2,1,0:T(8,128)(2,1)} %get-tuple-element.123), channel_id=1, source_target_pairs={{0,8},{2,10},{4,12},{6,14},{8,0},{10,2},{12,4},{14,6},{16,24},{18,... | collective-permute-start | bytes 1769480 | tf_op jit(solution)/shard_map/ppermute | solution.py:87
  517.7 42.7 %collective-permute-start.13 = (bf16[2,96,1536]{2,1,0:T(8,128)(2,1)}, bf16[2,96,1536]{2,1,0:T(8,128)(2,1)}, u32[]{:S(2)}, u32[]{:S(2)}) collective-permute-start(bf16[2,96,1536]{2,1,0:T(8,128)(2,1)} %get-tuple-element.122), channel_id=1, source_target_pairs={{0,16},{2,18},{4,20},{6,22},{8,24},{10,26},{12,28},{14,30},{16,0},... | collective-permute-start | bytes 1769480 | tf_op jit(solution)/shard_map/ppermute | solution.py:87
  520.0 4.6 copy-start.11
  520.0 40.5 %collective-permute-start.14 = (bf16[2,96,1536]{2,1,0:T(8,128)(2,1)}, bf16[2,96,1536]{2,1,0:T(8,128)(2,1)}, u32[]{:S(2)}, u32[]{:S(2)}) collective-permute-start(bf16[2,96,1536]{2,1,0:T(8,128)(2,1)} %get-tuple-element.121), channel_id=1, source_target_pairs={{0,24},{2,26},{4,28},{6,30},{8,16},{10,18},{12,20},{14,22},{16,8},... | collective-permute-start | bytes 1769480 | tf_op jit(solution)/shard_map/ppermute | solution.py:87
  523.6 42.6 %collective-permute-start.11 = (bf16[4,96,2432]{2,1,0:T(8,128)(2,1)}, bf16[4,96,2432]{2,1,0:T(8,128)(2,1)}, u32[]{:S(2)}, u32[]{:S(2)}) collective-permute-start(bf16[4,96,2432]{2,1,0:T(8,128)(2,1)} %get-tuple-element.111), channel_id=1, source_target_pairs={{0,4},{2,6},{4,0},{6,2},{8,12},{10,14},{12,8},{14,10},{16,20},{18,... | collective-permute-start | bytes 5603336 | tf_op jit(solution)/shard_map/ppermute | solution.py:87
  524.2 3.8 collective-permute-start.16
  566.2 8.7 %collective-permute-start.17 = (f32[25,128]{1,0:T(8,128)S(1)}, f32[25,128]{1,0:T(8,128)S(1)}, u32[]{:S(2)}, u32[]{:S(2)}) collective-permute-start(f32[25,128]{1,0:T(8,128)S(1)} %fusion.116), channel_id=1, source_target_pairs={{0,8},{2,10},{4,12},{6,14},{8,0},{10,2},{12,4},{14,6},{16,24},{18,... | collective-permute-start | bytes 38408 | tf_op jit(solution)/shard_map/ppermute | solution.py:87
  575.0 4.7 collective-permute-start.18
  579.7 8.5 %collective-permute-start.23 = (bf16[96,1536]{1,0:T(8,128)(2,1)S(1)}, bf16[96,1536]{1,0:T(8,128)(2,1)S(1)}, u32[]{:S(2)}, u32[]{:S(2)}) collective-permute-start(bf16[96,1536]{1,0:T(8,128)(2,1)S(1)} %dynamic-slice_bitcast_fusion.12), channel_id=1, source_target_pairs={{0,4},{2,6},{4,0},{6,2},{8,12},{10,14},{12,8},{14,10},{16,20},{18,... | collective-permute-start | bytes 884744 | tf_op jit(solution)/shard_map/ppermute | solution.py:87
  580.4 6.7 %collective-permute-start.19 = (f32[25,128]{1,0:T(8,128)S(1)}, f32[25,128]{1,0:T(8,128)S(1)}, u32[]{:S(2)}, u32[]{:S(2)}) collective-permute-start(f32[25,128]{1,0:T(8,128)S(1)} %add.242), channel_id=1, source_target_pairs={{0,4},{2,6},{4,0},{6,2},{8,12},{10,14},{12,8},{14,10},{16,20},{18,... | collective-permute-start | bytes 38408 | tf_op jit(solution)/shard_map/ppermute | solution.py:87
  582.0 18.5 %collective-permute-start.20 = (bf16[96,2432]{1,0:T(8,128)(2,1)S(1)}, bf16[96,2432]{1,0:T(8,128)(2,1)S(1)}, u32[]{:S(2)}, u32[]{:S(2)}) collective-permute-start(bf16[96,2432]{1,0:T(8,128)(2,1)S(1)} %get-tuple-element.125), channel_id=1, source_target_pairs={{0,8},{2,10},{4,12},{6,14},{8,0},{10,2},{12,4},{14,6},{16,24},{18,... | collective-permute-start | bytes 1400840 | tf_op jit(solution)/shard_map/ppermute | solution.py:87
  583.7 34.5 %collective-permute-start.21 = (bf16[96,2432]{1,0:T(8,128)(2,1)S(1)}, bf16[96,2432]{1,0:T(8,128)(2,1)S(1)}, u32[]{:S(2)}, u32[]{:S(2)}) collective-permute-start(bf16[96,2432]{1,0:T(8,128)(2,1)S(1)} %get-tuple-element.127), channel_id=1, source_target_pairs={{0,16},{2,18},{4,20},{6,22},{8,24},{10,26},{12,28},{14,30},{16,0},... | collective-permute-start | bytes 1400840 | tf_op jit(solution)/shard_map/ppermute | solution.py:87
  585.2 33.0 %collective-permute-start.22 = (bf16[96,2432]{1,0:T(8,128)(2,1)S(1)}, bf16[96,2432]{1,0:T(8,128)(2,1)S(1)}, u32[]{:S(2)}, u32[]{:S(2)}) collective-permute-start(bf16[96,2432]{1,0:T(8,128)(2,1)S(1)} %get-tuple-element.126), channel_id=1, source_target_pairs={{0,24},{2,26},{4,28},{6,30},{8,16},{10,18},{12,20},{14,22},{16,8},... | collective-permute-start | bytes 1400840 | tf_op jit(solution)/shard_map/ppermute | solution.py:87
  (3 other events, 8.7 us)
Sparse Core Ops, SparseCore 0:
  13.7 100.7 all-gather.2
  116.7 97.1 all-gather.4
  290.6 83.5 reduce-scatter.4
  378.0 133.8 reduce-scatter.2

commit v6 on v5

--- a/solution.py
+++ b/solution.py
@@ -546,41 +546,44 @@
     leaving, staying = term_parts(attn_back_term, own_rows)
     leaving, grad_later = hold(leaving, grad_proj)
     arrived_back = cross(leaving)
-    main_grad = dot_tn(normed_all, grad_later[:, : 3 * part + PAD]).astype(BF16)
-    gate_grad = dot_tn(normed_all, grad_later[:, 3 * part + PAD :]).astype(BF16)
+    grad_a = dot_tn(normed_all, grad_later[:, : 2 * part]).astype(BF16)
+    grad_b = dot_tn(normed_all, grad_later[:, 2 * part :]).astype(BF16)
     size = lax.axis_size("dp")
     tensor_size = lax.axis_size("tensor")
     if size % 4 or size & (size - 1) or tensor_size & (tensor_size - 1):
-        main_part, gate_part = (scatter_dp(main_grad).astype(F32), scatter_dp(gate_grad).astype(F32))
+        part_a, part_b = (scatter_dp(grad_a).astype(F32), scatter_dp(grad_b).astype(F32))
         out_part = scatter_dp(dot_tn(grad_branch_all, gated).astype(BF16))
         grad_input, sums = finish(arrived_back)
         sums = lax.psum(sums, ("dp", "tensor"))
     else:
+        half_a = over_core(grad_a)
+        half_a, gated, grad_branch_all = hold(half_a, gated, grad_branch_all)
+        side_a = side_pieces(half_a, 1)
+        half_b = over_core(grad_b)
         out_grad = dot_tn(grad_branch_all, gated).astype(BF16)
-        main_half, gate_half, out_half, arrived_back = hold(
-            over_core(main_grad), over_core(gate_grad), over_core(out_grad), arrived_back
-        )
-        rest_half = jnp.concatenate([gate_half, out_half], axis=-1)
+        out_layers = layer_pieces(over_core(out_grad))
+        side_a, half_b, out_layers, arrived_back = hold(side_a, half_b, out_layers, arrived_back)
+        layers_a = layer_pieces(total(side_a).astype(BF16))
+        side_b = side_pieces(half_b, 1)
         grad_input, sums = finish(arrived_back)
         sums = add_traded(sums, "dp", [1])
         sums = add_traded(sums, "tensor", masks_of(tensor_size))
-        main_half, rest_half, sums = hold(side_pieces(main_half, 1), layer_pieces(rest_half), sums)
+        layers_a, side_b, sums = hold(layers_a, side_b, sums)
         sums = add_traded(sums, "dp", masks_of(size)[2:])
-        main_half, rest_half, sums = hold(
-            total(main_half).astype(BF16), total(rest_half).astype(BF16), sums
-        )
-        main_part, rest_part = (total(layer_pieces(main_half)), total(side_pieces(rest_half, 0)))
-        gate_part, out_part = (rest_part[:, :part], rest_part[:, part:])
+        half_b, sums = hold(total(side_b).astype(BF16), sums)
+        part_b = total(layer_pieces(half_b))
+        part_a = total(layers_a)
+        out_part = total(side_pieces(total(out_layers).astype(BF16), 0))
         sums = add_traded(sums, "dp", [2])
     sums = sums.reshape(-1)
     return (
         layer_output,
         grad_input,
         sums[:width],
-        jnp.concatenate([main_part[:, : 3 * part], gate_part], axis=1).reshape(
+        jnp.concatenate([part_a, part_b[:, :part], part_b[:, part + PAD :]], axis=1).reshape(
             own_d, 4, part
         ),
-        main_part[:, 3 * part : 3 * part + heads_dev],
+        part_b[:, part : part + heads_dev],
         sums[2 * width : 2 * width + heads],
         out_part.astype(F32).T,
         sums[width : 2 * width],

time: 639 us -> 621 us (0.972)
  waiting for transfers between devices: 265 us -> 233 us
  starting transfers between devices: 33.3 us -> 56.3 us
    ppermute x16 -> x20, waiting for transfers between devices: 67.2 us -> 36.4 us  [trade(): return lax.ppermute(value, axis, [(i, i ^ mask) for i in range(size)])]
    ppermute x16 -> x20, starting transfers between devices: 22.1 us -> 45.5 us  [trade(): return lax.ppermute(value, axis, [(i, i ^ mask) for i in range(size)])]
  transfers between devices with their start and end apart: 28 -> 32, of which waited for: 16 -> 16; matrix products, arithmetic and copies ran while one was open for 30% -> 29% of each run, Pallas kernels for 10% -> 10%
where the time goes in v6:
time: 621 us; the launch traced here: 614 us
  waiting for transfers between devices  233 us (38%)
  matrix products  182 us (29%)
  Pallas kernels  63.8 us (10%)
  starting transfers between devices  56.3 us (9%)
  other arithmetic  42.8 us (7%)
  local copies, waits for them, and re-layouts  20.4 us (3%)
  between operations  15.3 us (2%)
    ppermute x8, waiting for transfers between devices, swap(): return lax.ppermute(rows, 'tensor', [(0, 1), (1, 0)])  173 us
    dot_general x8, matrix products, dot_nt(): lax.dot_general(a, b, (((1,), (1,)), ((), ())), preferred_element_type=F32)  67.8 us
    dot_general x6, matrix products, dot_nn(): lax.dot_general(a, b, (((1,), (0,)), ((), ())), preferred_element_type=F32)  64.8 us
    dot_general x5, matrix products, dot_tn(): lax.dot_general(a, b, (((0,), (0,)), ((), ())), preferred_element_type=F32)  49.8 us
    ppermute x20, starting transfers between devices, trade(): return lax.ppermute(value, axis, [(i, i ^ mask) for i in range(size)])  45.5 us
    pallas_call x1, Pallas kernels, attend_back(): pl.pallas_call(functools.partial(attend_back_body, per_group=per_group, g...  38.8 us
    ppermute x20, waiting for transfers between devices, trade(): return lax.ppermute(value, axis, [(i, i ^ mask) for i in range(size)])  36.4 us
    pallas_call x1, Pallas kernels, attend(): pl.pallas_call(functools.partial(attend_body, per_group=per_group), out_s...  25 us
  transfers between devices with their start and end apart: 32, of which 16 were waited for; matrix products, arithmetic and copies ran while one was open for 29% of the time, Pallas kernels for 10%

profile of v6, /device:TPU:0, one launch (start us, length us, event | category | flops | bytes accessed | tf_op | source)
XLA Modules:
  0.0 613.6 jit_solution(10025833415093973266)
XLA Ops:
  8.7 1.9 copy.36
  11.6 2.0 fusion.81
  15.8 3.0 collective-permute-start.1
  23.3 31.1 %collective-permute-done.1 = bf16[512,1536]{1,0:T(8,128)(2,1)} collective-permute-done((bf16[512,1536]{1,0:T(8,128)(2,1)}, bf16[512,1536]{1,0:T(8,128)(2,1)}, u32[]{:S(2)}, u32[]{:S(2)}) %collective-permute-start.1) | collective-permute-done | bytes 1572896 | tf_op jit(solution)/shard_map/ppermute | solution.py:45
  54.4 2.1 broadcast_select_fusion.5
  56.5 30.7 %collective-permute-done = bf16[512,1536]{1,0:T(8,128)(2,1)} collective-permute-done((bf16[512,1536]{1,0:T(8,128)(2,1)}, bf16[512,1536]{1,0:T(8,128)(2,1)}, u32[]{:S(2)}, u32[]{:S(2)}) %collective-permute-start) | collective-permute-done | bytes 1572896 | tf_op jit(solution)/shard_map/ppermute | solution.py:45
  87.2 2.2 broadcast_select_fusion.7
  89.5 1.9 pad_maximum_fusion.2
  91.4 23.1 %all-gather.3.cloned.1.call-done = bf16[1536,3968]{1,0:T(8,128)(2,1)} async-done(((bf16[96,3968]{1,0:T(8,128)(2,1)}), bf16[1536,3968]{1,0:T(8,128)(2,1)}) %all-gather.3.cloned.1.call-update) | async-done | bytes 12189712 | tf_op jit(solution)/shard_map/all_gather | solution.py:78
  114.7 7.2 %fusion.62.gate_ref.logit_ref = f32[1024,896]{1,0:T(8,128)} fusion(bf16[1024,1536]{1,0:T(8,128)(2,1)S(1)} %get-tuple-element.56, bf16[1536,3968]{1,0:T(8,128)(2,1)} %all-gather.3.cloned.1.call-done), kind=kOutput, calls=%fused_computation.78 | convolution fusion | flops 2818572288 | bytes 9568256 | tf_op jit(solution)/shard_map/dot_general | solution.py:33
  121.9 9.6 %fusion.15.q_ref.k_ref.v_ref = bf16[1024,2304]{1,0:T(8,128)(2,1)} fusion(bf16[1024,1536]{1,0:T(8,128)(2,1)S(1)} %get-tuple-element.56, bf16[1536,3968]{1,0:T(8,128)(2,1)S(1)} %copy-done.31), kind=kOutput, calls=%fused_computation.28 | convolution fusion | flops 7250116608 | bytes 14942208 | tf_op jit(solution)/shard_map/dot_general | solution.py:33
  131.5 25.0 %attend.1 = (bf16[1024,768]{1,0:T(8,128)(2,1)S(1)}, bf16[1024,768]{1,0:T(8,128)(2,1)S(1)}, f32[128,1024]{1,0:T(8,128)S(1)}, f32[1024,128]{1,0:T(8,128)S(1)}) custom-call(s32[1]{0:T(128)} %copy.41.lengths, bf16[1024,2304]{1,0:T(8,128)(2,1)} %fusion.15.q_ref.k_ref.v_ref, bf16[1024,2304]{1,0:T(8,128)(2,1)} %fusion.15.q_ref.k_ref.v_ref, ...), custom_call_target="tpu_custom_call" | custom-call | tf_op jit(solution)/shard_map/attend/pallas_call | solution.py:374
  156.5 4.6 convolution_convert_fusion.5
  162.7 3.2 fusion.69
  166.0 31.9 %collective-permute-done.2 = bf16[512,1536]{1,0:T(8,128)(2,1)} collective-permute-done((bf16[512,1536]{1,0:T(8,128)(2,1)S(1)}, bf16[512,1536]{1,0:T(8,128)(2,1)}, u32[]{:S(2)}, u32[]{:S(2)}) %collective-permute-start.2) | collective-permute-done | bytes 1572896 | tf_op jit(solution)/shard_map/ppermute | solution.py:45
  197.9 2.2 multiply_reduce_fusion.2
  201.9 34.2 %collective-permute-done.3 = bf16[512,1536]{1,0:T(8,128)(2,1)S(1)} collective-permute-done((bf16[512,1536]{1,0:T(8,128)(2,1)S(1)}, bf16[512,1536]{1,0:T(8,128)(2,1)S(1)}, u32[]{:S(2)}, u32[]{:S(2)}) %collective-permute-start.3) | collective-permute-done | bytes 1572896 | tf_op jit(solution)/shard_map/ppermute | solution.py:45
  236.9 1.9 pad_maximum_fusion.4
  238.8 11.8 %fusion.23 = f32[1024,2048]{1,0:T(8,128)} fusion(bf16[1024,1536]{1,0:T(8,128)(2,1)} %get-tuple-element.61, bf16[1536,6144]{1,0:T(8,128)(2,1)} %all-gather.5.cloned.1.call-done), kind=kOutput, calls=%fused_computation.35 | convolution fusion | flops 6442450944 | bytes 17825792 | tf_op jit(solution)/shard_map/dot_general | solution.py:33
  250.6 10.9 %fusion.11 = f32[1024,2048]{1,0:T(8,128)} fusion(bf16[1024,1536]{1,0:T(8,128)(2,1)S(1)} %copy-done.16, bf16[1536,6144]{1,0:T(8,128)(2,1)} %all-gather.5.cloned.1.call-done), kind=kOutput, calls=%fused_computation.24 | convolution fusion | flops 6442450944 | bytes 17825792 | tf_op jit(solution)/shard_map/dot_general | solution.py:33
  261.5 18.1 %multiply_convert_fusion = (bf16[1024,2048]{1,0:T(8,128)(2,1)}, bf16[1024,2048]{1,0:T(8,128)(2,1)}, bf16[1024,2048]{1,0:T(8,128)(2,1)}) fusion(f32[1024,2048]{1,0:T(8,128)} %fusion.11, f32[1024,2048]{1,0:T(8,128)} %fusion.23, bf16[1024,1536]{1,0:T(8,128)(2,1)S(1)} %copy-done.16, bf16[1536,6144]{1,0:T(8,128)(2,1)} %all-gather.5.cloned.1.call-done), kind=kOutput, calls=%fused_computation.14 | convolution fusion | flops 6473908224 | bytes 38797312 | tf_op jit(solution)/shard_map/dot_general | solution.py:33
  279.5 10.9 %convolution_convert_fusion.3 = bf16[1536,2048]{1,0:T(8,128)(2,1)} fusion(bf16[1024,1536]{1,0:T(8,128)(2,1)S(1)} %copy-done.20, bf16[1024,2048]{1,0:T(8,128)(2,1)} %get-tuple-element.68), kind=kOutput, calls=%fused_computation.21 | convolution fusion | flops 6445596672 | bytes 13631488 | tf_op jit(solution)/shard_map/dot_general | solution.py:41
  290.5 12.5 %fusion.57 = bf16[512,1536]{1,0:T(8,128)(2,1)} fusion(bf16[1536,6144]{1,0:T(8,128)(2,1)} %all-gather.5.cloned.1.call-done, s32[]{:T(128)S(6)} %select_n.172, bf16[1024,2048]{1,0:T(8,128)(2,1)} %get-tuple-element.121, bf16[1024,2048]{1,0:T(8,128)(2,1)} %get-tuple-element.122), kind=kOutput, calls=%fused_computation.77 | convolution fusion | flops 6451625984 | bytes 22544388 | tf_op jit(solution)/shard_map/dot_general | solution.py:37
  304.3 19.9 %convolution_convert_fusion = bf16[1536,4096]{1,0:T(8,128)(2,1)} fusion(bf16[1024,1536]{1,0:T(8,128)(2,1)S(1)} %copy-done.17, bf16[1024,2048]{1,0:T(8,128)(2,1)} %get-tuple-element.122, bf16[1024,2048]{1,0:T(8,128)(2,1)} %get-tuple-element.121), kind=kOutput, calls=%fused_computation | convolution fusion | flops 12907970560 | bytes 24117248 | tf_op jit(solution)/shard_map/dot_general | solution.py:41
  324.1 11.4 %fusion = f32[512,1536]{1,0:T(8,128)S(1)} fusion(bf16[1536,6144]{1,0:T(8,128)(2,1)} %all-gather.5.cloned.1.call-done, s32[]{:T(128)S(6)} %select_n.173, bf16[1024,2048]{1,0:T(8,128)(2,1)} %get-tuple-element.121, bf16[1024,2048]{1,0:T(8,128)(2,1)} %get-tuple-element.122), kind=kOutput, calls=%fused_computation.1 | convolution fusion | flops 6450839552 | bytes 24117252 | tf_op jit(solution)/shard_map/dot_general | solution.py:37
  335.5 2.3 collective-permute-done.4
  337.8 2.5 multiply_reduce_fusion
  340.3 4.9 fusion.102
  346.7 8.7 %fusion.19 = f32[512,1536]{1,0:T(8,128)} fusion(bf16[1536,6144]{1,0:T(8,128)(2,1)} %all-gather.5.cloned.1.call-done, bf16[1024,2048]{1,0:T(8,128)(2,1)} %get-tuple-element.68, s32[]{:T(128)S(6)} %select_n.173), kind=kOutput, calls=%fused_computation.31 | convolution fusion | flops 3221225472 | bytes 11534340 | tf_op jit(solution)/shard_map/dot_general | solution.py:37
  355.5 7.8 %fusion.49 = bf16[512,1536]{1,0:T(8,128)(2,1)} fusion(bf16[1536,6144]{1,0:T(8,128)(2,1)} %all-gather.5.cloned.1.call-done, bf16[1024,2048]{1,0:T(8,128)(2,1)S(1)} %copy-done.33, s32[]{:T(128)S(6)} %select_n.172), kind=kOutput, calls=%fused_computation.74 | convolution fusion | flops 3222011904 | bytes 9961476 | tf_op jit(solution)/shard_map/dot_general | solution.py:37
  363.3 15.8 %collective-permute-done.5 = bf16[512,1536]{1,0:T(8,128)(2,1)} collective-permute-done((bf16[512,1536]{1,0:T(8,128)(2,1)}, bf16[512,1536]{1,0:T(8,128)(2,1)}, u32[]{:S(2)}, u32[]{:S(2)}) %collective-permute-start.5) | collective-permute-done | bytes 1572896 | tf_op jit(solution)/shard_map/ppermute | solution.py:45
  379.1 2.1 broadcast_select_fusion.1
  381.2 1.9 pad_maximum_fusion.5
  383.1 1.6 collective-permute-start.6
  384.8 7.2 %fusion.72.grad_ref = bf16[1024,768]{1,0:T(8,128)(2,1)} fusion(bf16[1024,1536]{1,0:T(8,128)(2,1)} %pad_maximum_fusion.5, bf16[1536,3968]{1,0:T(8,128)(2,1)} %all-gather.3.cloned.1.call-done), kind=kOutput, calls=%fused_computation.95 | convolution fusion | flops 2416705536 | bytes 7077888 | tf_op jit(solution)/shard_map/dot_general | solution.py:33
  392.0 38.8 %attend_back.1 = (bf16[1024,3200]{1,0:T(8,128)(2,1)}, f32[8,128]{1,0:T(8,128)}) custom-call(bf16[1024,2304]{1,0:T(8,128)(2,1)} %fusion.15.q_ref.k_ref.v_ref, bf16[1024,2304]{1,0:T(8,128)(2,1)} %fusion.15.q_ref.k_ref.v_ref, bf16[1024,2304]{1,0:T(8,128)(2,1)} %fusion.15.q_ref.k_ref.v_ref, f32[1024,896]{1,0:T(8,128)} %fusion.62.gate_ref.logit_ref, ...), custom_call_target="tpu_custom_call" | custom-call | tf_op jit(solution)/shard_map/attend_back/pallas_call | solution.py:401
  430.8 10.2 %fusion.52 = bf16[512,1536]{1,0:T(8,128)(2,1)} fusion(bf16[1536,3968]{1,0:T(8,128)(2,1)} %all-gather.3.cloned.1.call-done, bf16[1024,3200]{1,0:T(8,128)(2,1)} %get-tuple-element.78, s32[]{:T(128)S(6)} %select_n.172), kind=kOutput, calls=%fused_computation.75 | convolution fusion | flops 5033951232 | bytes 14680068 | tf_op jit(solution)/shard_map/dot_general | solution.py:37
  441.0 7.3 %convolution_convert_fusion.2 = bf16[1536,1536]{1,0:T(8,128)(2,1)S(1)} fusion(bf16[1024,1536]{1,0:T(8,128)(2,1)S(1)} %copy-done.19, bf16[1024,3200]{1,0:T(8,128)(2,1)} %get-tuple-element.78), kind=kOutput, calls=%fused_computation.20 | convolution fusion | flops 4834197504 | bytes 11010048 | tf_op jit(solution)/shard_map/dot_general | solution.py:41
  448.3 2.1 copy-done.12
  452.0 8.8 %convolution_convert_fusion.1 = bf16[1536,1664]{1,0:T(8,128)(2,1)S(1)} fusion(bf16[1024,1536]{1,0:T(8,128)(2,1)} %copy-done.18, bf16[1024,3200]{1,0:T(8,128)(2,1)} %get-tuple-element.78), kind=kOutput, calls=%fused_computation.19 | convolution fusion | flops 5237047296 | bytes 11665408 | tf_op jit(solution)/shard_map/dot_general | solution.py:41
  463.2 2.9 fusion.29
  466.1 2.9 convolution_convert_fusion.4
  471.7 3.2 multiply_convert_fusion.3
  475.7 2.2 collective-permute-start.12
  478.0 1.8 collective-permute-start.13
  480.5 27.1 %collective-permute-done.14 = bf16[512,1536]{1,0:T(8,128)(2,1)} collective-permute-done((bf16[512,1536]{1,0:T(8,128)(2,1)}, bf16[512,1536]{1,0:T(8,128)(2,1)}, u32[]{:S(2)}, u32[]{:S(2)}) %collective-permute-start.14) | collective-permute-done | bytes 1572896 | tf_op jit(solution)/shard_map/ppermute | solution.py:45
  507.5 2.7 collective-permute-done.13
  511.6 9.4 %fusion.45 = (f32[1536]{0:T(1024)S(1)}, f32[512]{0:T(512)S(1)}, f32[512,1536]{1,0:T(8,128)S(1)}) fusion(bf16[512,1536]{1,0:T(8,128)(2,1)S(1)} %copy-done.8, f32[512]{0:T(512)S(1)} %copy-done.30, f32[1536]{0:T(1024)S(1)} %copy-done.26, bf16[512,1536]{1,0:T(8,128)(2,1)} %collective-permute-done.14, bf16[1536,3968]{1,0:T(8,128)(2,1)} %all-gather.3.cloned.1.call-done, ...), kind=kOutput, calls=%fused_computation.58 | convolution fusion | flops 5040240640 | bytes 19417092 | tf_op jit(solution)/shard_map/dot_general | solution.py:37
  522.8 13.7 %collective-permute-start.15 = (bf16[96,1536]{1,0:T(8,128)(2,1)S(1)}, bf16[96,1536]{1,0:T(8,128)(2,1)S(1)}, u32[]{:S(2)}, u32[]{:S(2)}) collective-permute-start(bf16[96,1536]{1,0:T(8,128)(2,1)S(1)} %get-tuple-element.140), channel_id=1, source_target_pairs={{0,8},{2,10},{4,12},{6,14},{8,0},{10,2},{12,4},{14,6},{16,24},{18,... | collective-permute-start | bytes 884744 | tf_op jit(solution)/shard_map/ppermute | solution.py:87
  536.5 2.8 collective-permute-start.16
  539.3 2.7 collective-permute-start.20
  542.0 2.5 fusion.44
  546.7 3.5 collective-permute-done.15
  550.2 10.3 %collective-permute-done.17 = bf16[96,1536]{1,0:T(8,128)(2,1)S(1)} collective-permute-done((bf16[96,1536]{1,0:T(8,128)(2,1)S(1)}, bf16[96,1536]{1,0:T(8,128)(2,1)S(1)}, u32[]{:S(2)}, u32[]{:S(2)}) %collective-permute-start.17) | collective-permute-done | bytes 294944 | tf_op jit(solution)/shard_map/ppermute | solution.py:87
  561.2 6.6 %collective-permute-start.21 = (f32[25,128]{1,0:T(8,128)S(1)}, f32[25,128]{1,0:T(8,128)S(1)}, u32[]{:S(2)}, u32[]{:S(2)}) collective-permute-start(f32[25,128]{1,0:T(8,128)S(1)} %fusion.118), channel_id=1, source_target_pairs={{0,8},{2,10},{4,12},{6,14},{8,0},{10,2},{12,4},{14,6},{16,24},{18,... | collective-permute-start | bytes 38408 | tf_op jit(solution)/shard_map/ppermute | solution.py:87
  567.8 1.9 convert_bitcast_fusion
  569.8 3.2 collective-permute-start.22
  576.4 1.8 collective-permute-start.25
  579.5 1.7 collective-permute-start.23
  581.3 1.9 collective-permute-done.23
  584.3 4.4 collective-permute-done.24
  588.8 12.1 %collective-permute-done.25 = bf16[96,1664]{1,0:T(8,128)(2,1)S(1)} collective-permute-done((bf16[96,1664]{1,0:T(8,128)(2,1)S(1)}, bf16[96,1664]{1,0:T(8,128)(2,1)S(1)}, u32[]{:S(2)}, u32[]{:S(2)}) %collective-permute-start.25) | collective-permute-done | bytes 319520 | tf_op jit(solution)/shard_map/ppermute | solution.py:87
  601.2 1.6 reshape.142
  603.5 3.3 reshape.152
  (164 shorter events, 36.8 us)
Async XLA Ops:
  7.2 7.2 %copy-start.9 = (bf16[512,1536]{1,0:T(8,128)(2,1)S(1)}, bf16[512,1536]{1,0:T(8,128)(2,1)}, u32[]{:S(2)}) copy-start(bf16[512,1536]{1,0:T(8,128)(2,1)} %param.21) | copy-start | bytes 4718596
  7.2 107.3 %all-gather.3.cloned.1.call-start = ((), (), s32[]{:S(2)}) async-start(), calls=%async_computation.2 | async-start | bytes 12951552 | tf_op jit(solution)/shard_map/all_gather | solution.py:78
  10.6 8.2 %copy-start.6 = (bf16[512,1536]{1,0:T(8,128)(2,1)S(1)}, bf16[512,1536]{1,0:T(8,128)(2,1)}, u32[]{:S(2)}) copy-start(bf16[512,1536]{1,0:T(8,128)(2,1)} %param.11) | copy-start | bytes 4718596
  11.6 7.7 %copy-start.25 = (f32[1536]{0:T(1024)S(1)}, f32[1536]{0:T(1024)}, u32[]{:S(2)}) copy-start(f32[1536]{0:T(1024)} %param.12) | copy-start | bytes 18436
  13.6 225.2 %all-gather.5.cloned.1.call-start = ((), (), s32[]{:S(2)}) async-start(), calls=%async_computation.3 | async-start | bytes 20054016 | tf_op jit(solution)/shard_map/all_gather | solution.py:78
  14.4 40.0 %copy-start.27 = (f32[512]{0:T(512)}, f32[512]{0:T(512)S(1)}, u32[]{:S(2)}) copy-start(f32[512]{0:T(512)S(1)} %fusion.98) | copy-start | bytes 6148
  15.8 6.4 %copy-start.21 = (bf16[2048,96]{0,1:T(8,128)(2,1)S(1)}, bf16[2048,96]{0,1:T(8,128)(2,1)}, u32[]{:S(2)}) copy-start(bf16[2048,96]{0,1:T(8,128)(2,1)} %param.19) | copy-start | bytes 1179652
  15.8 38.6 %collective-permute-start.1 = (bf16[512,1536]{1,0:T(8,128)(2,1)}, bf16[512,1536]{1,0:T(8,128)(2,1)}, u32[]{:S(2)}, u32[]{:S(2)}) collective-permute-start(bf16[512,1536]{1,0:T(8,128)(2,1)} %fusion.48), channel_id=1, source_target_pairs={{0,1},{1,0},{2,3},{3,2},{4,5},{5,4},{6,7},{7,6},{8,9},{9,8},{10,11... | collective-permute-start | bytes 4718600 | tf_op jit(solution)/shard_map/ppermute | solution.py:45
  19.2 68.0 %copy-start.29 = (f32[512]{0:T(512)}, f32[512]{0:T(512)S(1)}, u32[]{:S(2)}) copy-start(f32[512]{0:T(512)S(1)} %add_rsqrt_fusion.1) | copy-start | bytes 6148
  20.8 66.4 %collective-permute-start = (bf16[512,1536]{1,0:T(8,128)(2,1)}, bf16[512,1536]{1,0:T(8,128)(2,1)}, u32[]{:S(2)}, u32[]{:S(2)}) collective-permute-start(bf16[512,1536]{1,0:T(8,128)(2,1)} %fusion.40), channel_id=1, source_target_pairs={{0,1},{1,0},{2,3},{3,2},{4,5},{5,4},{6,7},{7,6},{8,9},{9,8},{10,11... | collective-permute-start | bytes 4718600 | tf_op jit(solution)/shard_map/ppermute | solution.py:45
  89.5 25.1 %copy-start.32 = (f32[24]{0:T(128)S(1)}, f32[24]{0:T(128)}, u32[]{:S(2)}) copy-start(f32[24]{0:T(128)} %param.15) | copy-start | bytes 292
  91.4 30.6 %copy-start.18 = (bf16[1024,1536]{1,0:T(8,128)(2,1)}, bf16[1024,1536]{1,0:T(8,128)(2,1)S(1)}, u32[]{:S(2)}) copy-start(bf16[1024,1536]{1,0:T(8,128)(2,1)S(1)} %get-tuple-element.56) | copy-start | bytes 9437188
  114.5 453.3 %reduce-scatter.5.cloned.1.call-start = ((), (), s32[]{:S(2)}) async-start(), calls=%async_computation.5 | async-start | bytes 6684672 | tf_op jit(solution)/shard_map/reduce_scatter | solution.py:82
  114.7 7.2 %copy-start.31 = (bf16[1536,3968]{1,0:T(8,128)(2,1)S(1)}, bf16[1536,3968]{1,0:T(8,128)(2,1)}, u32[]{:S(2)}) copy-start(bf16[1536,3968]{1,0:T(8,128)(2,1)} %all-gather.3.cloned.1.call-done) | copy-start | bytes 36569092
  131.5 25.0 %copy-start.3 = (f32[8,128]{1,0:T(8,128)}, f32[8,128]{1,0:T(8,128)S(1)}, u32[]{:S(2)}) copy-start(f32[8,128]{1,0:T(8,128)S(1)} %broadcast_in_dim.16.bias_ref) | copy-start | bytes 12292
  156.5 4.6 copy-start
  156.5 4.6 copy-start.1
  156.5 4.6 copy-start.2
  156.5 6.2 %copy-start.4 = (bf16[1024,768]{1,0:T(8,128)(2,1)}, bf16[1024,768]{1,0:T(8,128)(2,1)S(1)}, u32[]{:S(2)}) copy-start(bf16[1024,768]{1,0:T(8,128)(2,1)S(1)} %get-tuple-element.81) | copy-start | bytes 4718596
  161.2 36.7 %collective-permute-start.2 = (bf16[512,1536]{1,0:T(8,128)(2,1)S(1)}, bf16[512,1536]{1,0:T(8,128)(2,1)}, u32[]{:S(2)}, u32[]{:S(2)}) collective-permute-start(bf16[512,1536]{1,0:T(8,128)(2,1)S(1)} %convolution_convert_fusion.5), channel_id=1, source_target_pairs={{0,1},{1,0},{2,3},{3,2},{4,5},{5,4},{6,7},{7,6},{8,9},{9,8},{10,11... | collective-permute-start | bytes 4718600 | tf_op jit(solution)/shard_map/ppermute | solution.py:45
  162.7 35.2 %copy-start.7 = (bf16[512,1536]{1,0:T(8,128)(2,1)S(1)}, bf16[512,1536]{1,0:T(8,128)(2,1)}, u32[]{:S(2)}) copy-start(bf16[512,1536]{1,0:T(8,128)(2,1)} %param.11) | copy-start | bytes 4718596
  165.9 34.1 %copy-start.24 = (f32[1536]{0:T(1024)S(1)}, f32[1536]{0:T(1024)}, u32[]{:S(2)}) copy-start(f32[1536]{0:T(1024)} %param.17) | copy-start | bytes 18436
  200.4 35.7 %collective-permute-start.3 = (bf16[512,1536]{1,0:T(8,128)(2,1)S(1)}, bf16[512,1536]{1,0:T(8,128)(2,1)S(1)}, u32[]{:S(2)}, u32[]{:S(2)}) collective-permute-start(bf16[512,1536]{1,0:T(8,128)(2,1)S(1)} %multiply_convert_fusion.4), channel_id=1, source_target_pairs={{0,1},{1,0},{2,3},{3,2},{4,5},{5,4},{6,7},{7,6},{8,9},{9,8},{10,11... | collective-permute-start | bytes 4718600 | tf_op jit(solution)/shard_map/ppermute | solution.py:45
  238.8 11.8 %copy-start.16 = (bf16[1024,1536]{1,0:T(8,128)(2,1)S(1)}, bf16[1024,1536]{1,0:T(8,128)(2,1)}, u32[]{:S(2)}) copy-start(bf16[1024,1536]{1,0:T(8,128)(2,1)} %pad_maximum_fusion.4) | copy-start | bytes 9437188
  261.5 18.1 %copy-start.20 = (bf16[1024,1536]{1,0:T(8,128)(2,1)S(1)}, bf16[1024,1536]{1,0:T(8,128)(2,1)}, u32[]{:S(2)}) copy-start(bf16[1024,1536]{1,0:T(8,128)(2,1)} %get-tuple-element.61) | copy-start | bytes 9437188
  290.4 313.0 %reduce-scatter.3.cloned.1.call-start = ((), (), s32[]{:S(2)}) async-start(), calls=%async_computation.4 | async-start | bytes 13369344 | tf_op jit(solution)/shard_map/reduce_scatter | solution.py:82
  290.5 13.8 %copy-start.17 = (bf16[1024,1536]{1,0:T(8,128)(2,1)S(1)}, bf16[1024,1536]{1,0:T(8,128)(2,1)}, u32[]{:S(2)}) copy-start(bf16[1024,1536]{1,0:T(8,128)(2,1)} %pad_maximum_fusion.4) | copy-start | bytes 9437188
  303.0 34.9 %collective-permute-start.4 = (bf16[512,1536]{1,0:T(8,128)(2,1)}, bf16[512,1536]{1,0:T(8,128)(2,1)}, u32[]{:S(2)}, u32[]{:S(2)}) collective-permute-start(bf16[512,1536]{1,0:T(8,128)(2,1)} %fusion.57), channel_id=1, source_target_pairs={{0,1},{1,0},{2,3},{3,2},{4,5},{5,4},{6,7},{7,6},{8,9},{9,8},{10,11... | collective-permute-start | bytes 4718600 | tf_op jit(solution)/shard_map/ppermute | solution.py:45
  335.5 4.8 copy-start.10
  335.5 4.8 copy-start.28
  345.2 33.9 %collective-permute-start.5 = (bf16[512,1536]{1,0:T(8,128)(2,1)}, bf16[512,1536]{1,0:T(8,128)(2,1)}, u32[]{:S(2)}, u32[]{:S(2)}) collective-permute-start(bf16[512,1536]{1,0:T(8,128)(2,1)} %get-tuple-element.67), channel_id=1, source_target_pairs={{0,1},{1,0},{2,3},{3,2},{4,5},{5,4},{6,7},{7,6},{8,9},{9,8},{10,11... | collective-permute-start | bytes 4718600 | tf_op jit(solution)/shard_map/ppermute | solution.py:45
  346.7 8.7 %copy-start.33 = (bf16[1024,2048]{1,0:T(8,128)(2,1)S(1)}, bf16[1024,2048]{1,0:T(8,128)(2,1)}, u32[]{:S(2)}) copy-start(bf16[1024,2048]{1,0:T(8,128)(2,1)} %get-tuple-element.68) | copy-start | bytes 12582916
  383.1 47.6 %collective-permute-start.6 = (bf16[512,1536]{1,0:T(8,128)(2,1)}, bf16[512,1536]{1,0:T(8,128)(2,1)}, u32[]{:S(2)}, u32[]{:S(2)}) collective-permute-start(bf16[512,1536]{1,0:T(8,128)(2,1)} %fusion.49), channel_id=1, source_target_pairs={{0,1},{1,0},{2,3},{3,2},{4,5},{5,4},{6,7},{7,6},{8,9},{9,8},{10,11... | collective-permute-start | bytes 4718600 | tf_op jit(solution)/shard_map/ppermute | solution.py:45
  430.8 10.2 %copy-start.19 = (bf16[1024,1536]{1,0:T(8,128)(2,1)S(1)}, bf16[1024,1536]{1,0:T(8,128)(2,1)}, u32[]{:S(2)}) copy-start(bf16[1024,1536]{1,0:T(8,128)(2,1)} %copy-done.18) | copy-start | bytes 9437188
  452.0 9.8 %collective-permute-start.7 = (bf16[4,2,96,1536]{3,2,1,0:T(8,128)(2,1)}, bf16[4,2,96,1536]{3,2,1,0:T(8,128)(2,1)}, u32[]{:S(2)}, u32[]{:S(2)}) collective-permute-start(bf16[4,2,96,1536]{3,2,1,0:T(8,128)(2,1)} %dynamic-slice_bitcast_fusion.1), channel_id=1, source_target_pairs={{0,2},{2,0},{4,6},{6,4},{8,10},{10,8},{12,14},{14,12},{16,18},{18,... | collective-permute-start | bytes 7077896 | tf_op jit(solution)/shard_map/ppermute | solution.py:87
  461.1 5.1 copy-start.5
  461.1 5.1 copy-start.15
  461.1 16.9 %collective-permute-start.9 = (bf16[4,2,96,1664]{3,2,1,0:T(8,128)(2,1)S(1)}, bf16[4,2,96,1664]{3,2,1,0:T(8,128)(2,1)S(1)}, u32[]{:S(2)}, u32[]{:S(2)}) collective-permute-start(bf16[4,2,96,1664]{3,2,1,0:T(8,128)(2,1)S(1)} %dynamic-slice_bitcast_fusion), channel_id=1, source_target_pairs={{0,2},{2,0},{4,6},{6,4},{8,10},{10,8},{12,14},{14,12},{16,18},{18,... | collective-permute-start | bytes 7667720 | tf_op jit(solution)/shard_map/ppermute | solution.py:87
  469.2 5.7 collective-permute-start.10
  470.8 36.7 %collective-permute-start.14 = (bf16[512,1536]{1,0:T(8,128)(2,1)}, bf16[512,1536]{1,0:T(8,128)(2,1)}, u32[]{:S(2)}, u32[]{:S(2)}) collective-permute-start(bf16[512,1536]{1,0:T(8,128)(2,1)} %fusion.52), channel_id=1, source_target_pairs={{0,1},{1,0},{2,3},{3,2},{4,5},{5,4},{6,7},{7,6},{8,9},{9,8},{10,11... | collective-permute-start | bytes 4718600 | tf_op jit(solution)/shard_map/ppermute | solution.py:45
  471.1 36.4 %collective-permute-start.8 = (bf16[4,96,1536]{2,1,0:T(8,128)(2,1)S(1)}, bf16[4,96,1536]{2,1,0:T(8,128)(2,1)S(1)}, u32[]{:S(2)}, u32[]{:S(2)}) collective-permute-start(bf16[4,96,1536]{2,1,0:T(8,128)(2,1)S(1)} %get-tuple-element.133), channel_id=1, source_target_pairs={{0,4},{2,6},{4,0},{6,2},{8,12},{10,14},{12,8},{14,10},{16,20},{18,... | collective-permute-start | bytes 3538952 | tf_op jit(solution)/shard_map/ppermute | solution.py:87
  474.9 36.7 %slice-start = ((s8[6553600]{0:T(1024)(128)(4,1)}), s8[4194304]{0:T(1024)(128)(4,1)S(1)}, s32[]{:S(2)}) async-start(s8[6553600]{0:T(1024)(128)(4,1)} %bitcast.113), calls=%async_computation.6 | async-start | bytes 8388608
  475.3 32.3 %collective-permute-start.11 = (bf16[2,96,768]{2,1,0:T(8,128)(2,1)S(1)}, bf16[2,96,768]{2,1,0:T(8,128)(2,1)S(1)}, u32[]{:S(2)}, u32[]{:S(2)}) collective-permute-start(bf16[2,96,768]{2,1,0:T(8,128)(2,1)S(1)} %get-tuple-element.144), channel_id=1, source_target_pairs={{0,8},{2,10},{4,12},{6,14},{8,0},{10,2},{12,4},{14,6},{16,24},{18,... | collective-permute-start | bytes 884744 | tf_op jit(solution)/shard_map/ppermute | solution.py:87
  475.7 31.8 %collective-permute-start.12 = (bf16[2,96,768]{2,1,0:T(8,128)(2,1)S(1)}, bf16[2,96,768]{2,1,0:T(8,128)(2,1)S(1)}, u32[]{:S(2)}, u32[]{:S(2)}) collective-permute-start(bf16[2,96,768]{2,1,0:T(8,128)(2,1)S(1)} %get-tuple-element.143), channel_id=1, source_target_pairs={{0,16},{2,18},{4,20},{6,22},{8,24},{10,26},{12,28},{14,30},{16,0},... | collective-permute-start | bytes 884744 | tf_op jit(solution)/shard_map/ppermute | solution.py:87
  477.9 33.7 %copy-start.8 = (bf16[512,1536]{1,0:T(8,128)(2,1)S(1)}, bf16[512,1536]{1,0:T(8,128)(2,1)}, u32[]{:S(2)}) copy-start(bf16[512,1536]{1,0:T(8,128)(2,1)} %param.11) | copy-start | bytes 4718596
  477.9 33.7 %copy-start.26 = (f32[1536]{0:T(1024)S(1)}, f32[1536]{0:T(1024)}, u32[]{:S(2)}) copy-start(f32[1536]{0:T(1024)} %param.12) | copy-start | bytes 18436
  477.9 33.7 %copy-start.30 = (f32[512]{0:T(512)S(1)}, f32[512]{0:T(512)}, u32[]{:S(2)}) copy-start(f32[512]{0:T(512)} %copy-done.29) | copy-start | bytes 6148
  478.0 33.7 %slice-start.1 = ((s8[6553600]{0:T(1024)(128)(4,1)}), s8[2359296]{0:T(1024)(128)(4,1)S(1)}, s32[]{:S(2)}) async-start(s8[6553600]{0:T(1024)(128)(4,1)} %bitcast.113), calls=%async_computation.7 | async-start | bytes 4718592
  478.0 32.2 %collective-permute-start.13 = (bf16[2,96,768]{2,1,0:T(8,128)(2,1)S(1)}, bf16[2,96,768]{2,1,0:T(8,128)(2,1)S(1)}, u32[]{:S(2)}, u32[]{:S(2)}) collective-permute-start(bf16[2,96,768]{2,1,0:T(8,128)(2,1)S(1)} %get-tuple-element.142), channel_id=1, source_target_pairs={{0,24},{2,26},{4,28},{6,30},{8,16},{10,18},{12,20},{14,22},{16,8},... | collective-permute-start | bytes 884744 | tf_op jit(solution)/shard_map/ppermute | solution.py:87
  510.4 35.5 %collective-permute-start.27 = (bf16[96,768]{1,0:T(8,128)(2,1)S(1)}, bf16[96,768]{1,0:T(8,128)(2,1)S(1)}, u32[]{:S(2)}, u32[]{:S(2)}) collective-permute-start(bf16[96,768]{1,0:T(8,128)(2,1)S(1)} %dynamic-slice_bitcast_fusion.18), channel_id=1, source_target_pairs={{0,4},{2,6},{4,0},{6,2},{8,12},{10,14},{12,8},{14,10},{16,20},{18,... | collective-permute-start | bytes 442376 | tf_op jit(solution)/shard_map/ppermute | solution.py:87
  521.0 18.3 %collective-permute-start.19 = (f32[25,128]{1,0:T(8,128)S(1)}, f32[25,128]{1,0:T(8,128)S(1)}, u32[]{:S(2)}, u32[]{:S(2)}) collective-permute-start(f32[25,128]{1,0:T(8,128)S(1)} %fusion.85), channel_id=1, source_target_pairs={{0,2},{2,0},{4,6},{6,4},{8,10},{10,8},{12,14},{14,12},{16,18},{18,... | collective-permute-start | bytes 38408 | tf_op jit(solution)/shard_map/ppermute | solution.py:87
  521.4 20.6 %copy-start.11 = (f32[512,1536]{1,0:T(8,128)S(1)}, f32[512,1536]{1,0:T(8,128)}, u32[]{:S(2)}) copy-start(f32[512,1536]{1,0:T(8,128)} %get-tuple-element.117) | copy-start | bytes 9437188
  521.4 39.1 %collective-permute-start.18 = (bf16[4,96,1664]{2,1,0:T(8,128)(2,1)S(1)}, bf16[4,96,1664]{2,1,0:T(8,128)(2,1)S(1)}, u32[]{:S(2)}, u32[]{:S(2)}) collective-permute-start(bf16[4,96,1664]{2,1,0:T(8,128)(2,1)S(1)} %get-tuple-element.131), channel_id=1, source_target_pairs={{0,4},{2,6},{4,0},{6,2},{8,12},{10,14},{12,8},{14,10},{16,20},{18,... | collective-permute-start | bytes 3833864 | tf_op jit(solution)/shard_map/ppermute | solution.py:87
  522.8 27.4 %collective-permute-start.15 = (bf16[96,1536]{1,0:T(8,128)(2,1)S(1)}, bf16[96,1536]{1,0:T(8,128)(2,1)S(1)}, u32[]{:S(2)}, u32[]{:S(2)}) collective-permute-start(bf16[96,1536]{1,0:T(8,128)(2,1)S(1)} %get-tuple-element.140), channel_id=1, source_target_pairs={{0,8},{2,10},{4,12},{6,14},{8,0},{10,2},{12,4},{14,6},{16,24},{18,... | collective-permute-start | bytes 884744 | tf_op jit(solution)/shard_map/ppermute | solution.py:87
  536.5 13.8 %collective-permute-start.16 = (bf16[96,1536]{1,0:T(8,128)(2,1)S(1)}, bf16[96,1536]{1,0:T(8,128)(2,1)S(1)}, u32[]{:S(2)}, u32[]{:S(2)}) collective-permute-start(bf16[96,1536]{1,0:T(8,128)(2,1)S(1)} %get-tuple-element.139), channel_id=1, source_target_pairs={{0,16},{2,18},{4,20},{6,22},{8,24},{10,26},{12,28},{14,30},{16,0},... | collective-permute-start | bytes 884744 | tf_op jit(solution)/shard_map/ppermute | solution.py:87
  539.3 5.2 collective-permute-start.20
  544.5 16.0 %collective-permute-start.17 = (bf16[96,1536]{1,0:T(8,128)(2,1)S(1)}, bf16[96,1536]{1,0:T(8,128)(2,1)S(1)}, u32[]{:S(2)}, u32[]{:S(2)}) collective-permute-start(bf16[96,1536]{1,0:T(8,128)(2,1)S(1)} %get-tuple-element.138), channel_id=1, source_target_pairs={{0,24},{2,26},{4,28},{6,30},{8,16},{10,18},{12,20},{14,22},{16,8},... | collective-permute-start | bytes 884744 | tf_op jit(solution)/shard_map/ppermute | solution.py:87
  561.2 8.5 %collective-permute-start.21 = (f32[25,128]{1,0:T(8,128)S(1)}, f32[25,128]{1,0:T(8,128)S(1)}, u32[]{:S(2)}, u32[]{:S(2)}) collective-permute-start(f32[25,128]{1,0:T(8,128)S(1)} %fusion.118), channel_id=1, source_target_pairs={{0,8},{2,10},{4,12},{6,14},{8,0},{10,2},{12,4},{14,6},{16,24},{18,... | collective-permute-start | bytes 38408 | tf_op jit(solution)/shard_map/ppermute | solution.py:87
  569.7 11.4 %copy-start.23 = (bf16[96,1536]{1,0:T(8,128)(2,1)S(1)}, bf16[96,1536]{1,0:T(8,128)(2,1)}, u32[]{:S(2)}) copy-start(bf16[96,1536]{1,0:T(8,128)(2,1)} %copy-done.22) | copy-start | bytes 884740
  569.8 5.0 collective-permute-start.22
  574.8 13.9 %collective-permute-start.24 = (bf16[96,1664]{1,0:T(8,128)(2,1)S(1)}, bf16[96,1664]{1,0:T(8,128)(2,1)S(1)}, u32[]{:S(2)}, u32[]{:S(2)}) collective-permute-start(bf16[96,1664]{1,0:T(8,128)(2,1)S(1)} %get-tuple-element.135), channel_id=1, source_target_pairs={{0,8},{2,10},{4,12},{6,14},{8,0},{10,2},{12,4},{14,6},{16,24},{18,... | collective-permute-start | bytes 958472 | tf_op jit(solution)/shard_map/ppermute | solution.py:87
  576.4 24.5 %collective-permute-start.25 = (bf16[96,1664]{1,0:T(8,128)(2,1)S(1)}, bf16[96,1664]{1,0:T(8,128)(2,1)S(1)}, u32[]{:S(2)}, u32[]{:S(2)}) collective-permute-start(bf16[96,1664]{1,0:T(8,128)(2,1)S(1)} %get-tuple-element.137), channel_id=1, source_target_pairs={{0,16},{2,18},{4,20},{6,22},{8,24},{10,26},{12,28},{14,30},{16,0},... | collective-permute-start | bytes 958472 | tf_op jit(solution)/shard_map/ppermute | solution.py:87
  578.1 22.7 %collective-permute-start.26 = (bf16[96,1664]{1,0:T(8,128)(2,1)S(1)}, bf16[96,1664]{1,0:T(8,128)(2,1)S(1)}, u32[]{:S(2)}, u32[]{:S(2)}) collective-permute-start(bf16[96,1664]{1,0:T(8,128)(2,1)S(1)} %get-tuple-element.136), channel_id=1, source_target_pairs={{0,24},{2,26},{4,28},{6,30},{8,16},{10,18},{12,20},{14,22},{16,8},... | collective-permute-start | bytes 958472 | tf_op jit(solution)/shard_map/ppermute | solution.py:87
  579.5 3.7 collective-permute-start.23
  (4 other events, 7.8 us)
Sparse Core Ops, SparseCore 0:
  13.7 100.7 all-gather.2
  116.7 97.1 all-gather.4
  290.6 83.4 reduce-scatter.4
  378.0 152.7 reduce-scatter.2

commit v7 on v6

--- a/solution.py
+++ b/solution.py
@@ -561,15 +561,19 @@
         side_a = side_pieces(half_a, 1)
         half_b = over_core(grad_b)
         out_grad = dot_tn(grad_branch_all, gated).astype(BF16)
-        out_layers = layer_pieces(over_core(out_grad))
-        side_a, half_b, out_layers, arrived_back = hold(side_a, half_b, out_layers, arrived_back)
+        out_half = over_core(out_grad)
+        out_layers = layer_pieces(out_half)
+        side_a, half_b, arrived_back, layer_output = hold(
+            side_a, half_b, arrived_back, layer_output
+        )
         layers_a = layer_pieces(total(side_a).astype(BF16))
         side_b = side_pieces(half_b, 1)
         grad_input, sums = finish(arrived_back)
         sums = add_traded(sums, "dp", [1])
         sums = add_traded(sums, "tensor", masks_of(tensor_size))
-        layers_a, side_b, sums = hold(layers_a, side_b, sums)
-        sums = add_traded(sums, "dp", masks_of(size)[2:])
+        sums = add_traded(sums, "dp", masks_of(size)[2:-1])
+        layers_a, side_b, out_layers, sums = hold(layers_a, side_b, out_layers, sums)
+        sums = add_traded(sums, "dp", masks_of(size)[2:][-1:])
         half_b, sums = hold(total(side_b).astype(BF16), sums)
         part_b = total(layer_pieces(half_b))
         part_a = total(layers_a)

time: 621 us -> 626 us (level)
  waiting for transfers between devices: 233 us -> 261 us
  starting transfers between devices: 56.3 us -> 38.9 us
    ppermute x20, waiting for transfers between devices: 36.4 us -> 65.9 us  [trade(): return lax.ppermute(value, axis, [(i, i ^ mask) for i in range(size)])]
    ppermute x20, starting transfers between devices: 45.5 us -> 27.8 us  [trade(): return lax.ppermute(value, axis, [(i, i ^ mask) for i in range(size)])]
  transfers between devices with their start and end apart: 32 -> 32, of which waited for: 16 -> 15; matrix products, arithmetic and copies ran while one was open for 29% -> 29% of each run, Pallas kernels for 10% -> 10%
where the time goes in v7:
time: 626 us; the launch traced here: 619 us
  waiting for transfers between devices  261 us (42%)
  matrix products  178 us (28%)
  Pallas kernels  63.8 us (10%)
  other arithmetic  44.1 us (7%)
  starting transfers between devices  38.9 us (6%)
  local copies, waits for them, and re-layouts  18.4 us (3%)
  between operations  15.3 us (2%)
    ppermute x8, waiting for transfers between devices, swap(): return lax.ppermute(rows, 'tensor', [(0, 1), (1, 0)])  172 us
    dot_general x8, matrix products, dot_nt(): lax.dot_general(a, b, (((1,), (1,)), ((), ())), preferred_element_type=F32)  67.8 us
    ppermute x20, waiting for transfers between devices, trade(): return lax.ppermute(value, axis, [(i, i ^ mask) for i in range(size)])  65.9 us
    dot_general x6, matrix products, dot_nn(): lax.dot_general(a, b, (((1,), (0,)), ((), ())), preferred_element_type=F32)  64.8 us
    dot_general x5, matrix products, dot_tn(): lax.dot_general(a, b, (((0,), (0,)), ((), ())), preferred_element_type=F32)  45.6 us
    pallas_call x1, Pallas kernels, attend_back(): pl.pallas_call(functools.partial(attend_back_body, per_group=per_group, g...  38.8 us
    ppermute x20, starting transfers between devices, trade(): return lax.ppermute(value, axis, [(i, i ^ mask) for i in range(size)])  27.8 us
    pallas_call x1, Pallas kernels, attend(): pl.pallas_call(functools.partial(attend_body, per_group=per_group), out_s...  25 us
  transfers between devices with their start and end apart: 32, of which 15 were waited for; matrix products, arithmetic and copies ran while one was open for 29% of the time, Pallas kernels for 10%

profile of v7, /device:TPU:0, one launch (start us, length us, event | category | flops | bytes accessed | tf_op | source)
XLA Modules:
  0.0 619.3 jit_solution(2149855855434080544)
XLA Ops:
  8.7 1.9 copy.36
  11.6 2.0 fusion.81
  15.8 3.0 collective-permute-start.1
  19.2 1.6 fusion.40
  23.3 31.1 %collective-permute-done.1 = bf16[512,1536]{1,0:T(8,128)(2,1)} collective-permute-done((bf16[512,1536]{1,0:T(8,128)(2,1)}, bf16[512,1536]{1,0:T(8,128)(2,1)}, u32[]{:S(2)}, u32[]{:S(2)}) %collective-permute-start.1) | collective-permute-done | bytes 1572896 | tf_op jit(solution)/shard_map/ppermute | solution.py:45
  54.4 2.1 broadcast_select_fusion.5
  56.5 30.7 %collective-permute-done = bf16[512,1536]{1,0:T(8,128)(2,1)} collective-permute-done((bf16[512,1536]{1,0:T(8,128)(2,1)}, bf16[512,1536]{1,0:T(8,128)(2,1)}, u32[]{:S(2)}, u32[]{:S(2)}) %collective-permute-start) | collective-permute-done | bytes 1572896 | tf_op jit(solution)/shard_map/ppermute | solution.py:45
  87.2 2.2 broadcast_select_fusion.7
  89.5 1.9 pad_maximum_fusion.2
  91.4 23.1 %all-gather.3.cloned.1.call-done = bf16[1536,3968]{1,0:T(8,128)(2,1)} async-done(((bf16[96,3968]{1,0:T(8,128)(2,1)}), bf16[1536,3968]{1,0:T(8,128)(2,1)}) %all-gather.3.cloned.1.call-update) | async-done | bytes 12189712 | tf_op jit(solution)/shard_map/all_gather | solution.py:78
  114.7 7.2 %fusion.62.gate_ref.logit_ref = f32[1024,896]{1,0:T(8,128)} fusion(bf16[1024,1536]{1,0:T(8,128)(2,1)S(1)} %get-tuple-element.57, bf16[1536,3968]{1,0:T(8,128)(2,1)} %all-gather.3.cloned.1.call-done), kind=kOutput, calls=%fused_computation.78 | convolution fusion | flops 2818572288 | bytes 9568256 | tf_op jit(solution)/shard_map/dot_general | solution.py:33
  121.9 9.6 %fusion.15.q_ref.k_ref.v_ref = bf16[1024,2304]{1,0:T(8,128)(2,1)} fusion(bf16[1024,1536]{1,0:T(8,128)(2,1)S(1)} %get-tuple-element.57, bf16[1536,3968]{1,0:T(8,128)(2,1)S(1)} %copy-done.27), kind=kOutput, calls=%fused_computation.28 | convolution fusion | flops 7250116608 | bytes 14942208 | tf_op jit(solution)/shard_map/dot_general | solution.py:33
  131.5 25.0 %attend.1 = (bf16[1024,768]{1,0:T(8,128)(2,1)S(1)}, bf16[1024,768]{1,0:T(8,128)(2,1)S(1)}, f32[128,1024]{1,0:T(8,128)S(1)}, f32[1024,128]{1,0:T(8,128)S(1)}) custom-call(s32[1]{0:T(128)} %copy.41.lengths, bf16[1024,2304]{1,0:T(8,128)(2,1)} %fusion.15.q_ref.k_ref.v_ref, bf16[1024,2304]{1,0:T(8,128)(2,1)} %fusion.15.q_ref.k_ref.v_ref, ...), custom_call_target="tpu_custom_call" | custom-call | tf_op jit(solution)/shard_map/attend/pallas_call | solution.py:374
  156.5 4.6 convolution_convert_fusion.5
  162.6 3.2 fusion.69
  165.9 31.9 %collective-permute-done.2 = bf16[512,1536]{1,0:T(8,128)(2,1)} collective-permute-done((bf16[512,1536]{1,0:T(8,128)(2,1)S(1)}, bf16[512,1536]{1,0:T(8,128)(2,1)}, u32[]{:S(2)}, u32[]{:S(2)}) %collective-permute-start.2) | collective-permute-done | bytes 1572896 | tf_op jit(solution)/shard_map/ppermute | solution.py:45
  197.8 2.2 multiply_reduce_fusion.2
  201.9 34.2 %collective-permute-done.3 = bf16[512,1536]{1,0:T(8,128)(2,1)S(1)} collective-permute-done((bf16[512,1536]{1,0:T(8,128)(2,1)S(1)}, bf16[512,1536]{1,0:T(8,128)(2,1)S(1)}, u32[]{:S(2)}, u32[]{:S(2)}) %collective-permute-start.3) | collective-permute-done | bytes 1572896 | tf_op jit(solution)/shard_map/ppermute | solution.py:45
  236.9 1.9 pad_maximum_fusion.4
  238.8 11.8 %fusion.23 = f32[1024,2048]{1,0:T(8,128)} fusion(bf16[1024,1536]{1,0:T(8,128)(2,1)} %get-tuple-element.63, bf16[1536,6144]{1,0:T(8,128)(2,1)} %all-gather.5.cloned.1.call-done), kind=kOutput, calls=%fused_computation.35 | convolution fusion | flops 6442450944 | bytes 17825792 | tf_op jit(solution)/shard_map/dot_general | solution.py:33
  250.7 11.0 %fusion.11 = f32[1024,2048]{1,0:T(8,128)} fusion(bf16[1024,1536]{1,0:T(8,128)(2,1)S(1)} %copy-done.14, bf16[1536,6144]{1,0:T(8,128)(2,1)} %all-gather.5.cloned.1.call-done), kind=kOutput, calls=%fused_computation.24 | convolution fusion | flops 6442450944 | bytes 17825792 | tf_op jit(solution)/shard_map/dot_general | solution.py:33
  261.7 18.0 %multiply_convert_fusion = (bf16[1024,2048]{1,0:T(8,128)(2,1)}, bf16[1024,2048]{1,0:T(8,128)(2,1)}, bf16[1024,2048]{1,0:T(8,128)(2,1)}) fusion(f32[1024,2048]{1,0:T(8,128)} %fusion.11, f32[1024,2048]{1,0:T(8,128)} %fusion.23, bf16[1024,1536]{1,0:T(8,128)(2,1)S(1)} %copy-done.14, bf16[1536,6144]{1,0:T(8,128)(2,1)} %all-gather.5.cloned.1.call-done), kind=kOutput, calls=%fused_computation.14 | convolution fusion | flops 6473908224 | bytes 38797312 | tf_op jit(solution)/shard_map/dot_general | solution.py:33
  279.7 10.9 %convolution_convert_fusion.3 = bf16[1536,2048]{1,0:T(8,128)(2,1)} fusion(bf16[1024,1536]{1,0:T(8,128)(2,1)S(1)} %copy-done.18, bf16[1024,2048]{1,0:T(8,128)(2,1)} %get-tuple-element.70), kind=kOutput, calls=%fused_computation.21 | convolution fusion | flops 6445596672 | bytes 13631488 | tf_op jit(solution)/shard_map/dot_general | solution.py:41
  290.7 12.4 %fusion.57 = bf16[512,1536]{1,0:T(8,128)(2,1)} fusion(bf16[1536,6144]{1,0:T(8,128)(2,1)} %all-gather.5.cloned.1.call-done, s32[]{:T(128)S(6)} %select_n.172, bf16[1024,2048]{1,0:T(8,128)(2,1)} %get-tuple-element.123, bf16[1024,2048]{1,0:T(8,128)(2,1)} %get-tuple-element.124), kind=kOutput, calls=%fused_computation.77 | convolution fusion | flops 6451625984 | bytes 22544388 | tf_op jit(solution)/shard_map/dot_general | solution.py:37
  304.5 19.8 %convolution_convert_fusion = bf16[1536,4096]{1,0:T(8,128)(2,1)} fusion(bf16[1024,1536]{1,0:T(8,128)(2,1)S(1)} %copy-done.15, bf16[1024,2048]{1,0:T(8,128)(2,1)} %get-tuple-element.124, bf16[1024,2048]{1,0:T(8,128)(2,1)} %get-tuple-element.123), kind=kOutput, calls=%fused_computation | convolution fusion | flops 12907970560 | bytes 24117248 | tf_op jit(solution)/shard_map/dot_general | solution.py:41
  324.4 11.7 %fusion = f32[512,1536]{1,0:T(8,128)S(1)} fusion(bf16[1536,6144]{1,0:T(8,128)(2,1)} %all-gather.5.cloned.1.call-done, s32[]{:T(128)S(6)} %select_n.173, bf16[1024,2048]{1,0:T(8,128)(2,1)} %get-tuple-element.123, bf16[1024,2048]{1,0:T(8,128)(2,1)} %get-tuple-element.124), kind=kOutput, calls=%fused_computation.1 | convolution fusion | flops 6450839552 | bytes 24117252 | tf_op jit(solution)/shard_map/dot_general | solution.py:37
  336.1 2.1 collective-permute-done.4
  338.1 2.5 multiply_reduce_fusion
  340.6 4.9 fusion.102
  345.5 1.5 collective-permute-start.5
  347.1 8.7 %fusion.19 = f32[512,1536]{1,0:T(8,128)} fusion(bf16[1536,6144]{1,0:T(8,128)(2,1)} %all-gather.5.cloned.1.call-done, bf16[1024,2048]{1,0:T(8,128)(2,1)} %get-tuple-element.70, s32[]{:T(128)S(6)} %select_n.173), kind=kOutput, calls=%fused_computation.31 | convolution fusion | flops 3221225472 | bytes 11534340 | tf_op jit(solution)/shard_map/dot_general | solution.py:37
  355.9 7.8 %fusion.49 = bf16[512,1536]{1,0:T(8,128)(2,1)} fusion(bf16[1536,6144]{1,0:T(8,128)(2,1)} %all-gather.5.cloned.1.call-done, bf16[1024,2048]{1,0:T(8,128)(2,1)S(1)} %copy-done.30, s32[]{:T(128)S(6)} %select_n.172), kind=kOutput, calls=%fused_computation.74 | convolution fusion | flops 3222011904 | bytes 9961476 | tf_op jit(solution)/shard_map/dot_general | solution.py:37
  363.7 15.9 %collective-permute-done.5 = bf16[512,1536]{1,0:T(8,128)(2,1)} collective-permute-done((bf16[512,1536]{1,0:T(8,128)(2,1)}, bf16[512,1536]{1,0:T(8,128)(2,1)}, u32[]{:S(2)}, u32[]{:S(2)}) %collective-permute-start.5) | collective-permute-done | bytes 1572896 | tf_op jit(solution)/shard_map/ppermute | solution.py:45
  379.6 2.1 broadcast_select_fusion.1
  381.7 1.9 pad_maximum_fusion.5
  383.6 1.7 collective-permute-start.6
  385.4 7.1 %fusion.72.grad_ref = bf16[1024,768]{1,0:T(8,128)(2,1)} fusion(bf16[1024,1536]{1,0:T(8,128)(2,1)} %pad_maximum_fusion.5, bf16[1536,3968]{1,0:T(8,128)(2,1)} %all-gather.3.cloned.1.call-done), kind=kOutput, calls=%fused_computation.95 | convolution fusion | flops 2416705536 | bytes 7077888 | tf_op jit(solution)/shard_map/dot_general | solution.py:33
  392.5 38.8 %attend_back.1 = (bf16[1024,3200]{1,0:T(8,128)(2,1)}, f32[8,128]{1,0:T(8,128)}) custom-call(bf16[1024,2304]{1,0:T(8,128)(2,1)} %fusion.15.q_ref.k_ref.v_ref, bf16[1024,2304]{1,0:T(8,128)(2,1)} %fusion.15.q_ref.k_ref.v_ref, bf16[1024,2304]{1,0:T(8,128)(2,1)} %fusion.15.q_ref.k_ref.v_ref, f32[1024,896]{1,0:T(8,128)} %fusion.62.gate_ref.logit_ref, ...), custom_call_target="tpu_custom_call" | custom-call | tf_op jit(solution)/shard_map/attend_back/pallas_call | solution.py:401
  431.3 10.2 %fusion.52 = bf16[512,1536]{1,0:T(8,128)(2,1)} fusion(bf16[1536,3968]{1,0:T(8,128)(2,1)} %all-gather.3.cloned.1.call-done, bf16[1024,3200]{1,0:T(8,128)(2,1)} %get-tuple-element.77, s32[]{:T(128)S(6)} %select_n.172), kind=kOutput, calls=%fused_computation.75 | convolution fusion | flops 5033951232 | bytes 14680068 | tf_op jit(solution)/shard_map/dot_general | solution.py:37
  441.5 5.4 convolution_convert_fusion.2
  447.2 6.3 %convolution_convert_fusion.1 = bf16[1536,1664]{1,0:T(8,128)(2,1)S(1)} fusion(bf16[1024,1536]{1,0:T(8,128)(2,1)S(1)} %copy-done.17, bf16[1024,3200]{1,0:T(8,128)(2,1)S(1)} %copy-done.28), kind=kOutput, calls=%fused_computation.19 | convolution fusion | flops 5237047296 | bytes 11665408 | tf_op jit(solution)/shard_map/dot_general | solution.py:41
  455.5 3.2 multiply_convert_fusion.3
  461.7 3.1 convolution_convert_fusion.4
  466.2 25.7 %collective-permute-done.10 = bf16[512,1536]{1,0:T(8,128)(2,1)} collective-permute-done((bf16[512,1536]{1,0:T(8,128)(2,1)}, bf16[512,1536]{1,0:T(8,128)(2,1)}, u32[]{:S(2)}, u32[]{:S(2)}) %collective-permute-start.10) | collective-permute-done | bytes 1572896 | tf_op jit(solution)/shard_map/ppermute | solution.py:45
  491.9 8.3 %collective-permute-done.8 = bf16[4,96,1536]{2,1,0:T(8,128)(2,1)S(1)} collective-permute-done((bf16[4,96,1536]{2,1,0:T(8,128)(2,1)S(1)}, bf16[4,96,1536]{2,1,0:T(8,128)(2,1)S(1)}, u32[]{:S(2)}, u32[]{:S(2)}) %collective-permute-start.8) | collective-permute-done | bytes 1179680 | tf_op jit(solution)/shard_map/ppermute | solution.py:87
  500.2 9.1 %fusion.45 = (f32[1536]{0:T(1024)S(1)}, f32[512]{0:T(512)S(1)}, f32[512,1536]{1,0:T(8,128)S(1)}) fusion(bf16[512,1536]{1,0:T(8,128)(2,1)S(1)} %copy-done.8, f32[512]{0:T(512)S(1)} %copy-done.26, f32[1536]{0:T(1024)S(1)} %copy-done.22, bf16[512,1536]{1,0:T(8,128)(2,1)} %collective-permute-done.10, bf16[1536,3968]{1,0:T(8,128)(2,1)} %all-gather.3.cloned.1.call-done, ...), kind=kOutput, calls=%fused_computation.58 | convolution fusion | flops 5040240640 | bytes 19417092 | tf_op jit(solution)/shard_map/dot_general | solution.py:37
  512.1 2.9 collective-permute-start.18
  516.2 2.5 fusion.44
  518.7 1.6 collective-permute-start.20
  520.6 1.9 collective-permute-done.20
  523.5 14.8 %collective-permute-done.21 = f32[25,128]{1,0:T(8,128)S(1)} collective-permute-done((f32[25,128]{1,0:T(8,128)S(1)}, f32[25,128]{1,0:T(8,128)S(1)}, u32[]{:S(2)}, u32[]{:S(2)}) %collective-permute-start.21) | collective-permute-done | bytes 12832 | tf_op jit(solution)/shard_map/ppermute | solution.py:87
  538.4 2.5 collective-permute-start.11
  540.8 2.7 collective-permute-start.12
  544.5 1.9 convert_bitcast_fusion
  546.5 6.2 collective-permute-done.11
  552.6 13.9 %collective-permute-done.12 = bf16[96,1536]{1,0:T(8,128)(2,1)} collective-permute-done((bf16[96,1536]{1,0:T(8,128)(2,1)}, bf16[96,1536]{1,0:T(8,128)(2,1)}, u32[]{:S(2)}, u32[]{:S(2)}) %collective-permute-start.12) | collective-permute-done | bytes 294944 | tf_op jit(solution)/shard_map/ppermute | solution.py:87
  567.9 1.5 collective-permute-start.27
  569.4 6.8 %collective-permute-start.22 = (f32[25,128]{1,0:T(8,128)S(1)}, f32[25,128]{1,0:T(8,128)S(1)}, u32[]{:S(2)}, u32[]{:S(2)}) collective-permute-start(f32[25,128]{1,0:T(8,128)S(1)} %add.260), channel_id=1, source_target_pairs={{0,16},{2,18},{4,20},{6,22},{8,24},{10,26},{12,28},{14,30},{16,0},... | collective-permute-start | bytes 38408 | tf_op jit(solution)/shard_map/ppermute | solution.py:87
  576.2 1.6 add_convert_fusion
  579.6 2.0 collective-permute-start.24
  585.9 7.1 %collective-permute-done.24 = bf16[96,1664]{1,0:T(8,128)(2,1)S(1)} collective-permute-done((bf16[96,1664]{1,0:T(8,128)(2,1)S(1)}, bf16[96,1664]{1,0:T(8,128)(2,1)S(1)}, u32[]{:S(2)}, u32[]{:S(2)}) %collective-permute-start.24) | collective-permute-done | bytes 319520 | tf_op jit(solution)/shard_map/ppermute | solution.py:87
  593.1 13.5 %collective-permute-done.25 = bf16[96,1664]{1,0:T(8,128)(2,1)S(1)} collective-permute-done((bf16[96,1664]{1,0:T(8,128)(2,1)S(1)}, bf16[96,1664]{1,0:T(8,128)(2,1)S(1)}, u32[]{:S(2)}, u32[]{:S(2)}) %collective-permute-start.25) | collective-permute-done | bytes 319520 | tf_op jit(solution)/shard_map/ppermute | solution.py:87
  606.9 1.6 reshape.142
  609.2 3.3 reshape.152
  (158 shorter events, 34.0 us)
Async XLA Ops:
  7.2 7.2 %copy-start.9 = (bf16[512,1536]{1,0:T(8,128)(2,1)S(1)}, bf16[512,1536]{1,0:T(8,128)(2,1)}, u32[]{:S(2)}) copy-start(bf16[512,1536]{1,0:T(8,128)(2,1)} %param.21) | copy-start | bytes 4718596
  7.2 107.3 %all-gather.3.cloned.1.call-start = ((), (), s32[]{:S(2)}) async-start(), calls=%async_computation.2 | async-start | bytes 12951552 | tf_op jit(solution)/shard_map/all_gather | solution.py:78
  10.6 8.2 %copy-start.6 = (bf16[512,1536]{1,0:T(8,128)(2,1)S(1)}, bf16[512,1536]{1,0:T(8,128)(2,1)}, u32[]{:S(2)}) copy-start(bf16[512,1536]{1,0:T(8,128)(2,1)} %param.11) | copy-start | bytes 4718596
  11.6 7.7 %copy-start.21 = (f32[1536]{0:T(1024)S(1)}, f32[1536]{0:T(1024)}, u32[]{:S(2)}) copy-start(f32[1536]{0:T(1024)} %param.12) | copy-start | bytes 18436
  13.6 225.2 %all-gather.5.cloned.1.call-start = ((), (), s32[]{:S(2)}) async-start(), calls=%async_computation.3 | async-start | bytes 20054016 | tf_op jit(solution)/shard_map/all_gather | solution.py:78
  14.4 40.0 %copy-start.23 = (f32[512]{0:T(512)}, f32[512]{0:T(512)S(1)}, u32[]{:S(2)}) copy-start(f32[512]{0:T(512)S(1)} %fusion.98) | copy-start | bytes 6148
  15.8 6.4 %copy-start.19 = (bf16[2048,96]{0,1:T(8,128)(2,1)S(1)}, bf16[2048,96]{0,1:T(8,128)(2,1)}, u32[]{:S(2)}) copy-start(bf16[2048,96]{0,1:T(8,128)(2,1)} %param.19) | copy-start | bytes 1179652
  15.8 38.6 %collective-permute-start.1 = (bf16[512,1536]{1,0:T(8,128)(2,1)}, bf16[512,1536]{1,0:T(8,128)(2,1)}, u32[]{:S(2)}, u32[]{:S(2)}) collective-permute-start(bf16[512,1536]{1,0:T(8,128)(2,1)} %fusion.48), channel_id=1, source_target_pairs={{0,1},{1,0},{2,3},{3,2},{4,5},{5,4},{6,7},{7,6},{8,9},{9,8},{10,11... | collective-permute-start | bytes 4718600 | tf_op jit(solution)/shard_map/ppermute | solution.py:45
  19.2 68.0 %copy-start.25 = (f32[512]{0:T(512)}, f32[512]{0:T(512)S(1)}, u32[]{:S(2)}) copy-start(f32[512]{0:T(512)S(1)} %add_rsqrt_fusion.1) | copy-start | bytes 6148
  20.8 66.4 %collective-permute-start = (bf16[512,1536]{1,0:T(8,128)(2,1)}, bf16[512,1536]{1,0:T(8,128)(2,1)}, u32[]{:S(2)}, u32[]{:S(2)}) collective-permute-start(bf16[512,1536]{1,0:T(8,128)(2,1)} %fusion.40), channel_id=1, source_target_pairs={{0,1},{1,0},{2,3},{3,2},{4,5},{5,4},{6,7},{7,6},{8,9},{9,8},{10,11... | collective-permute-start | bytes 4718600 | tf_op jit(solution)/shard_map/ppermute | solution.py:45
  89.5 25.1 %copy-start.29 = (f32[24]{0:T(128)S(1)}, f32[24]{0:T(128)}, u32[]{:S(2)}) copy-start(f32[24]{0:T(128)} %param.15) | copy-start | bytes 292
  91.4 30.5 %copy-start.16 = (bf16[1024,1536]{1,0:T(8,128)(2,1)}, bf16[1024,1536]{1,0:T(8,128)(2,1)S(1)}, u32[]{:S(2)}) copy-start(bf16[1024,1536]{1,0:T(8,128)(2,1)S(1)} %get-tuple-element.57) | copy-start | bytes 9437188
  114.5 430.0 %reduce-scatter.5.cloned.1.call-start = ((), (), s32[]{:S(2)}) async-start(), calls=%async_computation.5 | async-start | bytes 6684672 | tf_op jit(solution)/shard_map/reduce_scatter | solution.py:82
  114.7 7.2 %copy-start.27 = (bf16[1536,3968]{1,0:T(8,128)(2,1)S(1)}, bf16[1536,3968]{1,0:T(8,128)(2,1)}, u32[]{:S(2)}) copy-start(bf16[1536,3968]{1,0:T(8,128)(2,1)} %all-gather.3.cloned.1.call-done) | copy-start | bytes 36569092
  131.5 25.0 %copy-start.3 = (f32[8,128]{1,0:T(8,128)}, f32[8,128]{1,0:T(8,128)S(1)}, u32[]{:S(2)}) copy-start(f32[8,128]{1,0:T(8,128)S(1)} %broadcast_in_dim.16.bias_ref) | copy-start | bytes 12292
  156.4 4.6 copy-start
  156.5 4.6 copy-start.1
  156.5 4.6 copy-start.2
  156.5 6.2 copy-start.4
  161.1 36.7 %collective-permute-start.2 = (bf16[512,1536]{1,0:T(8,128)(2,1)S(1)}, bf16[512,1536]{1,0:T(8,128)(2,1)}, u32[]{:S(2)}, u32[]{:S(2)}) collective-permute-start(bf16[512,1536]{1,0:T(8,128)(2,1)S(1)} %convolution_convert_fusion.5), channel_id=1, source_target_pairs={{0,1},{1,0},{2,3},{3,2},{4,5},{5,4},{6,7},{7,6},{8,9},{9,8},{10,11... | collective-permute-start | bytes 4718600 | tf_op jit(solution)/shard_map/ppermute | solution.py:45
  162.6 35.2 %copy-start.7 = (bf16[512,1536]{1,0:T(8,128)(2,1)S(1)}, bf16[512,1536]{1,0:T(8,128)(2,1)}, u32[]{:S(2)}) copy-start(bf16[512,1536]{1,0:T(8,128)(2,1)} %param.11) | copy-start | bytes 4718596
  165.9 34.1 %copy-start.20 = (f32[1536]{0:T(1024)S(1)}, f32[1536]{0:T(1024)}, u32[]{:S(2)}) copy-start(f32[1536]{0:T(1024)} %param.17) | copy-start | bytes 18436
  200.3 35.8 %collective-permute-start.3 = (bf16[512,1536]{1,0:T(8,128)(2,1)S(1)}, bf16[512,1536]{1,0:T(8,128)(2,1)S(1)}, u32[]{:S(2)}, u32[]{:S(2)}) collective-permute-start(bf16[512,1536]{1,0:T(8,128)(2,1)S(1)} %multiply_convert_fusion.4), channel_id=1, source_target_pairs={{0,1},{1,0},{2,3},{3,2},{4,5},{5,4},{6,7},{7,6},{8,9},{9,8},{10,11... | collective-permute-start | bytes 4718600 | tf_op jit(solution)/shard_map/ppermute | solution.py:45
  238.8 11.9 %copy-start.14 = (bf16[1024,1536]{1,0:T(8,128)(2,1)S(1)}, bf16[1024,1536]{1,0:T(8,128)(2,1)}, u32[]{:S(2)}) copy-start(bf16[1024,1536]{1,0:T(8,128)(2,1)} %pad_maximum_fusion.4) | copy-start | bytes 9437188
  261.7 18.0 %copy-start.18 = (bf16[1024,1536]{1,0:T(8,128)(2,1)S(1)}, bf16[1024,1536]{1,0:T(8,128)(2,1)}, u32[]{:S(2)}) copy-start(bf16[1024,1536]{1,0:T(8,128)(2,1)} %get-tuple-element.63) | copy-start | bytes 9437188
  290.6 318.6 %reduce-scatter.3.cloned.1.call-start = ((), (), s32[]{:S(2)}) async-start(), calls=%async_computation.4 | async-start | bytes 13369344 | tf_op jit(solution)/shard_map/reduce_scatter | solution.py:82
  290.7 13.9 %copy-start.15 = (bf16[1024,1536]{1,0:T(8,128)(2,1)S(1)}, bf16[1024,1536]{1,0:T(8,128)(2,1)}, u32[]{:S(2)}) copy-start(bf16[1024,1536]{1,0:T(8,128)(2,1)} %pad_maximum_fusion.4) | copy-start | bytes 9437188
  303.1 35.0 %collective-permute-start.4 = (bf16[512,1536]{1,0:T(8,128)(2,1)}, bf16[512,1536]{1,0:T(8,128)(2,1)}, u32[]{:S(2)}, u32[]{:S(2)}) collective-permute-start(bf16[512,1536]{1,0:T(8,128)(2,1)} %fusion.57), channel_id=1, source_target_pairs={{0,1},{1,0},{2,3},{3,2},{4,5},{5,4},{6,7},{7,6},{8,9},{9,8},{10,11... | collective-permute-start | bytes 4718600 | tf_op jit(solution)/shard_map/ppermute | solution.py:45
  336.1 4.6 copy-start.10
  336.1 4.6 copy-start.24
  345.5 34.1 %collective-permute-start.5 = (bf16[512,1536]{1,0:T(8,128)(2,1)}, bf16[512,1536]{1,0:T(8,128)(2,1)}, u32[]{:S(2)}, u32[]{:S(2)}) collective-permute-start(bf16[512,1536]{1,0:T(8,128)(2,1)} %get-tuple-element.69), channel_id=1, source_target_pairs={{0,1},{1,0},{2,3},{3,2},{4,5},{5,4},{6,7},{7,6},{8,9},{9,8},{10,11... | collective-permute-start | bytes 4718600 | tf_op jit(solution)/shard_map/ppermute | solution.py:45
  347.1 8.7 %copy-start.30 = (bf16[1024,2048]{1,0:T(8,128)(2,1)S(1)}, bf16[1024,2048]{1,0:T(8,128)(2,1)}, u32[]{:S(2)}) copy-start(bf16[1024,2048]{1,0:T(8,128)(2,1)} %get-tuple-element.70) | copy-start | bytes 12582916
  383.6 47.7 %collective-permute-start.6 = (bf16[512,1536]{1,0:T(8,128)(2,1)}, bf16[512,1536]{1,0:T(8,128)(2,1)}, u32[]{:S(2)}, u32[]{:S(2)}) collective-permute-start(bf16[512,1536]{1,0:T(8,128)(2,1)} %fusion.49), channel_id=1, source_target_pairs={{0,1},{1,0},{2,3},{3,2},{4,5},{5,4},{6,7},{7,6},{8,9},{9,8},{10,11... | collective-permute-start | bytes 4718600 | tf_op jit(solution)/shard_map/ppermute | solution.py:45
  431.3 10.2 %copy-start.17 = (bf16[1024,1536]{1,0:T(8,128)(2,1)S(1)}, bf16[1024,1536]{1,0:T(8,128)(2,1)}, u32[]{:S(2)}) copy-start(bf16[1024,1536]{1,0:T(8,128)(2,1)} %copy-done.16) | copy-start | bytes 9437188
  431.3 10.2 %copy-start.28 = (bf16[1024,3200]{1,0:T(8,128)(2,1)S(1)}, bf16[1024,3200]{1,0:T(8,128)(2,1)}, u32[]{:S(2)}) copy-start(bf16[1024,3200]{1,0:T(8,128)(2,1)} %get-tuple-element.77) | copy-start | bytes 19660804
  447.1 11.6 %collective-permute-start.7 = (bf16[4,2,96,1536]{3,2,1,0:T(8,128)(2,1)S(1)}, bf16[4,2,96,1536]{3,2,1,0:T(8,128)(2,1)S(1)}, u32[]{:S(2)}, u32[]{:S(2)}) collective-permute-start(bf16[4,2,96,1536]{3,2,1,0:T(8,128)(2,1)S(1)} %dynamic-slice_bitcast_fusion.1), channel_id=1, source_target_pairs={{0,2},{2,0},{4,6},{6,4},{8,10},{10,8},{12,14},{14,12},{16,18},{18,... | collective-permute-start | bytes 7077896 | tf_op jit(solution)/shard_map/ppermute | solution.py:87
  453.5 2.0 copy-start.12
  453.7 11.8 %collective-permute-start.9 = (bf16[4,2,96,1664]{3,2,1,0:T(8,128)(2,1)S(1)}, bf16[4,2,96,1664]{3,2,1,0:T(8,128)(2,1)S(1)}, u32[]{:S(2)}, u32[]{:S(2)}) collective-permute-start(bf16[4,2,96,1664]{3,2,1,0:T(8,128)(2,1)S(1)} %dynamic-slice_bitcast_fusion), channel_id=1, source_target_pairs={{0,2},{2,0},{4,6},{6,4},{8,10},{10,8},{12,14},{14,12},{16,18},{18,... | collective-permute-start | bytes 7667720 | tf_op jit(solution)/shard_map/ppermute | solution.py:87
  455.4 36.5 %collective-permute-start.10 = (bf16[512,1536]{1,0:T(8,128)(2,1)}, bf16[512,1536]{1,0:T(8,128)(2,1)}, u32[]{:S(2)}, u32[]{:S(2)}) collective-permute-start(bf16[512,1536]{1,0:T(8,128)(2,1)} %fusion.52), channel_id=1, source_target_pairs={{0,1},{1,0},{2,3},{3,2},{4,5},{5,4},{6,7},{7,6},{8,9},{9,8},{10,11... | collective-permute-start | bytes 4718600 | tf_op jit(solution)/shard_map/ppermute | solution.py:45
  459.4 2.4 copy-start.13
  459.4 40.8 %slice-start = ((s8[6553600]{0:T(1024)(128)(4,1)}), s8[4194304]{0:T(1024)(128)(4,1)S(1)}, s32[]{:S(2)}) async-start(s8[6553600]{0:T(1024)(128)(4,1)} %bitcast.113), calls=%async_computation.6 | async-start | bytes 8388608
  459.6 40.6 %slice-start.1 = ((s8[6553600]{0:T(1024)(128)(4,1)}), s8[2359296]{0:T(1024)(128)(4,1)S(1)}, s32[]{:S(2)}) async-start(s8[6553600]{0:T(1024)(128)(4,1)} %bitcast.113), calls=%async_computation.7 | async-start | bytes 4718592
  459.6 40.6 %collective-permute-start.8 = (bf16[4,96,1536]{2,1,0:T(8,128)(2,1)S(1)}, bf16[4,96,1536]{2,1,0:T(8,128)(2,1)S(1)}, u32[]{:S(2)}, u32[]{:S(2)}) collective-permute-start(bf16[4,96,1536]{2,1,0:T(8,128)(2,1)S(1)} %get-tuple-element.135), channel_id=1, source_target_pairs={{0,4},{2,6},{4,0},{6,2},{8,12},{10,14},{12,8},{14,10},{16,20},{18,... | collective-permute-start | bytes 3538952 | tf_op jit(solution)/shard_map/ppermute | solution.py:87
  465.0 35.2 %copy-start.8 = (bf16[512,1536]{1,0:T(8,128)(2,1)S(1)}, bf16[512,1536]{1,0:T(8,128)(2,1)}, u32[]{:S(2)}) copy-start(bf16[512,1536]{1,0:T(8,128)(2,1)} %param.11) | copy-start | bytes 4718596
  465.0 35.2 %copy-start.22 = (f32[1536]{0:T(1024)S(1)}, f32[1536]{0:T(1024)}, u32[]{:S(2)}) copy-start(f32[1536]{0:T(1024)} %param.12) | copy-start | bytes 18436
  465.0 35.2 %copy-start.26 = (f32[512]{0:T(512)S(1)}, f32[512]{0:T(512)}, u32[]{:S(2)}) copy-start(f32[512]{0:T(512)} %copy-done.25) | copy-start | bytes 6148
  465.0 44.4 %collective-permute-start.15 = (bf16[4,2,96,768]{3,2,1,0:T(8,128)(2,1)S(1)}, bf16[4,2,96,768]{3,2,1,0:T(8,128)(2,1)S(1)}, u32[]{:S(2)}, u32[]{:S(2)}) collective-permute-start(bf16[4,2,96,768]{3,2,1,0:T(8,128)(2,1)S(1)} %dynamic-slice_bitcast_fusion.4), channel_id=1, source_target_pairs={{0,2},{2,0},{4,6},{6,4},{8,10},{10,8},{12,14},{14,12},{16,18},{18,... | collective-permute-start | bytes 3538952 | tf_op jit(solution)/shard_map/ppermute | solution.py:87
  509.4 9.3 %collective-permute-start.19 = (f32[25,128]{1,0:T(8,128)S(1)}, f32[25,128]{1,0:T(8,128)S(1)}, u32[]{:S(2)}, u32[]{:S(2)}) collective-permute-start(f32[25,128]{1,0:T(8,128)S(1)} %fusion.85), channel_id=1, source_target_pairs={{0,2},{2,0},{4,6},{6,4},{8,10},{10,8},{12,14},{14,12},{16,18},{18,... | collective-permute-start | bytes 38408 | tf_op jit(solution)/shard_map/ppermute | solution.py:87
  510.6 5.6 copy-start.11
  510.6 30.3 %collective-permute-start.16 = (bf16[2,96,768]{2,1,0:T(8,128)(2,1)S(1)}, bf16[2,96,768]{2,1,0:T(8,128)(2,1)}, u32[]{:S(2)}, u32[]{:S(2)}) collective-permute-start(bf16[2,96,768]{2,1,0:T(8,128)(2,1)S(1)} %get-tuple-element.142), channel_id=1, source_target_pairs={{0,8},{2,10},{4,12},{6,14},{8,0},{10,2},{12,4},{14,6},{16,24},{18,... | collective-permute-start | bytes 884744 | tf_op jit(solution)/shard_map/ppermute | solution.py:87
  510.6 32.9 %collective-permute-start.17 = (bf16[2,96,768]{2,1,0:T(8,128)(2,1)S(1)}, bf16[2,96,768]{2,1,0:T(8,128)(2,1)}, u32[]{:S(2)}, u32[]{:S(2)}) collective-permute-start(bf16[2,96,768]{2,1,0:T(8,128)(2,1)S(1)} %get-tuple-element.141), channel_id=1, source_target_pairs={{0,16},{2,18},{4,20},{6,22},{8,24},{10,26},{12,28},{14,30},{16,0},... | collective-permute-start | bytes 884744 | tf_op jit(solution)/shard_map/ppermute | solution.py:87
  512.1 34.4 %collective-permute-start.18 = (bf16[2,96,768]{2,1,0:T(8,128)(2,1)}, bf16[2,96,768]{2,1,0:T(8,128)(2,1)}, u32[]{:S(2)}, u32[]{:S(2)}) collective-permute-start(bf16[2,96,768]{2,1,0:T(8,128)(2,1)} %get-tuple-element.140), channel_id=1, source_target_pairs={{0,24},{2,26},{4,28},{6,30},{8,16},{10,18},{12,20},{14,22},{16,8},... | collective-permute-start | bytes 884744 | tf_op jit(solution)/shard_map/ppermute | solution.py:87
  515.3 51.3 %collective-permute-start.14 = (bf16[4,96,1664]{2,1,0:T(8,128)(2,1)S(1)}, bf16[4,96,1664]{2,1,0:T(8,128)(2,1)}, u32[]{:S(2)}, u32[]{:S(2)}) collective-permute-start(bf16[4,96,1664]{2,1,0:T(8,128)(2,1)S(1)} %get-tuple-element.133), channel_id=1, source_target_pairs={{0,4},{2,6},{4,0},{6,2},{8,12},{10,14},{12,8},{14,10},{16,20},{18,... | collective-permute-start | bytes 3833864 | tf_op jit(solution)/shard_map/ppermute | solution.py:87
  518.7 3.8 collective-permute-start.20
  522.5 15.8 %collective-permute-start.21 = (f32[25,128]{1,0:T(8,128)S(1)}, f32[25,128]{1,0:T(8,128)S(1)}, u32[]{:S(2)}, u32[]{:S(2)}) collective-permute-start(f32[25,128]{1,0:T(8,128)S(1)} %fusion.118), channel_id=1, source_target_pairs={{0,8},{2,10},{4,12},{6,14},{8,0},{10,2},{12,4},{14,6},{16,24},{18,... | collective-permute-start | bytes 38408 | tf_op jit(solution)/shard_map/ppermute | solution.py:87
  538.4 14.3 %collective-permute-start.11 = (bf16[96,1536]{1,0:T(8,128)(2,1)}, bf16[96,1536]{1,0:T(8,128)(2,1)S(1)}, u32[]{:S(2)}, u32[]{:S(2)}) collective-permute-start(bf16[96,1536]{1,0:T(8,128)(2,1)} %get-tuple-element.146), channel_id=1, source_target_pairs={{0,8},{2,10},{4,12},{6,14},{8,0},{10,2},{12,4},{14,6},{16,24},{18,... | collective-permute-start | bytes 884744 | tf_op jit(solution)/shard_map/ppermute | solution.py:87
  540.8 25.7 %collective-permute-start.12 = (bf16[96,1536]{1,0:T(8,128)(2,1)}, bf16[96,1536]{1,0:T(8,128)(2,1)}, u32[]{:S(2)}, u32[]{:S(2)}) collective-permute-start(bf16[96,1536]{1,0:T(8,128)(2,1)} %get-tuple-element.145), channel_id=1, source_target_pairs={{0,16},{2,18},{4,20},{6,22},{8,24},{10,26},{12,28},{14,30},{16,0},... | collective-permute-start | bytes 884744 | tf_op jit(solution)/shard_map/ppermute | solution.py:87
  543.5 23.1 %collective-permute-start.13 = (bf16[96,1536]{1,0:T(8,128)(2,1)}, bf16[96,1536]{1,0:T(8,128)(2,1)}, u32[]{:S(2)}, u32[]{:S(2)}) collective-permute-start(bf16[96,1536]{1,0:T(8,128)(2,1)} %get-tuple-element.144), channel_id=1, source_target_pairs={{0,24},{2,26},{4,28},{6,30},{8,16},{10,18},{12,20},{14,22},{16,8},... | collective-permute-start | bytes 884744 | tf_op jit(solution)/shard_map/ppermute | solution.py:87
  567.9 17.3 %collective-permute-start.27 = (bf16[96,768]{1,0:T(8,128)(2,1)S(1)}, bf16[96,768]{1,0:T(8,128)(2,1)S(1)}, u32[]{:S(2)}, u32[]{:S(2)}) collective-permute-start(bf16[96,768]{1,0:T(8,128)(2,1)S(1)} %dynamic-slice_bitcast_fusion.18), channel_id=1, source_target_pairs={{0,4},{2,6},{4,0},{6,2},{8,12},{10,14},{12,8},{14,10},{16,20},{18,... | collective-permute-start | bytes 442376 | tf_op jit(solution)/shard_map/ppermute | solution.py:87
  569.4 9.6 %collective-permute-start.22 = (f32[25,128]{1,0:T(8,128)S(1)}, f32[25,128]{1,0:T(8,128)S(1)}, u32[]{:S(2)}, u32[]{:S(2)}) collective-permute-start(f32[25,128]{1,0:T(8,128)S(1)} %add.260), channel_id=1, source_target_pairs={{0,16},{2,18},{4,20},{6,22},{8,24},{10,26},{12,28},{14,30},{16,0},... | collective-permute-start | bytes 38408 | tf_op jit(solution)/shard_map/ppermute | solution.py:87
  579.0 5.0 collective-permute-start.23
  579.6 13.5 %collective-permute-start.24 = (bf16[96,1664]{1,0:T(8,128)(2,1)S(1)}, bf16[96,1664]{1,0:T(8,128)(2,1)S(1)}, u32[]{:S(2)}, u32[]{:S(2)}) collective-permute-start(bf16[96,1664]{1,0:T(8,128)(2,1)S(1)} %get-tuple-element.137), channel_id=1, source_target_pairs={{0,8},{2,10},{4,12},{6,14},{8,0},{10,2},{12,4},{14,6},{16,24},{18,... | collective-permute-start | bytes 958472 | tf_op jit(solution)/shard_map/ppermute | solution.py:87
  581.6 25.0 %collective-permute-start.25 = (bf16[96,1664]{1,0:T(8,128)(2,1)S(1)}, bf16[96,1664]{1,0:T(8,128)(2,1)S(1)}, u32[]{:S(2)}, u32[]{:S(2)}) collective-permute-start(bf16[96,1664]{1,0:T(8,128)(2,1)S(1)} %get-tuple-element.139), channel_id=1, source_target_pairs={{0,16},{2,18},{4,20},{6,22},{8,24},{10,26},{12,28},{14,30},{16,0},... | collective-permute-start | bytes 958472 | tf_op jit(solution)/shard_map/ppermute | solution.py:87
  582.8 23.8 %collective-permute-start.26 = (bf16[96,1664]{1,0:T(8,128)(2,1)S(1)}, bf16[96,1664]{1,0:T(8,128)(2,1)S(1)}, u32[]{:S(2)}, u32[]{:S(2)}) collective-permute-start(bf16[96,1664]{1,0:T(8,128)(2,1)S(1)} %get-tuple-element.138), channel_id=1, source_target_pairs={{0,24},{2,26},{4,28},{6,30},{8,16},{10,18},{12,20},{14,22},{16,8},... | collective-permute-start | bytes 958472 | tf_op jit(solution)/shard_map/ppermute | solution.py:87
  (1 other events, 1.4 us)
Sparse Core Ops, SparseCore 0:
  13.7 100.7 all-gather.2
  116.7 97.1 all-gather.4
  290.7 83.3 reduce-scatter.4
  378.1 154.2 reduce-scatter.2
